TPU v7x, 32 devices: a whole 2x2x4 slice. The times are simulated.
32 devices in a mesh: seq: 2 (over core), pipe: 4 (over y, x), tp: 4 (over z).
Axes of the slice: x: 2, y: 2, z: 4, core: 2. Of those that a mesh axis runs over, the one named last changes fastest.
Arguments:
- queries: bfloat16 [4, 1024, 3072], P('pipe', 'seq', 'tp'), may hold values from -6 to 6
- keys: bfloat16 [4, 1024, 3072], P('pipe', 'seq', 'tp'), may hold values from -6 to 6
- values: bfloat16 [4, 1024, 3072], P('pipe', 'seq', 'tp'), may hold values from -6 to 6
- grad_out: bfloat16 [4, 1024, 3072], P('pipe', 'seq', 'tp'), may hold values from -6 to 6
- router: float32 [4, 1024], P('pipe', 'seq'), may hold values from 0.1 to 1
- blocks: int32 [4, 2, 3], P('pipe', 'seq'), may hold values from 0 to 3, as said below
- counts: int32 [4, 2], P('pipe', 'seq'), may hold values from 1 to 3, as said below
Outputs:
- section_grads: bfloat16 [4, 3, 768, 3072], P('pipe', None, 'seq', 'tp')
- router_grad: float32 [4, 768], P('pipe', 'seq')
Inputs may be any that keep to these rules, and one draw needn't show every extreme that they name: Per section and shard, the first counts entries are distinct block numbers in increasing order; the remaining entries are 0. In every draw some shard routes its last 3 blocks. `counts`: in every draw some shard routes 3 blocks and some routes 1.
All inputs are finite; a program needn't handle non-finite values.
Results may differ from a plain program's by a relative error of at most 0.0058.
Values may be sent and summed in bfloat16 or wider, within the bound.
No kernel may reach another device: no remote copies, remote signals or barrier semaphores. Data moves between devices by JAX's collectives and lax.ppermute only.
A program may use at most 128 MiB of HBM per device.

v0:
```python
import math

import jax
import jax.numpy as jnp
from jax import lax
from jax.sharding import PartitionSpec as P

HEAD_SIZE = 128
BLOCK_ROWS = 128


def carried_in(part, axis, combine, identity, reverse):
    count = lax.axis_size(axis)
    place = lax.axis_index(axis)
    ahead = count - 1 - place if reverse else place
    gathered = lax.all_gather(part, axis)
    state = jnp.zeros_like(part) + jnp.asarray(identity, part.dtype)

    def one(turn, state):
        source = count - 1 - turn if reverse else turn
        return combine(state, lax.dynamic_index_in_dim(gathered, source, 0, False))

    return lax.fori_loop(0, ahead, one, state)


def from_behind(x, axis, by):
    count = lax.axis_size(axis)
    return lax.ppermute(x, axis, [(i, (i + by) % count) for i in range(count)])


def plus_state(earlier, later):
    return earlier + later


def on_device(queries, keys, values, grad_out, router, blocks, counts):
    heads_dev = queries.shape[2] // HEAD_SIZE
    width_dev = queries.shape[2]
    slot_count = blocks.shape[2]
    shard_blocks = queries.shape[1] // BLOCK_ROWS
    seq_count = lax.axis_size("seq")
    factor = 1.0 / math.sqrt(HEAD_SIZE * slot_count * BLOCK_ROWS * seq_count)
    valid_slot = jnp.arange(slot_count, dtype=jnp.int32) < counts[0, 0]
    picker = (
        blocks[0, 0, :, None] == jnp.arange(shard_blocks, dtype=jnp.int32)[None, :]
    ) & valid_slot[:, None]
    picker_half = picker.astype(jnp.bfloat16)
    picker_full = picker.astype(jnp.float32)

    def select(array):
        grouped = array[0].reshape(shard_blocks, BLOCK_ROWS, width_dev)
        taken_blocks = jnp.einsum(
            "jb,btf->jtf", picker_half, grouped, preferred_element_type=jnp.float32
        ).astype(jnp.bfloat16)
        return taken_blocks.reshape(slot_count, BLOCK_ROWS, heads_dev, HEAD_SIZE)

    query_rows = select(queries)
    key_rows = select(keys)
    value_rows = select(values)
    grad_rows = select(grad_out)
    grad_wide = grad_rows.astype(jnp.float32)
    router_weight = jnp.einsum(
        "jb,bt->jt",
        picker_full,
        router[0].reshape(shard_blocks, BLOCK_ROWS),
        precision=lax.Precision.HIGHEST,
    )
    output_gradient = (router_weight.reshape(slot_count, BLOCK_ROWS, 1, 1) * grad_wide).astype(
        jnp.bfloat16
    )
    key_value = jnp.einsum(
        "nthd,nthe->nhde", key_rows, value_rows, preferred_element_type=jnp.float32
    )
    query_grad = jnp.einsum(
        "nthd,nthe->nhde", query_rows, output_gradient, preferred_element_type=jnp.float32
    )
    zero_state = jnp.zeros((1,) + key_value.shape[1:], jnp.float32)
    local_before = jnp.concatenate([zero_state, jnp.cumsum(key_value, axis=0)[:-1]], axis=0)
    flipped = jnp.flip(query_grad, axis=0)
    local_after = jnp.flip(
        jnp.concatenate([zero_state, jnp.cumsum(flipped, axis=0)[:-1]], axis=0), axis=0
    )
    shard_state = jnp.sum(key_value, axis=0)
    shard_grad = jnp.sum(query_grad, axis=0)
    empty_state = jnp.zeros_like(shard_state)
    earlier_state = carried_in(shard_state, "seq", plus_state, empty_state, False)
    later_grad = carried_in(shard_grad, "seq", plus_state, empty_state, True)
    before = (earlier_state[None] + local_before).astype(jnp.bfloat16)
    after = (later_grad[None] + local_after).astype(jnp.bfloat16)
    causal = jnp.arange(BLOCK_ROWS)[:, None] >= jnp.arange(BLOCK_ROWS)[None, :]
    grad_scores = jnp.where(
        causal,
        jnp.einsum(
            "nthe,nshe->nhts", output_gradient, value_rows, preferred_element_type=jnp.float32
        ),
        0.0,
    ).astype(jnp.bfloat16)
    scores = jnp.where(
        causal,
        jnp.einsum("nthd,nshd->nhts", query_rows, key_rows, preferred_element_type=jnp.float32),
        0.0,
    ).astype(jnp.bfloat16)
    output_core = factor * (
        jnp.einsum("nhts,nshe->nthe", scores, value_rows, preferred_element_type=jnp.float32)
        + jnp.einsum("nthd,nhde->nthe", query_rows, before, preferred_element_type=jnp.float32)
    )
    partial_router = jnp.sum(grad_wide * output_core, axis=(2, 3)).reshape(-1)
    router_grad = lax.psum(partial_router, "tp")
    query_gradient = factor * (
        jnp.einsum("nhts,nshd->nthd", grad_scores, key_rows, preferred_element_type=jnp.float32)
        + jnp.einsum("nthe,nhde->nthd", output_gradient, before, preferred_element_type=jnp.float32)
    )
    key_gradient = factor * (
        jnp.einsum("nhts,nthd->nshd", grad_scores, query_rows, preferred_element_type=jnp.float32)
        + jnp.einsum("nshe,nhde->nshd", value_rows, after, preferred_element_type=jnp.float32)
    )
    value_gradient = factor * (
        jnp.einsum("nhts,nthe->nshe", scores, output_gradient, preferred_element_type=jnp.float32)
        + jnp.einsum("nshd,nhde->nshe", key_rows, after, preferred_element_type=jnp.float32)
    )
    stacked_gradients = (
        jnp.stack([query_gradient, key_gradient, value_gradient])
        .reshape(1, 3, slot_count * BLOCK_ROWS, heads_dev * HEAD_SIZE)
        .astype(jnp.bfloat16)
    )
    handed = from_behind(stacked_gradients, "pipe", -1)
    return (handed, router_grad.reshape(1, slot_count * BLOCK_ROWS))


def solution(mesh):
    return jax.shard_map(
        on_device,
        mesh=mesh,
        in_specs=(
            P("pipe", "seq", "tp"),
            P("pipe", "seq", "tp"),
            P("pipe", "seq", "tp"),
            P("pipe", "seq", "tp"),
            P("pipe", "seq"),
            P("pipe", "seq", None),
            P("pipe", "seq"),
        ),
        out_specs=(P("pipe", None, "seq", "tp"), P("pipe", "seq")),
        check_vma=False,
    )
```

profile of v0, /device:TPU:0, one launch (start us, length us, event | category | flops | bytes accessed | tf_op | source)
XLA Modules:
  0.0 111.4 jit_solution(18025959512974319276)
XLA Ops:
  0.6 0.0 copy-start
  1.4 0.7 fusion.20
  2.1 0.0 copy-done
  2.1 0.7 fusion.6
  2.8 0.0 copy-start.8
  2.8 1.5 %copy.58 = f32[3,128,768]{1,2,0:T(8,128)} copy(f32[3,128,768]{2,0,1:T(4,128)S(1)} %fusion.6) | data formatting | bytes 2359296 | tf_op jit(solution)/shard_map/convert_element_type | solution.py:60
  4.3 0.0 copy-done.8
  4.3 0.1 fusion.31
  4.4 1.8 %convolution_convert_fusion = bf16[3,128,768]{2,0,1:T(4,128)(2,1)S(1)} fusion(bf16[4,128,768]{2,1,0:T(8,128)(2,1)} %bitcast.94, pred[3,4]{1,0:T(4,128)(4,1)S(1)} %fusion.20), kind=kOutput, calls=%fused_computation.12 | convolution fusion | flops 2654208 | bytes 1376268 | tf_op jit(solution)/shard_map/jb,btf->jtf/dot_general | solution.py:51
  6.3 0.6 copy.67
  6.9 1.8 %convolution_convert_fusion.3 = bf16[3,128,768]{2,0,1:T(4,128)(2,1)S(1)} fusion(bf16[4,128,768]{2,1,0:T(8,128)(2,1)} %bitcast.95, pred[3,4]{1,0:T(4,128)(4,1)S(1)} %fusion.20), kind=kOutput, calls=%fused_computation.19 | convolution fusion | flops 2654208 | bytes 1376268 | tf_op jit(solution)/shard_map/jb,btf->jtf/dot_general | solution.py:51
  8.8 0.6 copy.56
  9.4 2.7 %convolution_convert_fusion.1 = bf16[3,128,768]{2,0,1:T(4,128)(2,1)} fusion(bf16[4,128,768]{2,1,0:T(8,128)(2,1)} %bitcast.96, pred[3,4]{1,0:T(4,128)(4,1)S(1)} %fusion.20), kind=kOutput, calls=%fused_computation.16 | convolution fusion | flops 2654208 | bytes 1376268 | tf_op jit(solution)/shard_map/jb,btf->jtf/dot_general | solution.py:51
  12.1 1.5 %copy.60 = bf16[3,128,768]{1,2,0:T(8,128)(2,1)S(1)} copy(bf16[3,128,768]{2,0,1:T(4,128)(2,1)} %convolution_convert_fusion.1) | data formatting | bytes 1179648 | tf_op jit(solution)/shard_map/convert_element_type | solution.py:53
  13.6 1.4 %multiply_convert_fusion = bf16[3,128,6,128]{1,3,2,0:T(8,128)(2,1)S(1)} fusion(f32[3,128,6,128]{1,3,2,0:T(8,128)} %bitcast.87, f32[3,128]{1,0:T(4,128)S(1)} %fusion.31), kind=kLoop, calls=%fused_computation.31 | loop fusion | flops 589824 | bytes 1771008 | tf_op jit(solution)/shard_map/convert_element_type | solution.py:67
  15.0 1.6 %fusion.27 = (f32[6,128,128]{2,1,0:T(8,128)S(1)}, f32[3,6,128,128]{3,2,1,0:T(8,128)}) fusion(bf16[3,128,6,128]{1,3,2,0:T(8,128)(2,1)S(1)} %bitcast.75, bf16[3,128,6,128]{1,3,2,0:T(8,128)(2,1)S(1)} %multiply_convert_fusion), kind=kOutput, calls=%fused_computation.47 | convolution fusion | flops 75694080 | bytes 2752512 | tf_op jit(solution)/shard_map/nthd,nthe->nhde/dot_general | solution.py:73
  16.6 1.2 %fusion.10 = bf16[3,6,128,128]{3,2,1,0:T(8,128)(2,1)} fusion(bf16[3,128,6,128]{1,3,2,0:T(8,128)(2,1)S(1)} %bitcast.76, bf16[3,128,6,128]{1,3,2,0:T(8,128)(2,1)S(1)} %bitcast.83, pred[128,128]{1,0:T(8,128)(4,1)S(1)} %iota_compare_fusion), kind=kOutput, calls=%fused_computation.23 | convolution fusion | flops 76087296 | bytes 1785856 | tf_op jit(solution)/shard_map/nthd,nshd->nhts/dot_general | solution.py:99
  17.8 0.4 fusion.7
  18.2 1.3 %fusion.33 = f32[3,6,128,128]{3,2,1,0:T(8,128)} fusion(bf16[3,128,6,128]{1,3,2,0:T(8,128)(2,1)S(1)} %bitcast.77, bf16[3,6,128,128]{3,2,1,0:T(8,128)(2,1)S(1)} %fusion.7), kind=kOutput, calls=%fused_computation.53 | convolution fusion | flops 75497472 | bytes 2359296 | tf_op jit(solution)/shard_map/nhts,nthd->nshd/dot_general | solution.py:113
  19.5 1.5 %fusion.32 = f32[3,6,128,128]{3,2,1,0:T(8,128)} fusion(bf16[3,128,6,128]{1,3,2,0:T(8,128)(2,1)S(1)} %bitcast.84, bf16[3,6,128,128]{3,2,1,0:T(8,128)(2,1)S(1)} %fusion.7), kind=kOutput, calls=%fused_computation.52 | convolution fusion | flops 75497472 | bytes 2359296 | tf_op jit(solution)/shard_map/nhts,nshd->nthd/dot_general | solution.py:109
  21.1 2.4 %fusion.28 = (f32[6,128,128]{2,1,0:T(8,128)}, f32[3,6,128,128]{3,2,1,0:T(8,128)}) fusion(bf16[3,128,6,128]{1,3,2,0:T(8,128)(2,1)S(1)} %bitcast.85, bf16[3,128,6,128]{1,3,2,0:T(8,128)(2,1)S(1)} %bitcast.80), kind=kOutput, calls=%fused_computation.48 | convolution fusion | flops 75694080 | bytes 2752512 | tf_op jit(solution)/shard_map/nthd,nthe->nhde/dot_general | solution.py:70
  23.4 2.4 %fusion.34 = f32[3,6,128,128]{3,2,1,0:T(8,128)} fusion(bf16[3,128,6,128]{1,3,2,0:T(8,128)(2,1)S(1)} %multiply_convert_fusion, bf16[3,6,128,128]{3,2,1,0:T(8,128)(2,1)} %fusion.10), kind=kOutput, calls=%fused_computation.54 | convolution fusion | flops 75497472 | bytes 2359296 | tf_op jit(solution)/shard_map/nhts,nthe->nshe/dot_general | solution.py:117
  25.8 2.4 %rev.7 = f32[3,6,128,128]{3,2,1,0:T(8,128)} reverse(f32[3,6,128,128]{3,2,1,0:T(8,128)} %get-tuple-element.100), dimensions={0} | reverse | bytes 2359296 | tf_op jit(solution)/shard_map/jit(_flip)/rev | solution.py:78
  28.2 1.4 %fusion.30 = f32[3,6,128,128]{3,2,1,0:T(8,128)S(1)} fusion(f32[3,6,128,128]{3,2,1,0:T(8,128)} %rev.7), kind=kOutput, calls=%fused_computation.50 | output fusion | flops 589824 | bytes 2359296 | tf_op jit(solution)/shard_map/jit(cumsum)/reduce_window_sum | solution.py:80
  29.6 1.0 slice.9
  30.6 2.6 %all-gather.1 = f32[12,128,128]{2,1,0:T(8,128)} all-gather(f32[6,128,128]{2,1,0:T(8,128)S(1)} %get-tuple-element.99), channel_id=3, replica_groups=mesh['seq'=2,'pipe'=4,'tp'=4] {'seq'}, dimensions={0}, use_global_device_ids=true | all-gather | bytes 1179648 | tf_op jit(solution)/shard_map/all_gather | solution.py:16
  33.2 1.1 %while.23 = (s32[]{:T(128)}, f32[6,128,128]{2,1,0:T(8,128)S(1)}, s32[]{:T(128)}, f32[2,6,128,128]{3,2,1,0:T(8,128)}, s32[]{:T(128)}, /*index=5*/s32[]{:T(128)}, s32[]{:T(128)}) while((s32[]{:T(128)}, f32[6,128,128]{2,1,0:T(8,128)S(1)}, s32[]{:T(128)}, f32[2,6,128,128]{3,2,1,0:T(8,128)}, s32[]{:T(128)}, /*index=5*/s32[]{:T(128)}, ...), condition=%wide.region_6.7_spmd, body=%wide.region_5.6_spmd.sunk | while | flops 98310 | bytes 1179783 | solution.py:23
  33.2 1.1 bitcast_add_fusion.5
  34.3 1.2 %concatenate.16 = f32[3,6,128,128]{3,2,1,0:T(8,128)S(1)} pad(f32[2,6,128,128]{3,2,1,0:T(8,128)} %slice.9, f32[]{:T(128)} %constant.41.clone.1), padding=1_0x0_0x0_0x0_0 | pad | bytes 1966084 | tf_op jit(solution)/shard_map/concatenate | solution.py:80
  35.6 0.0 copy-start.6
  35.6 0.1 add_convert_fusion
  35.7 0.0 copy-start.4
  35.7 0.8 copy-done.4
  36.6 0.5 copy-done.6
  37.1 1.2 %fusion.13 = bf16[3,128,6,128]{1,3,2,0:T(8,128)(2,1)} fusion(f32[3,6,128,128]{3,2,1,0:T(8,128)S(1)} %copy-done.6, bf16[3,6,128,128]{3,2,1,0:T(8,128)(2,1)S(1)} %add_convert_fusion, bf16[3,128,6,128]{1,3,2,0:T(8,128)(2,1)S(1)} %bitcast.86), kind=kOutput, calls=%fused_computation.26 | convolution fusion | flops 76382208 | bytes 2949120 | tf_op jit(solution)/shard_map/nshd,nhde->nshe/dot_general | solution.py:118
  38.3 0.0 copy-start.5
  38.3 2.4 %copy.75 = bf16[3,128,6,128]{3,2,1,0:T(8,128)(2,1)} copy(bf16[3,128,6,128]{1,3,2,0:T(8,128)(2,1)} %fusion.13) | data formatting | bytes 1179648 | tf_op jit(solution)/shard_map/mul | solution.py:116
  40.7 2.5 %stack.14 = bf16[1,1,384,768]{3,2,1,0:T(8,128)(2,1)} reshape(bf16[3,128,6,128]{3,2,1,0:T(8,128)(2,1)} %copy.75) | data formatting | bytes 1179648 | tf_op jit(solution)/shard_map/stack | solution.py:121
  43.1 0.0 copy-done.5
  43.1 2.4 %fusion.14 = bf16[3,128,6,128]{1,3,2,0:T(8,128)(2,1)} fusion(f32[3,6,128,128]{3,2,1,0:T(8,128)} %fusion.33, bf16[3,6,128,128]{3,2,1,0:T(8,128)(2,1)S(1)} %copy-done.5, bf16[3,128,6,128]{1,3,2,0:T(8,128)(2,1)S(1)} %bitcast.81), kind=kOutput, calls=%fused_computation.27 | convolution fusion | flops 76382208 | bytes 2949120 | tf_op jit(solution)/shard_map/nshe,nhde->nshd/dot_general | solution.py:114
  45.5 2.3 %copy.70 = bf16[3,128,6,128]{3,2,1,0:T(8,128)(2,1)} copy(bf16[3,128,6,128]{1,3,2,0:T(8,128)(2,1)} %fusion.14) | data formatting | bytes 1179648 | tf_op jit(solution)/shard_map/mul | solution.py:112
  47.8 2.5 %stack.13 = bf16[1,1,384,768]{3,2,1,0:T(8,128)(2,1)} reshape(bf16[3,128,6,128]{3,2,1,0:T(8,128)(2,1)} %copy.70) | data formatting | bytes 1179648 | tf_op jit(solution)/shard_map/stack | solution.py:121
  50.3 1.4 %fusion.29 = f32[3,6,128,128]{3,2,1,0:T(8,128)S(1)} fusion(f32[3,6,128,128]{3,2,1,0:T(8,128)} %get-tuple-element.102), kind=kOutput, calls=%fused_computation.49 | output fusion | flops 589824 | bytes 2359296 | tf_op jit(solution)/shard_map/jit(cumsum)/reduce_window_sum | solution.py:77
  51.7 0.0 copy-start.7
  51.7 0.9 slice.8
  52.6 0.1 copy-done.7
  52.7 2.5 %all-gather = f32[12,128,128]{2,1,0:T(8,128)} all-gather(f32[6,128,128]{2,1,0:T(8,128)S(1)} %copy-done.7), channel_id=2, replica_groups=mesh['seq'=2,'pipe'=4,'tp'=4] {'seq'}, dimensions={0}, use_global_device_ids=true | all-gather | bytes 1179648 | tf_op jit(solution)/shard_map/all_gather | solution.py:16
  55.3 0.2 while.22
  55.5 2.6 %fusion.15 = bf16[3,128,6,128]{1,3,2,0:T(8,128)(2,1)} fusion(f32[3,6,128,128]{3,2,1,0:T(8,128)} %fusion.32, bf16[3,128,6,128]{1,3,2,0:T(8,128)(2,1)S(1)} %multiply_convert_fusion, f32[2,6,128,128]{3,2,1,0:T(8,128)} %slice.8, f32[6,128,128]{2,1,0:T(8,128)S(1)} %get-tuple-element.81), kind=kOutput, calls=%fused_computation.28 | convolution fusion | flops 76972032 | bytes 3538944 | tf_op jit(solution)/shard_map/nthe,nhde->nthd/dot_general | solution.py:110
  58.1 2.3 %copy.65 = bf16[3,128,6,128]{3,2,1,0:T(8,128)(2,1)} copy(bf16[3,128,6,128]{1,3,2,0:T(8,128)(2,1)} %fusion.15) | data formatting | bytes 1179648 | tf_op jit(solution)/shard_map/mul | solution.py:108
  60.4 2.5 %stack.12 = bf16[1,1,384,768]{3,2,1,0:T(8,128)(2,1)} reshape(bf16[3,128,6,128]{3,2,1,0:T(8,128)(2,1)} %copy.65) | data formatting | bytes 1179648 | tf_op jit(solution)/shard_map/stack | solution.py:121
  62.9 0.0 copy-start.3
  62.9 2.9 %pad_maximum_fusion = bf16[1,3,384,768]{3,2,1,0:T(8,128)(2,1)} fusion(bf16[1,1,384,768]{3,2,1,0:T(8,128)(2,1)} %stack.14, bf16[1,1,384,768]{3,2,1,0:T(8,128)(2,1)} %stack.13, bf16[1,1,384,768]{3,2,1,0:T(8,128)(2,1)} %stack.12), kind=kLoop, calls=%fused_computation.2 | loop fusion | flops 1769472 | bytes 3538944 | tf_op jit(solution)/shard_map/stack | solution.py:121
  65.7 0.0 copy-start.1
  65.7 0.0 copy-start.2
  65.7 3.8 %collective-permute-start = (bf16[1,3,384,768]{3,2,1,0:T(8,128)(2,1)}, bf16[1,3,384,768]{3,2,1,0:T(8,128)(2,1)}, u32[]{:S(2)}, u32[]{:S(2)}) collective-permute-start(bf16[1,3,384,768]{3,2,1,0:T(8,128)(2,1)} %pad_maximum_fusion), channel_id=1, source_target_pairs={{0,12},{4,0},{8,4},{12,8},{1,13},{5,1},{9,5},{13,9},{2,14},{6,2},{... | collective-permute-start | bytes 5308424 | tf_op jit(solution)/shard_map/ppermute | solution.py:28
  69.6 0.0 copy-done.3
  69.6 0.5 fusion.35
  70.1 0.0 copy-done.1
  70.1 0.0 copy-done.2
  70.1 0.5 fusion.12
  70.6 12.6 %psum.7 = f32[1,384]{1,0:T(1,128)} all-reduce(f32[1,384]{1,0:T(1,128)S(1)} %bitcast.92), channel_id=1, replica_groups=mesh['seq'=2,'pipe'=4,'tp'=4] {'tp'}, use_global_device_ids=true, to_apply=%region_9.10 | all-reduce | flops 384 | bytes 3072 | tf_op jit(solution)/shard_map/psum | solution.py:107
  83.2 25.4 %collective-permute-done = bf16[1,3,384,768]{3,2,1,0:T(8,128)(2,1)} collective-permute-done((bf16[1,3,384,768]{3,2,1,0:T(8,128)(2,1)}, bf16[1,3,384,768]{3,2,1,0:T(8,128)(2,1)}, u32[]{:S(2)}, u32[]{:S(2)}) %collective-permute-start) | collective-permute-done | bytes 1769504 | tf_op jit(solution)/shard_map/ppermute | solution.py:28
  108.6 2.8 %copy.116 = bf16[1,3,384,768]{3,2,1,0:T(8,128)(2,1)} copy(bf16[1,3,384,768]{3,2,1,0:T(8,128)(2,1)} %collective-permute-done) | data formatting | bytes 3538944
  (5 shorter events, 0.1 us)
Async XLA Ops:
  0.6 1.5 %copy-start = (bf16[1,512,768]{2,1,0:T(8,128)(2,1)S(1)}, bf16[1,512,768]{2,1,0:T(8,128)(2,1)}, u32[]{:S(2)}) copy-start(bf16[1,512,768]{2,1,0:T(8,128)(2,1)} %param.14) | copy-start | bytes 2359300
  2.8 1.5 %copy-start.8 = (f32[1,512]{1,0:T(1,128)S(1)}, f32[1,512]{1,0:T(1,128)}, u32[]{:S(2)}) copy-start(f32[1,512]{1,0:T(1,128)} %param.15) | copy-start | bytes 6148
  35.6 1.5 %copy-start.6 = (f32[3,6,128,128]{3,2,1,0:T(8,128)S(1)}, f32[3,6,128,128]{3,2,1,0:T(8,128)}, u32[]{:S(2)}) copy-start(f32[3,6,128,128]{3,2,1,0:T(8,128)} %fusion.34) | copy-start | bytes 3538948
  35.7 0.8 copy-start.4
  38.3 4.8 %copy-start.5 = (bf16[3,6,128,128]{3,2,1,0:T(8,128)(2,1)S(1)}, bf16[3,6,128,128]{3,2,1,0:T(8,128)(2,1)}, u32[]{:S(2)}) copy-start(bf16[3,6,128,128]{3,2,1,0:T(8,128)(2,1)} %copy-done.4) | copy-start | bytes 1769476
  51.7 1.1 copy-start.7
  62.9 6.7 %copy-start.3 = (bf16[3,6,128,128]{3,2,1,0:T(8,128)(2,1)S(1)}, bf16[3,6,128,128]{3,2,1,0:T(8,128)(2,1)}, u32[]{:S(2)}) copy-start(bf16[3,6,128,128]{3,2,1,0:T(8,128)(2,1)} %fusion.10) | copy-start | bytes 1769476
  65.7 4.4 %copy-start.1 = (f32[3,128,768]{1,2,0:T(8,128)S(1)}, f32[3,128,768]{1,2,0:T(8,128)}, u32[]{:S(2)}) copy-start(f32[3,128,768]{1,2,0:T(8,128)} %copy.58) | copy-start | bytes 3538948
  65.7 4.4 %copy-start.2 = (f32[2,6,128,128]{3,2,1,0:T(8,128)S(1)}, f32[2,6,128,128]{3,2,1,0:T(8,128)}, u32[]{:S(2)}) copy-start(f32[2,6,128,128]{3,2,1,0:T(8,128)} %slice.8) | copy-start | bytes 2359300
  65.7 42.8 %collective-permute-start = (bf16[1,3,384,768]{3,2,1,0:T(8,128)(2,1)}, bf16[1,3,384,768]{3,2,1,0:T(8,128)(2,1)}, u32[]{:S(2)}, u32[]{:S(2)}) collective-permute-start(bf16[1,3,384,768]{3,2,1,0:T(8,128)(2,1)} %pad_maximum_fusion), channel_id=1, source_target_pairs={{0,12},{4,0},{8,4},{12,8},{1,13},{5,1},{9,5},{13,9},{2,14},{6,2},{... | collective-permute-start | bytes 5308424 | tf_op jit(solution)/shard_map/ppermute | solution.py:28
where the time goes:
time: 112 us; the launch traced here: 111 us
  local copies, waits for them, and re-layouts  28.5 us (25%)
  waiting for transfers between devices  25.4 us (23%)
  matrix products  25.3 us (23%)
  blocking collectives  17.7 us (16%)
  other arithmetic  8.97 us (8%)
  starting transfers between devices  3.82 us (3%)
  between operations  1.55 us (1%)
    ppermute x1, waiting for transfers between devices, from_behind(): return lax.ppermute(x, axis, [(i, (i + by) % count) for i in range(count)])  25.4 us
    psum x1, blocking collectives, on_device(): router_grad = lax.psum(partial_router, 'tp')  12.6 us
    another operation x3, local copies, waits for them, and re-layouts, on_device(): jnp.stack([query_gradient, key_gradient, value_gradient])  7.38 us
    dot_general x4, matrix products, select(): jnp.einsum('jb,btf->jtf', picker_half, grouped, preferred_element_type=jn...  7.09 us
    all_gather x2, blocking collectives, carried_in(): gathered = lax.all_gather(part, axis)  5.1 us
    unnamed x20, local copies, waits for them, and re-layouts  4.28 us
    ppermute x1, starting transfers between devices, from_behind(): return lax.ppermute(x, axis, [(i, (i + by) % count) for i in range(count)])  3.82 us
    another operation x1, other arithmetic, on_device(): jnp.stack([query_gradient, key_gradient, value_gradient])  2.88 us
  transfers between devices with their start and end apart: 1, of which 1 were waited for; matrix products, arithmetic and copies ran while one was open for 1% of the time, Pallas kernels for 0%

commit v1 on v0

v1 whole, which is shorter than its diff:
```python
import functools
import math

import jax
import jax.numpy as jnp
from jax import lax
from jax.experimental import pallas as pl
from jax.experimental.pallas import tpu as pltpu
from jax.sharding import PartitionSpec as P


HEAD_SIZE = 128
BLOCK_ROWS = 128
GRANT = 16 * 2**20


ANY = pl.BlockSpec(memory_space=pl.ANY)
HBM = pl.BlockSpec(memory_space=pltpu.HBM)
VMEM = pl.BlockSpec(memory_space=pltpu.VMEM)


def from_behind(x, axis, by):
    count = lax.axis_size(axis)
    return lax.ppermute(x, axis, [(i, (i + by) % count) for i in range(count)])


def in_hbm(x):
    return pltpu.with_memory_space_constraint(x, pltpu.HBM)


def dot(a, b):
    return jnp.dot(a, b, preferred_element_type=jnp.float32)


def dot_nt(a, b):
    return lax.dot_general(a, b, (((1,), (1,)), ((), ())), preferred_element_type=jnp.float32)


def dot_tn(a, b):
    return lax.dot_general(a, b, (((0,), (0,)), ((), ())), preferred_element_type=jnp.float32)


def lanes(h, count=1):
    return pl.ds(h * HEAD_SIZE, count * HEAD_SIZE)


def rows_of(n):
    if isinstance(n, int):
        return pl.ds(n * BLOCK_ROWS, BLOCK_ROWS)
    return pl.ds(pl.multiple_of(n * BLOCK_ROWS, BLOCK_ROWS), BLOCK_ROWS)


def down_rows(router, block):
    weight = router[0:1, rows_of(block)]
    return jnp.broadcast_to(weight, (BLOCK_ROWS, BLOCK_ROWS)).T


def row_minus_column():
    shape = (BLOCK_ROWS, BLOCK_ROWS)
    return lax.broadcasted_iota(jnp.int32, shape, 0) - lax.broadcasted_iota(jnp.int32, shape, 1)


def compiler_params():
    return pltpu.CompilerParams(vmem_limit_bytes=GRANT)


def cost(matmuls, moved):
    return pl.CostEstimate(
        flops=2 * matmuls * HEAD_SIZE**3, bytes_accessed=moved, transcendentals=0
    )


def is_first():
    return lax.axis_index("seq") == 0


def is_last():
    return lax.axis_index("seq") != 0


def always():
    return jnp.bool_(True)


def never():
    return jnp.bool_(False)


def start_small(router, blocks, router_buf, blocks_buf, sem):
    copies = [
        pltpu.make_async_copy(blocks, blocks_buf, sem.at[0]),
        pltpu.make_async_copy(router, router_buf, sem.at[1]),
    ]
    for copy in copies:
        copy.start()
    return copies


def small_scratch(router, blocks):
    return [
        pltpu.VMEM(router.shape, router.dtype),
        pltpu.SMEM(blocks.shape, blocks.dtype),
        pltpu.SemaphoreType.DMA((2,)),
    ]


def live_count(blocks):
    count = jnp.int32(1)
    for n in range(1, blocks.shape[2]):
        count = count + jnp.where(blocks[0, 0, n] > 0, 1, 0)
    return count


def drain(blocks, count, slots, shard_blocks, wait):
    for b in range(shard_blocks):
        taken = never()
        for n in range(slots):
            taken = jnp.logical_or(taken, jnp.logical_and(n < count, blocks[0, 0, n] == b))

        @pl.when(jnp.logical_not(taken))
        def _():
            wait(b)


def side_kernel(
    factor, query_side, begin, end, keep, seeded, *refs,
):
    router, blocks, q, k, v, g = refs[:6]
    refs = refs[6:]
    if seeded:
        seed, refs = refs[0], refs[1:]
    chunk, refs = refs[0], refs[1:]
    if keep:
        total, states, refs = refs[0], refs[1], refs[2:]
    router_buf, blocks_buf, small_sem, x_buf, vc_buf, g_buf, acc, in_sem = refs
    slots = blocks_buf.shape[2]
    shard_blocks = x_buf.shape[0]
    low, high = (0, acc.shape[0]) if keep else (begin, end)
    span = high - low

    for_query = query_side()
    left = jnp.where(for_query, 1, 0)
    right = 1 - left
    sign = jnp.where(for_query, 1, -1)

    def loads(b):
        return (
            pltpu.make_async_copy(g.at[0, rows_of(b), lanes(low, span)], g_buf.at[b], in_sem.at[0, b]),
            pltpu.make_async_copy(v.at[0, rows_of(b), lanes(low, span)], vc_buf.at[0, b], in_sem.at[1, b]),
            pltpu.make_async_copy(k.at[0, rows_of(b), lanes(low, span)], x_buf.at[b], in_sem.at[2, b]),
            pltpu.make_async_copy(q.at[0, rows_of(b), lanes(low, span)], x_buf.at[b], in_sem.at[2, b]),
        )

    small = start_small(router, blocks, router_buf, blocks_buf, small_sem)
    for j in range(shard_blocks):
        g_load, v_load, k_load, q_load = loads(
            jnp.where(for_query, j, shard_blocks - 1 - j)
        )
        g_load.start()
        v_load.start()
        pl.when(for_query)(k_load.start)
        pl.when(jnp.logical_not(for_query))(q_load.start)

    allowed = row_minus_column() * sign >= 0
    for copy in small:
        copy.wait()
    count = live_count(blocks_buf)

    for i in range(slots):
        @pl.when(i < count)
        def _():
            n = jnp.where(for_query, i, count - 1 - i)
            b = blocks_buf[0, 0, n]
            g_load, v_load, x_load, _ = loads(b)
            weight = down_rows(router_buf, b)
            g_load.wait()
            for h in range(span):
                vc_buf[1, b, :, lanes(h)] = (
                    weight * g_buf[b, :, lanes(h)].astype(jnp.float32)
                ).astype(jnp.bfloat16)
            v_load.wait()
            x_load.wait()
            for h in range(low, high):
                at = lanes(h - low)
                l_h = vc_buf[left, b, :, at]
                r_h = vc_buf[right, b, :, at]
                x_h = x_buf[b, :, at]
                if i > 0:
                    so_far = acc[h - low]
                elif seeded:
                    so_far = seed[h]
                else:
                    so_far = None
                if so_far is not None:
                    state = so_far.astype(jnp.bfloat16)
                if begin <= h < end:
                    scores = jnp.where(allowed, dot_nt(l_h, r_h), 0.0).astype(jnp.bfloat16)
                    if so_far is None:
                        out = dot(scores, x_h)
                    else:
                        out = dot(
                            jnp.concatenate([scores, l_h], axis=1),
                            jnp.concatenate([x_h, state], axis=0),
                        )
                    chunk[rows_of(n), lanes(h - begin)] = (factor * out).astype(jnp.bfloat16)
                if keep:
                    states[n, h] = (
                        jnp.zeros((HEAD_SIZE, HEAD_SIZE), jnp.bfloat16)
                        if so_far is None else state
                    )
                added = dot_tn(r_h, x_h)
                acc[h - low] = added if so_far is None else so_far + added

        @pl.when(i >= count)
        def _():
            chunk[rows_of(i), :] = jnp.zeros((BLOCK_ROWS, chunk.shape[1]), chunk.dtype)

    if keep:
        total[...] = acc[...]

    def wait(b):
        g_load, v_load, x_load, _ = loads(b)
        g_load.wait()
        v_load.wait()
        x_load.wait()

    drain(blocks_buf, count, slots, shard_blocks, wait)


def side(factor, query_side, begin, end, keep, small, arrays, seed=None):
    router, blocks = small
    _, shard_rows, width = arrays[0].shape
    shard_blocks = shard_rows // BLOCK_ROWS
    heads = width // HEAD_SIZE
    slots = blocks.shape[2]
    span = heads if keep else end - begin
    tile = (shard_blocks, BLOCK_ROWS, span * HEAD_SIZE)
    out_shape = [pltpu.VMEM((slots * BLOCK_ROWS, (end - begin) * HEAD_SIZE), jnp.bfloat16)]
    if keep:
        out_shape.append(pltpu.VMEM((heads, HEAD_SIZE, HEAD_SIZE), jnp.float32))
        out_shape.append(pltpu.VMEM((slots, heads, HEAD_SIZE, HEAD_SIZE), jnp.bfloat16))
    extra = () if seed is None else (seed,)
    return pl.pallas_call(
        functools.partial(
            side_kernel, factor, query_side, begin, end, keep, seed is not None
        ),
        name="side",
        out_shape=out_shape,
        in_specs=[HBM] * 6 + [VMEM] * len(extra),
        out_specs=[VMEM] * len(out_shape),
        scratch_shapes=small_scratch(*small)
        + [
            pltpu.VMEM(tile, jnp.bfloat16),
            pltpu.VMEM((2,) + tile, jnp.bfloat16),
            pltpu.VMEM(tile, jnp.bfloat16),
            pltpu.VMEM((span, HEAD_SIZE, HEAD_SIZE), jnp.float32),
            pltpu.SemaphoreType.DMA((3, shard_blocks)),
        ],
        compiler_params=compiler_params(),
        cost_estimate=cost(5 * slots * span, 8 * shard_rows * span * HEAD_SIZE),
    )(router, blocks, *arrays, *extra)


def value_kernel(
    factor, take_one, router, blocks, q, k, v, g, one, two, chunk,
    router_buf, blocks_buf, small_sem, q_buf, k_buf, g_buf, in_sem,
):
    del v
    slots = blocks_buf.shape[2]
    shard_blocks, _, width = q_buf.shape
    heads = width // HEAD_SIZE
    pick_one = take_one()

    def loads(b):
        return [
            pltpu.make_async_copy(source.at[0, rows_of(b)], buf.at[b], in_sem.at[j, b])
            for j, (source, buf) in enumerate(((q, q_buf), (k, k_buf), (g, g_buf)))
        ]

    small = start_small(router, blocks, router_buf, blocks_buf, small_sem)
    for b in range(shard_blocks):
        for load in loads(b):
            load.start()
    allowed = row_minus_column() <= 0
    for copy in small:
        copy.wait()
    count = live_count(blocks_buf)

    for n in range(slots):
        @pl.when(n < count)
        def _():
            b = blocks_buf[0, 0, n]
            weight = down_rows(router_buf, b)
            for load in loads(b):
                load.wait()
            for h in range(heads):
                q_h = q_buf[b, :, lanes(h)]
                k_h = k_buf[b, :, lanes(h)]
                c_h = (weight * g_buf[b, :, lanes(h)].astype(jnp.float32)).astype(jnp.bfloat16)
                state = jnp.where(pick_one, one[n, h], two[n, h])
                scores = jnp.where(allowed, dot_nt(k_h, q_h), 0.0).astype(jnp.bfloat16)
                out = dot(scores, c_h) + dot_nt(k_h, state)
                chunk[rows_of(n), lanes(h)] = (factor * out).astype(jnp.bfloat16)

        @pl.when(n >= count)
        def _():
            chunk[rows_of(n), :] = jnp.zeros((BLOCK_ROWS, width), chunk.dtype)

    def wait(b):
        for load in loads(b):
            load.wait()

    drain(blocks_buf, count, slots, shard_blocks, wait)


def value_side(factor, take_one, small, arrays, one, two):
    router, blocks = small
    _, shard_rows, width = arrays[0].shape
    shard_blocks = shard_rows // BLOCK_ROWS
    heads = width // HEAD_SIZE
    slots = blocks.shape[2]
    tile = (shard_blocks, BLOCK_ROWS, width)
    return pl.pallas_call(
        functools.partial(value_kernel, factor, take_one),
        name="value_side",
        out_shape=pltpu.VMEM((slots * BLOCK_ROWS, width), jnp.bfloat16),
        in_specs=[HBM] * 6 + [VMEM] * 2,
        out_specs=VMEM,
        scratch_shapes=small_scratch(*small)
        + [pltpu.VMEM(tile, jnp.bfloat16)] * 3
        + [pltpu.SemaphoreType.DMA((3, shard_blocks))],
        compiler_params=compiler_params(),
        cost_estimate=cost(3 * slots * heads, 8 * shard_rows * width),
    )(router, blocks, *arrays, one, two)


def router_kernel(
    factor, take_one, router, blocks, q, k, v, g, one, two, partial,
    router_buf, blocks_buf, small_sem, q_buf, k_buf, v_buf, g_buf, in_sem,
):
    slots = blocks_buf.shape[2]
    shard_blocks, _, width = q_buf.shape
    heads = width // HEAD_SIZE
    pick_one = take_one()

    def loads(b):
        return [
            pltpu.make_async_copy(source.at[0, rows_of(b)], buf.at[b], in_sem.at[j, b])
            for j, (source, buf) in enumerate(((q, q_buf), (k, k_buf), (v, v_buf), (g, g_buf)))
        ]

    small = start_small(router, blocks, router_buf, blocks_buf, small_sem)
    for b in range(shard_blocks):
        for load in loads(b):
            load.start()
    allowed = row_minus_column() >= 0
    for copy in small:
        copy.wait()
    count = live_count(blocks_buf)

    for n in range(slots):
        @pl.when(n < count)
        def _():
            b = blocks_buf[0, 0, n]
            for load in loads(b):
                load.wait()
            by_row = jnp.zeros((BLOCK_ROWS, HEAD_SIZE), jnp.float32)
            for h in range(heads):
                q_h = q_buf[b, :, lanes(h)]
                k_h = k_buf[b, :, lanes(h)]
                v_h = v_buf[b, :, lanes(h)]
                state = jnp.where(pick_one, one[n, h], two[n, h])
                scores = jnp.where(allowed, dot_nt(q_h, k_h), 0.0).astype(jnp.bfloat16)
                core = factor * (dot(scores, v_h) + dot_nt(q_h, state))
                by_row = by_row + g_buf[b, :, lanes(h)].astype(jnp.float32) * core
            partial[0:1, rows_of(n)] = jnp.sum(by_row.T, axis=0, keepdims=True)

        @pl.when(n >= count)
        def _():
            partial[0:1, rows_of(n)] = jnp.zeros((1, BLOCK_ROWS), jnp.float32)

    def wait(b):
        for load in loads(b):
            load.wait()

    drain(blocks_buf, count, slots, shard_blocks, wait)


def router_side(factor, take_one, small, arrays, one, two):
    router, blocks = small
    _, shard_rows, width = arrays[0].shape
    shard_blocks = shard_rows // BLOCK_ROWS
    heads = width // HEAD_SIZE
    slots = blocks.shape[2]
    tile = (shard_blocks, BLOCK_ROWS, width)
    return pl.pallas_call(
        functools.partial(router_kernel, factor, take_one),
        name="router_side",
        out_shape=jax.ShapeDtypeStruct((1, slots * BLOCK_ROWS), jnp.float32),
        in_specs=[HBM] * 6 + [VMEM] * 2,
        out_specs=VMEM,
        scratch_shapes=small_scratch(*small)
        + [pltpu.VMEM(tile, jnp.bfloat16)] * 4
        + [pltpu.SemaphoreType.DMA((4, shard_blocks))],
        compiler_params=compiler_params(),
        cost_estimate=cost(3 * slots * heads, 8 * shard_rows * width),
    )(router, blocks, *arrays, one, two)


def place_kernel(section_of, begin, *refs):
    chunk, out, sem = refs[-3:]
    width = chunk.shape[1] // HEAD_SIZE
    copy = pltpu.make_async_copy(chunk, out.at[0, section_of(), :, lanes(begin, width)], sem)
    copy.start()
    copy.wait()


def place(whole, chunk, shape, section_of, begin):
    rows, width = chunk.shape
    operands = (chunk,) if whole is None else (whole, chunk)
    return pl.pallas_call(
        functools.partial(place_kernel, section_of, begin),
        name="place",
        out_shape=jax.ShapeDtypeStruct(shape, chunk.dtype),
        in_specs=[HBM] * (len(operands) - 1) + [ANY],
        out_specs=HBM,
        scratch_shapes=[pltpu.SemaphoreType.DMA],
        input_output_aliases={} if whole is None else {0: 0},
        compiler_params=pltpu.CompilerParams(vmem_limit_bytes=2**20),
        cost_estimate=cost(0, 4 * rows * width),
    )(*operands)


def shard_states(queries, keys, values, grad_out, router, blocks, counts):
    heads = queries.shape[2] // HEAD_SIZE
    slots = blocks.shape[2]
    shard_blocks = queries.shape[1] // BLOCK_ROWS
    live = jnp.arange(slots, dtype=jnp.int32) < counts[0, 0]
    taken = (blocks[0, 0, :, None] == jnp.arange(shard_blocks, dtype=jnp.int32)) & live[:, None]
    mask = jnp.repeat(jnp.any(taken, axis=0), BLOCK_ROWS)[:, None]

    def rows(array):
        picked = jnp.where(mask, array[0], jnp.zeros((), array.dtype))
        return picked.reshape(-1, heads, HEAD_SIZE)

    weighted = (router[0][:, None, None] * rows(grad_out).astype(jnp.float32)).astype(jnp.bfloat16)
    key_value = jnp.einsum(
        "the,thd->hed", rows(values), rows(keys), preferred_element_type=jnp.float32
    )
    query_grad = jnp.einsum(
        "the,thd->hed", weighted, rows(queries), preferred_element_type=jnp.float32
    )
    return key_value, query_grad


def own_side():
    return jnp.where(is_first(), 0, 1)


def other_side():
    return jnp.where(is_first(), 1, 0)


def on_device(queries, keys, values, grad_out, router, blocks, counts):
    slots = blocks.shape[2]
    rows = slots * BLOCK_ROWS
    width = queries.shape[2]
    heads = width // HEAD_SIZE
    seq_count = lax.axis_size("seq")
    factor = 1.0 / math.sqrt(HEAD_SIZE * rows * seq_count)
    arrays = tuple(in_hbm(x) for x in (queries, keys, values, grad_out))
    small = (in_hbm(router), in_hbm(blocks))
    shape = (1, 3, rows, width)
    if seq_count == 2:
        head_start = max(1, heads // 3)

        def sent(x, axis="pipe", by=-1):
            return from_behind(x, axis, by)

        def kernel(call, *operands):
            return call(factor, *operands)

        (chunk_a,) = kernel(side, is_first, 0, head_start, False, small, arrays)
        chunk_a = sent(chunk_a)
        chunk_b, total, own = kernel(side, is_first, head_start, heads, True, small, arrays)
        total = sent(total, "seq", 1)
        chunk_b = sent(chunk_b)
        chunk_c, _, other = kernel(side, is_last, 0, heads, True, small, arrays, total)
        chunk_c = sent(chunk_c)
        chunk_d = kernel(value_side, is_last, small, arrays, own, other)
        chunk_d = sent(chunk_d)
        partial = kernel(router_side, is_first, small, arrays, own, other)
        handed = place(None, chunk_a, shape, own_side, 0)
        handed = place(handed, chunk_b, shape, own_side, head_start)
        handed = place(handed, chunk_c, shape, other_side, 0)
        handed = place(handed, chunk_d, shape, lambda: 2, 0)
    else:
        index = lax.axis_index("seq")
        places = jnp.arange(seq_count)[:, None, None, None]
        key_value, query_grad = shard_states(queries, keys, values, grad_out, router, blocks, counts)
        gathered = lax.all_gather(key_value, "seq")
        earlier = jnp.sum(jnp.where(places < index, gathered, 0.0), axis=0)
        gathered = lax.all_gather(query_grad, "seq")
        later = jnp.sum(jnp.where(places > index, gathered, 0.0), axis=0)
        d_query, _, before = side(factor, always, 0, heads, True, small, arrays, earlier)
        d_key, _, after = side(factor, never, 0, heads, True, small, arrays, later)
        d_value = value_side(factor, always, small, arrays, after, after)
        partial = router_side(factor, always, small, arrays, before, before)
        handed = None
        for section, chunk in enumerate((d_query, d_key, d_value)):
            chunk = from_behind(chunk, "pipe", -1)
            handed = place(handed, chunk, shape, functools.partial(int, section), 0)
    router_grad = lax.psum(partial, "tp")
    return (handed, router_grad)


def solution(mesh):
    return jax.shard_map(
        on_device,
        mesh=mesh,
        in_specs=(
            P("pipe", "seq", "tp"),
            P("pipe", "seq", "tp"),
            P("pipe", "seq", "tp"),
            P("pipe", "seq", "tp"),
            P("pipe", "seq"),
            P("pipe", "seq", None),
            P("pipe", "seq"),
        ),
        out_specs=(P("pipe", None, "seq", "tp"), P("pipe", "seq")),
        check_vma=False,
    )
```

time: 112 us -> 74.6 us (0.67)
  local copies, waits for them, and re-layouts: 28.5 us -> 0 us
  matrix products: 25.3 us -> 0 us
  Pallas kernels: 0 us -> 23.9 us
  other arithmetic: 8.97 us -> 0 us
  waiting for transfers between devices: 25.4 us -> 30.4 us
  blocking collectives: 17.7 us -> 13.6 us
  starting transfers between devices: 3.82 us -> 5.63 us
    dot_general x17 -> x0, matrix products: 25.3 us -> none  [the longest x4 7.09 us: select(): jnp.einsum('jb,btf->jtf', picker_half, grouped, preferred_element_type=jn...]
    pallas_call x0 -> x9, Pallas kernels: none -> 23.9 us  [the longest x3 12.3 us: side(): pl.pallas_call(functools.partial(side_kernel, factor, query_side, begin,...]
    another operation x3 -> x0, local copies, waits for them, and re-layouts: 7.38 us -> none  [on_device(): jnp.stack([query_gradient, key_gradient, value_gradient])]
    mul x3 -> x0, local copies, waits for them, and re-layouts: 6.98 us -> none  [the longest x1 2.37 us: on_device(): factor * (jnp.einsum('nhts,nthe->nshe', scores, output_gradient, preferre...]
    another operation x3 -> x0, other arithmetic: 5.59 us -> none  [the longest x1 2.88 us: on_device(): jnp.stack([query_gradient, key_gradient, value_gradient])]
    all_gather x2 -> x0, blocking collectives: 5.1 us -> none  [carried_in(): gathered = lax.all_gather(part, axis)]
    ppermute x1 -> x5, waiting for transfers between devices: 25.4 us -> 30.4 us  [from_behind(): return lax.ppermute(x, axis, [(i, (i + by) % count) for i in range(count)])]
    unnamed x20 -> x0, local copies, waits for them, and re-layouts: 4.28 us -> none
  transfers between devices with their start and end apart: 1 -> 5, of which waited for: 1 -> 2; matrix products, arithmetic and copies ran while one was open for 1% -> 0% of each run, Pallas kernels for 0% -> 18%
where the time goes in v1:
time: 74.6 us; the launch traced here: 74.3 us
  waiting for transfers between devices  30.4 us (41%)
  Pallas kernels  23.9 us (32%)
  blocking collectives  13.6 us (18%)
  starting transfers between devices  5.63 us (8%)
    ppermute x5, waiting for transfers between devices, from_behind(): return lax.ppermute(x, axis, [(i, (i + by) % count) for i in range(count)])  30.4 us
    psum x1, blocking collectives, on_device(): router_grad = lax.psum(partial, 'tp')  13.6 us
    pallas_call x3, Pallas kernels, side(): pl.pallas_call(functools.partial(side_kernel, factor, query_side, begin,...  12.3 us
    ppermute x5, starting transfers between devices, from_behind(): return lax.ppermute(x, axis, [(i, (i + by) % count) for i in range(count)])  5.63 us
    pallas_call x1, Pallas kernels, router_side(): pl.pallas_call(functools.partial(router_kernel, factor, take_one), name='...  4.45 us
    pallas_call x1, Pallas kernels, value_side(): pl.pallas_call(functools.partial(value_kernel, factor, take_one), name='v...  4.09 us
    pallas_call x4, Pallas kernels, place(): pl.pallas_call(functools.partial(place_kernel, section_of, begin), name='...  3.1 us
  transfers between devices with their start and end apart: 5, of which 2 were waited for; matrix products, arithmetic and copies ran while one was open for 0% of the time, Pallas kernels for 18%

profile of v1, /device:TPU:0, one launch (start us, length us, event | category | flops | bytes accessed | tf_op | source)
XLA Modules:
  0.0 74.3 jit_solution(8927431036765508321)
XLA Ops:
  0.6 4.0 %side.4 = (bf16[384,512]{1,0:T(8,128)(2,1)S(1)}, f32[6,128,128]{2,1,0:T(8,128)S(1)}, bf16[3,6,128,128]{3,2,1,0:T(8,128)(2,1)S(1)}) custom-call(f32[1,512]{1,0:T(1,128)} %router.3, s32[1,1,3]{2,1,0:T(1,128)} %blocks.3, bf16[1,512,768]{2,1,0:T(8,128)(2,1)} %q.3, bf16[1,512,768]{2,1,0:T(8,128)(2,1)} %k.3, bf16[1,512,768]{2,1,0:T(8,128)(2,1)} %v.3, ...), custom_call_target="tpu_custom_call" | custom-call | flops 377487360 | bytes 3145728 | tf_op jit(solution)/shard_map/side/pallas_call | solution.py:243
  4.6 0.6 collective-permute-start.2
  5.2 1.3 %collective-permute-done.2.refs_6_ = f32[6,128,128]{2,1,0:T(8,128)S(1)} collective-permute-done((f32[6,128,128]{2,1,0:T(8,128)S(1)}, f32[6,128,128]{2,1,0:T(8,128)S(1)}, u32[]{:S(2)}, u32[]{:S(2)}) %collective-permute-start.2) | collective-permute-done | bytes 393248 | tf_op jit(solution)/shard_map/ppermute | solution.py:24
  6.5 5.6 %side.5 = (bf16[384,768]{1,0:T(8,128)(2,1)S(1)}, f32[6,128,128]{2,1,0:T(8,128)}, bf16[3,6,128,128]{3,2,1,0:T(8,128)(2,1)S(1)}) custom-call(f32[1,512]{1,0:T(1,128)} %router.3, s32[1,1,3]{2,1,0:T(1,128)} %blocks.3, bf16[1,512,768]{2,1,0:T(8,128)(2,1)} %q.3, bf16[1,512,768]{2,1,0:T(8,128)(2,1)} %k.3, bf16[1,512,768]{2,1,0:T(8,128)(2,1)} %v.3, ...), custom_call_target="tpu_custom_call" | custom-call | flops 377487360 | bytes 3145728 | tf_op jit(solution)/shard_map/side/pallas_call | solution.py:243
  12.2 0.1 collective-permute-start.3
  12.2 4.1 %value_side.1 = bf16[384,768]{1,0:T(8,128)(2,1)S(1)} custom-call(f32[1,512]{1,0:T(1,128)} %router.3, s32[1,1,3]{2,1,0:T(1,128)} %blocks.3, bf16[1,512,768]{2,1,0:T(8,128)(2,1)} %q.3, bf16[1,512,768]{2,1,0:T(8,128)(2,1)} %k.3, bf16[1,512,768]{2,1,0:T(8,128)(2,1)} %v.3, bf16[1,512,768]{2,1,0:T(8,128)(2,1)} %g.3, ...), custom_call_target="tpu_custom_call" | custom-call | flops 226492416 | bytes 3145728 | tf_op jit(solution)/shard_map/value_side/pallas_call | solution.py:323
  16.3 0.8 %collective-permute-start.4 = (bf16[384,768]{1,0:T(8,128)(2,1)S(1)}, bf16[384,768]{1,0:T(8,128)(2,1)S(1)}, u32[]{:S(2)}, u32[]{:S(2)}) collective-permute-start(bf16[384,768]{1,0:T(8,128)(2,1)S(1)} %value_side.1), channel_id=1, source_target_pairs={{0,12},{4,0},{8,4},{12,8},{1,13},{5,1},{9,5},{13,9},{2,14},{6,2},{... | collective-permute-start | bytes 1769480 | tf_op jit(solution)/shard_map/ppermute | solution.py:24
  17.1 4.2 %collective-permute-start.1 = (bf16[384,512]{1,0:T(8,128)(2,1)S(1)}, bf16[384,512]{1,0:T(8,128)(2,1)S(1)}, u32[]{:S(2)}, u32[]{:S(2)}) collective-permute-start(bf16[384,512]{1,0:T(8,128)(2,1)S(1)} %get-tuple-element.7), channel_id=1, source_target_pairs={{0,12},{4,0},{8,4},{12,8},{1,13},{5,1},{9,5},{13,9},{2,14},{6,2},{... | collective-permute-start | bytes 1179656 | tf_op jit(solution)/shard_map/ppermute | solution.py:24
  21.3 2.7 %side.3 = bf16[384,256]{1,0:T(8,128)(2,1)S(1)} custom-call(f32[1,512]{1,0:T(1,128)} %router.3, s32[1,1,3]{2,1,0:T(1,128)} %blocks.3, bf16[1,512,768]{2,1,0:T(8,128)(2,1)} %q.3, bf16[1,512,768]{2,1,0:T(8,128)(2,1)} %k.3, bf16[1,512,768]{2,1,0:T(8,128)(2,1)} %v.3, bf16[1,512,768]{2,1,0:T(8,128)(2,1)} %g.3), custom_call_target="tpu_custom_call" | custom-call | flops 125829120 | bytes 1048576 | tf_op jit(solution)/shard_map/side/pallas_call | solution.py:243
  24.0 0.1 collective-permute-start
  24.0 29.1 %collective-permute-done.refs_0_ = bf16[384,256]{1,0:T(8,128)(2,1)S(1)} collective-permute-done((bf16[384,256]{1,0:T(8,128)(2,1)S(1)}, bf16[384,256]{1,0:T(8,128)(2,1)S(1)}, u32[]{:S(2)}, u32[]{:S(2)}) %collective-permute-start) | collective-permute-done | bytes 196640 | tf_op jit(solution)/shard_map/ppermute | solution.py:24
  53.1 0.7 place.4.refs_0_
  53.8 0.0 collective-permute-done.1.refs_1_
  53.8 0.8 %place.5.refs_0_ = bf16[1,3,384,768]{3,2,1,0:T(8,128)(2,1)} custom-call(bf16[1,3,384,768]{3,2,1,0:T(8,128)(2,1)} %place.4.refs_0_, bf16[384,512]{1,0:T(8,128)(2,1)S(1)} %collective-permute-done.1.refs_1_), custom_call_target="tpu_custom_call", output_to_operand_aliasing={{}: (0, {})} | custom-call | bytes 786432 | tf_op jit(solution)/shard_map/place/pallas_call | solution.py:421
  54.6 4.5 %router_side.1 = f32[1,384]{1,0:T(1,128)S(1)} custom-call(f32[1,512]{1,0:T(1,128)} %router.3, s32[1,1,3]{2,1,0:T(1,128)} %blocks.3, bf16[1,512,768]{2,1,0:T(8,128)(2,1)} %q.3, bf16[1,512,768]{2,1,0:T(8,128)(2,1)} %k.3, bf16[1,512,768]{2,1,0:T(8,128)(2,1)} %v.3, bf16[1,512,768]{2,1,0:T(8,128)(2,1)} %g.3, bf16[3,6,128,128]{3,2,1,0:T(8,128)(2,1)S(1)} %get-tuple-element.10.one, ...), custom_call_target="tpu_custom_call" | custom-call | flops 226492416 | bytes 3145728 | tf_op jit(solution)/shard_map/router_side/pallas_call | solution.py:396
  59.0 13.6 %psum.7 = f32[1,384]{1,0:T(1,128)} all-reduce(f32[1,384]{1,0:T(1,128)S(1)} %router_side.1), channel_id=1, replica_groups=mesh['seq'=2,'pipe'=4,'tp'=4] {'tp'}, use_global_device_ids=true, to_apply=%region_0.0 | all-reduce | flops 384 | bytes 3072 | tf_op jit(solution)/shard_map/psum | solution.py:513
  72.7 0.0 collective-permute-done.3.refs_1_
  72.7 0.8 %place.6.refs_0_ = bf16[1,3,384,768]{3,2,1,0:T(8,128)(2,1)} custom-call(bf16[1,3,384,768]{3,2,1,0:T(8,128)(2,1)} %place.5.refs_0_, bf16[384,768]{1,0:T(8,128)(2,1)S(1)} %collective-permute-done.3.refs_1_), custom_call_target="tpu_custom_call", output_to_operand_aliasing={{}: (0, {})} | custom-call | bytes 1179648 | tf_op jit(solution)/shard_map/place/pallas_call | solution.py:421
  73.5 0.0 collective-permute-done.4.refs_1_
  73.5 0.8 %place.7 = bf16[1,3,384,768]{3,2,1,0:T(8,128)(2,1)} custom-call(bf16[1,3,384,768]{3,2,1,0:T(8,128)(2,1)} %place.6.refs_0_, bf16[384,768]{1,0:T(8,128)(2,1)S(1)} %collective-permute-done.4.refs_1_), custom_call_target="tpu_custom_call", output_to_operand_aliasing={{}: (0, {})} | custom-call | bytes 1179648 | tf_op jit(solution)/shard_map/place/pallas_call | solution.py:421
Async XLA Ops:
  4.6 1.9 %collective-permute-start.2 = (f32[6,128,128]{2,1,0:T(8,128)S(1)}, f32[6,128,128]{2,1,0:T(8,128)S(1)}, u32[]{:S(2)}, u32[]{:S(2)}) collective-permute-start(f32[6,128,128]{2,1,0:T(8,128)S(1)} %get-tuple-element.8), channel_id=1, source_target_pairs={{0,16},{16,0},{1,17},{17,1},{2,18},{18,2},{3,19},{19,3},{4,20},{20... | collective-permute-start | bytes 1179656 | tf_op jit(solution)/shard_map/ppermute | solution.py:24
  12.2 60.5 %collective-permute-start.3 = (bf16[384,768]{1,0:T(8,128)(2,1)S(1)}, bf16[384,768]{1,0:T(8,128)(2,1)S(1)}, u32[]{:S(2)}, u32[]{:S(2)}) collective-permute-start(bf16[384,768]{1,0:T(8,128)(2,1)S(1)} %get-tuple-element.9), channel_id=1, source_target_pairs={{0,12},{4,0},{8,4},{12,8},{1,13},{5,1},{9,5},{13,9},{2,14},{6,2},{... | collective-permute-start | bytes 1769480 | tf_op jit(solution)/shard_map/ppermute | solution.py:24
  16.3 57.2 %collective-permute-start.4 = (bf16[384,768]{1,0:T(8,128)(2,1)S(1)}, bf16[384,768]{1,0:T(8,128)(2,1)S(1)}, u32[]{:S(2)}, u32[]{:S(2)}) collective-permute-start(bf16[384,768]{1,0:T(8,128)(2,1)S(1)} %value_side.1), channel_id=1, source_target_pairs={{0,12},{4,0},{8,4},{12,8},{1,13},{5,1},{9,5},{13,9},{2,14},{6,2},{... | collective-permute-start | bytes 1769480 | tf_op jit(solution)/shard_map/ppermute | solution.py:24
  17.1 36.7 %collective-permute-start.1 = (bf16[384,512]{1,0:T(8,128)(2,1)S(1)}, bf16[384,512]{1,0:T(8,128)(2,1)S(1)}, u32[]{:S(2)}, u32[]{:S(2)}) collective-permute-start(bf16[384,512]{1,0:T(8,128)(2,1)S(1)} %get-tuple-element.7), channel_id=1, source_target_pairs={{0,12},{4,0},{8,4},{12,8},{1,13},{5,1},{9,5},{13,9},{2,14},{6,2},{... | collective-permute-start | bytes 1179656 | tf_op jit(solution)/shard_map/ppermute | solution.py:24
  24.0 29.1 %collective-permute-start = (bf16[384,256]{1,0:T(8,128)(2,1)S(1)}, bf16[384,256]{1,0:T(8,128)(2,1)S(1)}, u32[]{:S(2)}, u32[]{:S(2)}) collective-permute-start(bf16[384,256]{1,0:T(8,128)(2,1)S(1)} %side.3), channel_id=1, source_target_pairs={{0,12},{4,0},{8,4},{12,8},{1,13},{5,1},{9,5},{13,9},{2,14},{6,2},{... | collective-permute-start | bytes 589832 | tf_op jit(solution)/shard_map/ppermute | solution.py:24

commit v2 on v0

v2 whole, which is shorter than its diff:
```python
import functools
import math

import jax
import jax.numpy as jnp
from jax import lax
from jax.experimental import pallas as pl
from jax.experimental.pallas import tpu as pltpu
from jax.sharding import PartitionSpec as P


HEAD_SIZE = 128
BLOCK_ROWS = 128
GRANT = 16 * 2**20


ANY = pl.BlockSpec(memory_space=pl.ANY)
HBM = pl.BlockSpec(memory_space=pltpu.HBM)
VMEM = pl.BlockSpec(memory_space=pltpu.VMEM)
SMEM = pl.BlockSpec(memory_space=pltpu.SMEM)


def from_behind(x, axis, by):
    count = lax.axis_size(axis)
    return lax.ppermute(x, axis, [(i, (i + by) % count) for i in range(count)])


def in_hbm(x):
    return pltpu.with_memory_space_constraint(x, pltpu.HBM)


def dot(a, b):
    return jnp.dot(a, b, preferred_element_type=jnp.float32)


def dot_nt(a, b):
    return lax.dot_general(a, b, (((1,), (1,)), ((), ())), preferred_element_type=jnp.float32)


def dot_tn(a, b):
    return lax.dot_general(a, b, (((0,), (0,)), ((), ())), preferred_element_type=jnp.float32)


def lanes(h, count=1):
    return pl.ds(h * HEAD_SIZE, count * HEAD_SIZE)


def rows_of(n):
    if isinstance(n, int):
        return pl.ds(n * BLOCK_ROWS, BLOCK_ROWS)
    return pl.ds(pl.multiple_of(n * BLOCK_ROWS, BLOCK_ROWS), BLOCK_ROWS)


def down_rows(router, block):
    weight = router[0:1, rows_of(block)]
    return jnp.broadcast_to(weight, (BLOCK_ROWS, BLOCK_ROWS)).T


def row_minus_column():
    shape = (BLOCK_ROWS, BLOCK_ROWS)
    return lax.broadcasted_iota(jnp.int32, shape, 0) - lax.broadcasted_iota(jnp.int32, shape, 1)


def compiler_params():
    return pltpu.CompilerParams(vmem_limit_bytes=GRANT)


def cost(matmuls, moved):
    return pl.CostEstimate(
        flops=2 * matmuls * HEAD_SIZE**3, bytes_accessed=moved, transcendentals=0
    )


def is_first():
    return lax.axis_index("seq") == 0


def is_last():
    return lax.axis_index("seq") != 0


def always():
    return True


def never():
    return False


def live_of(blocks, n):
    return jnp.bool_(True) if n == 0 else blocks[0, 0, n] > 0


def by_role(query_side, body):
    flag = query_side()
    if isinstance(flag, bool):
        body(flag)
    else:
        pl.when(flag)(lambda: body(True))
        pl.when(jnp.logical_not(flag))(lambda: body(False))


def in_order(query, slots):
    return list(range(slots)) if query else list(reversed(range(slots)))


def weigh(weight, grad):
    return (weight * grad.astype(jnp.float32)).astype(jnp.bfloat16)


def open_kernel(
    factor, query_side, end, router, blocks, q, k, v, g, chunk, q_all, k_all, v_all, g_all,
    router_all, blocks_all, acc, small_sem, head_sem, rest_sem,
):
    slots = blocks.shape[2]
    heads = q_all.shape[1] // HEAD_SIZE
    small = [
        pltpu.make_async_copy(blocks, blocks_all, small_sem.at[0]),
        pltpu.make_async_copy(router, router_all, small_sem.at[1]),
    ]
    pairs = ((g, g_all), (v, v_all), (k, k_all), (q, q_all))
    first_loads = [
        pltpu.make_async_copy(
            source.at[0, :, lanes(0, end)], target.at[:, lanes(0, end)], head_sem.at[j]
        )
        for j, (source, target) in enumerate(pairs)
    ]
    rest_loads = [
        pltpu.make_async_copy(
            source.at[0, :, lanes(end, heads - end)],
            target.at[:, lanes(end, heads - end)],
            rest_sem.at[j],
        )
        for j, (source, target) in enumerate(pairs)
    ]
    for load in small + first_loads + rest_loads:
        load.start()
    difference = row_minus_column()
    for load in small:
        load.wait()
    for load in first_loads:
        load.wait()

    def body(query):
        allowed = difference >= 0 if query else difference <= 0
        x_all = k_all if query else q_all
        order = in_order(query, slots)
        for i, n in enumerate(order):
            live = live_of(blocks_all, n)
            block = blocks_all[0, 0, n]
            rows = rows_of(block)
            weight = jnp.where(live, down_rows(router_all, block), 0.0)
            scale = jnp.where(live, factor, 0.0)
            for h in range(end):
                c_h = weigh(weight, g_all[rows, lanes(h)])
                v_h = v_all[rows, lanes(h)]
                l_h, r_h = (c_h, v_h) if query else (v_h, c_h)
                x_h = x_all[rows, lanes(h)]
                scores = jnp.where(allowed, dot_nt(l_h, r_h), 0.0).astype(jnp.bfloat16)
                if i == 0:
                    out = dot(scores, x_h)
                else:
                    out = dot(
                        jnp.concatenate([scores, l_h], axis=1),
                        jnp.concatenate([x_h, acc[h].astype(jnp.bfloat16)], axis=0),
                    )
                chunk[rows_of(n), lanes(h)] = (scale * out).astype(jnp.bfloat16)
                if i + 1 < slots:
                    added = dot_tn(r_h, x_h)
                    acc[h] = added if i == 0 else acc[h] + added

    by_role(query_side, body)
    for load in rest_loads:
        load.wait()


def opened(factor, query_side, end, small, arrays):
    router, blocks = small
    _, shard_rows, width = arrays[0].shape
    slots = blocks.shape[2]
    whole = pltpu.VMEM((shard_rows, width), jnp.bfloat16)
    out_shape = [
        pltpu.VMEM((slots * BLOCK_ROWS, end * HEAD_SIZE), jnp.bfloat16),
        whole, whole, whole, whole,
        pltpu.VMEM(router.shape, router.dtype),
        pltpu.SMEM(blocks.shape, blocks.dtype),
    ]
    return pl.pallas_call(
        functools.partial(open_kernel, factor, query_side, end),
        name="opened",
        out_shape=out_shape,
        in_specs=[HBM] * 6,
        out_specs=[VMEM] * 6 + [SMEM],
        scratch_shapes=[
            pltpu.VMEM((end, HEAD_SIZE, HEAD_SIZE), jnp.float32),
            pltpu.SemaphoreType.DMA((2,)),
            pltpu.SemaphoreType.DMA((4,)),
            pltpu.SemaphoreType.DMA((4,)),
        ],
        compiler_params=compiler_params(),
        cost_estimate=cost(4 * slots * end, 8 * shard_rows * width),
    )(router, blocks, *arrays)


def side_kernel(factor, query_side, begin, make_c, *refs):
    (router, blocks, q, k, v, g), refs = refs[:6], refs[6:]
    if make_c:
        chunk, states, total, c_all, scores_buf = refs
    else:
        c_all, seed, chunk, states, scores_buf, total = refs
    slots = blocks.shape[2]
    heads = states.shape[1]
    difference = row_minus_column()

    def body(query):
        allowed = difference >= 0 if query else difference <= 0
        x_all = k if query else q
        order = in_order(query, slots)
        for i, n in enumerate(order):
            live = live_of(blocks, n)
            block = blocks[0, 0, n]
            rows = rows_of(block)
            own = rows_of(n)
            scale = jnp.where(live, factor, 0.0)
            if make_c:
                weight = jnp.where(live, down_rows(router, block), 0.0)
                for h in range(heads):
                    c_all[own, lanes(h)] = weigh(weight, g[rows, lanes(h)])

            def sides(h):
                c_h, v_h = c_all[own, lanes(h)], v[rows, lanes(h)]
                return (c_h, v_h) if query else (v_h, c_h)

            for h in range(begin, heads):
                l_h, r_h = sides(h)
                scores_buf[n, h] = jnp.where(allowed, dot_nt(l_h, r_h), 0.0).astype(jnp.bfloat16)
            for h in range(heads):
                if i > 0:
                    so_far = total[h]
                elif make_c:
                    so_far = jnp.zeros((HEAD_SIZE, HEAD_SIZE), jnp.float32)
                else:
                    so_far = seed[h]
                states[n, h] = so_far.astype(jnp.bfloat16)
                if make_c or i + 1 < slots:
                    added = dot_tn(sides(h)[1], x_all[rows, lanes(h)])
                    if query and n > 0:
                        added = jnp.where(live, added, 0.0)
                    total[h] = so_far + added
            for h in range(begin, heads):
                l_h, _ = sides(h)
                x_h = x_all[rows, lanes(h)]
                if i == 0 and make_c:
                    out = dot(scores_buf[n, h], x_h)
                else:
                    out = dot(
                        jnp.concatenate([scores_buf[n, h], l_h], axis=1),
                        jnp.concatenate([x_h, states[n, h]], axis=0),
                    )
                chunk[own, lanes(h - begin)] = (scale * out).astype(jnp.bfloat16)

    by_role(query_side, body)


def side(factor, query_side, begin, loaded, c_all=None, seed=None):
    blocks = loaded[1]
    width = loaded[2].shape[1]
    heads = width // HEAD_SIZE
    slots = blocks.shape[2]
    make_c = seed is None
    square = (HEAD_SIZE, HEAD_SIZE)
    total = pltpu.VMEM((heads,) + square, jnp.float32)
    out_shape = [
        pltpu.VMEM((slots * BLOCK_ROWS, (heads - begin) * HEAD_SIZE), jnp.bfloat16),
        pltpu.VMEM((slots, heads) + square, jnp.bfloat16),
    ]
    scratch = [pltpu.VMEM((slots, heads) + square, jnp.bfloat16)]
    if make_c:
        out_shape += [total, pltpu.VMEM((slots * BLOCK_ROWS, width), jnp.bfloat16)]
        extra = ()
    else:
        scratch.append(total)
        extra = (c_all, seed)
    return pl.pallas_call(
        functools.partial(side_kernel, factor, query_side, begin, make_c),
        name="side",
        out_shape=out_shape,
        in_specs=[VMEM, SMEM] + [VMEM] * (4 + len(extra)),
        out_specs=[VMEM] * len(out_shape),
        scratch_shapes=scratch,
        compiler_params=compiler_params(),
        cost_estimate=cost(4 * slots * heads, 0),
    )(*loaded, *extra)


def value_kernel(factor, take_one, blocks, q, k, c_all, one, two, chunk, scores_buf):
    slots = blocks.shape[2]
    heads = q.shape[1] // HEAD_SIZE
    allowed = row_minus_column() <= 0

    def body(pick):
        states = one if pick else two
        for n in range(slots):
            rows = rows_of(blocks[0, 0, n])
            own = rows_of(n)
            scale = jnp.where(live_of(blocks, n), factor, 0.0)
            for h in range(heads):
                scores_buf[n, h] = jnp.where(
                    allowed, dot_nt(k[rows, lanes(h)], q[rows, lanes(h)]), 0.0
                ).astype(jnp.bfloat16)
            for h in range(heads):
                out = dot(scores_buf[n, h], c_all[own, lanes(h)])
                out = out + dot_nt(k[rows, lanes(h)], states[n, h])
                chunk[own, lanes(h)] = (scale * out).astype(jnp.bfloat16)

    by_role(take_one, body)


def value_side(factor, take_one, loaded, c_all, one, two):
    _, blocks, q, k, _, _ = loaded
    slots, heads = one.shape[:2]
    return pl.pallas_call(
        functools.partial(value_kernel, factor, take_one),
        name="value_side",
        out_shape=pltpu.VMEM((slots * BLOCK_ROWS, heads * HEAD_SIZE), jnp.bfloat16),
        in_specs=[SMEM] + [VMEM] * 5,
        out_specs=VMEM,
        scratch_shapes=[pltpu.VMEM(one.shape, jnp.bfloat16)],
        compiler_params=compiler_params(),
        cost_estimate=cost(3 * slots * heads, 0),
    )(blocks, q, k, c_all, one, two)


def router_kernel(factor, take_one, blocks, q, k, v, g, one, two, partial, scores_buf):
    slots = blocks.shape[2]
    heads = q.shape[1] // HEAD_SIZE
    allowed = row_minus_column() >= 0

    def body(pick):
        states = one if pick else two
        for n in range(slots):
            rows = rows_of(blocks[0, 0, n])
            for h in range(heads):
                scores_buf[n, h] = jnp.where(
                    allowed, dot_nt(q[rows, lanes(h)], k[rows, lanes(h)]), 0.0
                ).astype(jnp.bfloat16)
            by_row = jnp.zeros((BLOCK_ROWS, HEAD_SIZE), jnp.float32)
            for h in range(heads):
                core = dot(scores_buf[n, h], v[rows, lanes(h)])
                core = factor * (core + dot_nt(q[rows, lanes(h)], states[n, h]))
                by_row = by_row + g[rows, lanes(h)].astype(jnp.float32) * core
            by_row = jnp.where(live_of(blocks, n), by_row, 0.0)
            partial[0:1, rows_of(n)] = jnp.sum(by_row.T, axis=0, keepdims=True)

    by_role(take_one, body)


def router_side(factor, take_one, loaded, one, two):
    _, blocks, *arrays = loaded
    slots = one.shape[0]
    return pl.pallas_call(
        functools.partial(router_kernel, factor, take_one),
        name="router_side",
        out_shape=jax.ShapeDtypeStruct((1, slots * BLOCK_ROWS), jnp.float32),
        in_specs=[SMEM] + [VMEM] * 6,
        out_specs=VMEM,
        scratch_shapes=[pltpu.VMEM(one.shape, jnp.bfloat16)],
        compiler_params=compiler_params(),
        cost_estimate=cost(3 * slots * one.shape[1], 0),
    )(blocks, *arrays, one, two)


def place_kernel(section_of, begin, *refs):
    chunk, out, sem = refs[-3:]
    width = chunk.shape[1] // HEAD_SIZE
    copy = pltpu.make_async_copy(chunk, out.at[0, section_of(), :, lanes(begin, width)], sem)
    copy.start()
    copy.wait()


def place(whole, chunk, shape, section_of, begin):
    rows, width = chunk.shape
    operands = (chunk,) if whole is None else (whole, chunk)
    return pl.pallas_call(
        functools.partial(place_kernel, section_of, begin),
        name="place",
        out_shape=jax.ShapeDtypeStruct(shape, chunk.dtype),
        in_specs=[HBM] * (len(operands) - 1) + [ANY],
        out_specs=HBM,
        scratch_shapes=[pltpu.SemaphoreType.DMA],
        input_output_aliases={} if whole is None else {0: 0},
        compiler_params=pltpu.CompilerParams(vmem_limit_bytes=2**20),
        cost_estimate=cost(0, 4 * rows * width),
    )(*operands)


def shard_states(queries, keys, values, grad_out, router, blocks, counts):
    heads = queries.shape[2] // HEAD_SIZE
    slots = blocks.shape[2]
    shard_blocks = queries.shape[1] // BLOCK_ROWS
    live = jnp.arange(slots, dtype=jnp.int32) < counts[0, 0]
    taken = (blocks[0, 0, :, None] == jnp.arange(shard_blocks, dtype=jnp.int32)) & live[:, None]
    mask = jnp.repeat(jnp.any(taken, axis=0), BLOCK_ROWS)[:, None]

    def rows(array):
        picked = jnp.where(mask, array[0], jnp.zeros((), array.dtype))
        return picked.reshape(-1, heads, HEAD_SIZE)

    weighted = (router[0][:, None, None] * rows(grad_out).astype(jnp.float32)).astype(jnp.bfloat16)
    key_value = jnp.einsum(
        "the,thd->hed", rows(values), rows(keys), preferred_element_type=jnp.float32
    )
    query_grad = jnp.einsum(
        "the,thd->hed", weighted, rows(queries), preferred_element_type=jnp.float32
    )
    return key_value, query_grad


def gathered_gradient(grad_out, router, blocks, counts):
    slots = blocks.shape[2]
    live = jnp.arange(slots, dtype=jnp.int32) < counts[0, 0]
    grouped = grad_out[0].reshape(-1, BLOCK_ROWS, grad_out.shape[2])[blocks[0, 0]]
    weight = jnp.where(live[:, None], router[0].reshape(-1, BLOCK_ROWS)[blocks[0, 0]], 0.0)
    weighted = weight[:, :, None] * grouped.astype(jnp.float32)
    return weighted.astype(jnp.bfloat16).reshape(slots * BLOCK_ROWS, -1)


def own_side():
    return jnp.where(is_first(), 0, 1)


def other_side():
    return jnp.where(is_first(), 1, 0)


def on_device(queries, keys, values, grad_out, router, blocks, counts):
    slots = blocks.shape[2]
    rows = slots * BLOCK_ROWS
    width = queries.shape[2]
    heads = width // HEAD_SIZE
    seq_count = lax.axis_size("seq")
    factor = 1.0 / math.sqrt(HEAD_SIZE * rows * seq_count)
    arrays = (queries, keys, values, grad_out)
    shape = (1, 3, rows, width)
    if seq_count == 2:
        head_start = max(1, heads // 3)
        small = (in_hbm(router), in_hbm(blocks))
        arrays = tuple(in_hbm(x) for x in arrays)

        def sent(x, axis="pipe", by=-1):
            return from_behind(x, axis, by)

        def kernel(call, *operands):
            return call(factor, *operands)

        chunk_a, *loaded = kernel(opened, is_first, head_start, small, arrays)
        loaded = (loaded[4], loaded[5], *loaded[:4])
        chunk_a = sent(chunk_a)
        chunk_b, own, total, c_all = kernel(side, is_first, head_start, loaded)
        total = sent(total, "seq", 1)
        chunk_b = sent(chunk_b)
        chunk_c, other = kernel(side, is_last, 0, loaded, c_all, total)
        chunk_c = sent(chunk_c)
        chunk_d = kernel(value_side, is_last, loaded, c_all, own, other)
        chunk_d = sent(chunk_d)
        partial = kernel(router_side, is_first, loaded, own, other)
        handed = place(None, chunk_a, shape, own_side, 0)
        handed = place(handed, chunk_b, shape, own_side, head_start)
        handed = place(handed, chunk_c, shape, other_side, 0)
        handed = place(handed, chunk_d, shape, lambda: 2, 0)
    else:
        index = lax.axis_index("seq")
        places = jnp.arange(seq_count)[:, None, None, None]
        key_value, query_grad = shard_states(queries, keys, values, grad_out, router, blocks, counts)
        gathered = lax.all_gather(key_value, "seq")
        earlier = jnp.sum(jnp.where(places < index, gathered, 0.0), axis=0)
        gathered = lax.all_gather(query_grad, "seq")
        later = jnp.sum(jnp.where(places > index, gathered, 0.0), axis=0)
        loaded = (router, blocks) + tuple(x[0] for x in arrays)
        c_all = gathered_gradient(grad_out, router, blocks, counts)
        d_query, before = side(factor, always, 0, loaded, c_all, earlier)
        d_key, after = side(factor, never, 0, loaded, c_all, later)
        d_value = value_side(factor, always, loaded, c_all, after, after)
        partial = router_side(factor, always, loaded, before, before)
        handed = None
        for section, chunk in enumerate((d_query, d_key, d_value)):
            chunk = from_behind(chunk, "pipe", -1)
            handed = place(handed, chunk, shape, functools.partial(int, section), 0)
    router_grad = lax.psum(partial, "tp")
    return (handed, router_grad)


def solution(mesh):
    return jax.shard_map(
        on_device,
        mesh=mesh,
        in_specs=(
            P("pipe", "seq", "tp"),
            P("pipe", "seq", "tp"),
            P("pipe", "seq", "tp"),
            P("pipe", "seq", "tp"),
            P("pipe", "seq"),
            P("pipe", "seq", None),
            P("pipe", "seq"),
        ),
        out_specs=(P("pipe", None, "seq", "tp"), P("pipe", "seq")),
        check_vma=False,
    )
```

time: 112 us -> 66.4 us (0.59)
  local copies, waits for them, and re-layouts: 28.5 us -> 0 us
  matrix products: 25.3 us -> 0 us
  waiting for transfers between devices: 25.4 us -> 36.2 us
  Pallas kernels: 0 us -> 10.2 us
  other arithmetic: 8.97 us -> 0 us
  blocking collectives: 17.7 us -> 12.6 us
  starting transfers between devices: 3.82 us -> 6.49 us
    dot_general x17 -> x0, matrix products: 25.3 us -> none  [the longest x4 7.09 us: select(): jnp.einsum('jb,btf->jtf', picker_half, grouped, preferred_element_type=jn...]
    ppermute x1 -> x5, waiting for transfers between devices: 25.4 us -> 36.2 us  [from_behind(): return lax.ppermute(x, axis, [(i, (i + by) % count) for i in range(count)])]
    pallas_call x0 -> x9, Pallas kernels: none -> 10.2 us  [the longest x4 3.1 us: place(): pl.pallas_call(functools.partial(place_kernel, section_of, begin), name='...]
    another operation x3 -> x0, local copies, waits for them, and re-layouts: 7.38 us -> none  [on_device(): jnp.stack([query_gradient, key_gradient, value_gradient])]
    mul x3 -> x0, local copies, waits for them, and re-layouts: 6.98 us -> none  [the longest x1 2.37 us: on_device(): factor * (jnp.einsum('nhts,nthe->nshe', scores, output_gradient, preferre...]
    another operation x3 -> x0, other arithmetic: 5.59 us -> none  [the longest x1 2.88 us: on_device(): jnp.stack([query_gradient, key_gradient, value_gradient])]
    all_gather x2 -> x0, blocking collectives: 5.1 us -> none  [carried_in(): gathered = lax.all_gather(part, axis)]
    unnamed x20 -> x0, local copies, waits for them, and re-layouts: 4.28 us -> none
  transfers between devices with their start and end apart: 1 -> 5, of which waited for: 1 -> 2; matrix products, arithmetic and copies ran while one was open for 1% -> 0% of each run, Pallas kernels for 0% -> 7%
where the time goes in v2:
time: 66.4 us; the launch traced here: 66.2 us
  waiting for transfers between devices  36.2 us (55%)
  blocking collectives  12.6 us (19%)
  Pallas kernels  10.2 us (15%)
  starting transfers between devices  6.49 us (10%)
  between operations  0.72 us (1%)
    ppermute x5, waiting for transfers between devices, from_behind(): return lax.ppermute(x, axis, [(i, (i + by) % count) for i in range(count)])  36.2 us
    psum x1, blocking collectives, on_device(): router_grad = lax.psum(partial, 'tp')  12.6 us
    ppermute x5, starting transfers between devices, from_behind(): return lax.ppermute(x, axis, [(i, (i + by) % count) for i in range(count)])  6.49 us
    pallas_call x4, Pallas kernels, place(): pl.pallas_call(functools.partial(place_kernel, section_of, begin), name='...  3.1 us
    pallas_call x1, Pallas kernels, opened(): pl.pallas_call(functools.partial(open_kernel, factor, query_side, end), n...  2.58 us
    pallas_call x2, Pallas kernels, side(): pl.pallas_call(functools.partial(side_kernel, factor, query_side, begin,...  2.01 us
  transfers between devices with their start and end apart: 5, of which 2 were waited for; matrix products, arithmetic and copies ran while one was open for 0% of the time, Pallas kernels for 7%

profile of v2, /device:TPU:0, one launch (start us, length us, event | category | flops | bytes accessed | tf_op | source)
XLA Modules:
  0.0 66.2 jit_solution(12515855185746543011)
XLA Ops:
  0.6 2.6 %opened.1 = (bf16[384,256]{1,0:T(8,128)(2,1)S(1)}, bf16[512,768]{1,0:T(8,128)(2,1)S(1)}, bf16[512,768]{1,0:T(8,128)(2,1)S(1)}, bf16[512,768]{1,0:T(8,128)(2,1)S(...) custom-call(f32[1,512]{1,0:T(1,128)} %router.1, s32[1,1,3]{2,1,0:T(1,128)} %blocks.1, ...), custom_call_target="tpu_custom_call" | custom-call | flops 100663296 | bytes 3145728 | tf_op jit(solution)/shard_map/opened/pallas_call | solution.py:188
  3.2 1.0 %side.2 = (bf16[384,512]{1,0:T(8,128)(2,1)S(1)}, bf16[3,6,128,128]{3,2,1,0:T(8,128)(2,1)S(1)}, f32[6,128,128]{2,1,0:T(8,128)S(1)}, bf16[384,768]{1,0:T(8,128)(2,1)S(1)}) custom-call(f32[1,512]{1,0:T(1,128)S(1)} %get-tuple-element.16.refs_0_, s32[1,1,3]{2,1,0:T(1,128)S(4)} %get-tuple-element.17.refs_1_.blocks, ...), custom_call_target="tpu_custom_call" | custom-call | flops 301989888 | tf_op jit(solution)/shard_map/side/pallas_call | solution.py:284
  4.2 0.7 collective-permute-start.2
  4.9 1.3 %collective-permute-done.2.refs_7_ = f32[6,128,128]{2,1,0:T(8,128)S(1)} collective-permute-done((f32[6,128,128]{2,1,0:T(8,128)S(1)}, f32[6,128,128]{2,1,0:T(8,128)S(1)}, u32[]{:S(2)}, u32[]{:S(2)}) %collective-permute-start.2) | collective-permute-done | bytes 393248 | tf_op jit(solution)/shard_map/ppermute | solution.py:25
  6.2 1.0 %side.3 = (bf16[384,768]{1,0:T(8,128)(2,1)S(1)}, bf16[3,6,128,128]{3,2,1,0:T(8,128)(2,1)S(1)}) custom-call(f32[1,512]{1,0:T(1,128)S(1)} %get-tuple-element.16.refs_0_, s32[1,1,3]{2,1,0:T(1,128)S(4)} %get-tuple-element.17.refs_1_.blocks, bf16[512,768]{1,0:T(8,128)(2,1)S(1)} %get-tuple-element.18.refs_2_.q, bf16[512,768]{1,0:T(8,128)(2,1)S(1)} %get-tuple-element.19.refs_3_.k, ...), custom_call_target="tpu_custom_call" | custom-call | flops 301989888 | tf_op jit(solution)/shard_map/side/pallas_call | solution.py:284
  7.3 3.8 %collective-permute-start.3 = (bf16[384,768]{1,0:T(8,128)(2,1)S(1)}, bf16[384,768]{1,0:T(8,128)(2,1)S(1)}, u32[]{:S(2)}, u32[]{:S(2)}) collective-permute-start(bf16[384,768]{1,0:T(8,128)(2,1)S(1)} %get-tuple-element.25), channel_id=1, source_target_pairs={{0,12},{4,0},{8,4},{12,8},{1,13},{5,1},{9,5},{13,9},{2,14},{6,2},{... | collective-permute-start | bytes 1769480 | tf_op jit(solution)/shard_map/ppermute | solution.py:25
  11.0 1.2 %value_side.1 = bf16[384,768]{1,0:T(8,128)(2,1)S(1)} custom-call(s32[1,1,3]{2,1,0:T(1,128)S(4)} %get-tuple-element.17.refs_1_.blocks, bf16[512,768]{1,0:T(8,128)(2,1)S(1)} %get-tuple-element.18.refs_2_.q, bf16[512,768]{1,0:T(8,128)(2,1)S(1)} %get-tuple-element.19.refs_3_.k, bf16[384,768]{1,0:T(8,128)(2,1)S(1)} %get-tuple-element.23.refs_6_.c_all, ...), custom_call_target="tpu_custom_call" | custom-call | flops 226492416 | tf_op jit(solution)/shard_map/value_side/pallas_call | solution.py:322
  12.2 0.6 collective-permute-start.4
  12.8 1.4 %collective-permute-start.1 = (bf16[384,512]{1,0:T(8,128)(2,1)S(1)}, bf16[384,512]{1,0:T(8,128)(2,1)S(1)}, u32[]{:S(2)}, u32[]{:S(2)}) collective-permute-start(bf16[384,512]{1,0:T(8,128)(2,1)S(1)} %get-tuple-element.22), channel_id=1, source_target_pairs={{0,12},{4,0},{8,4},{12,8},{1,13},{5,1},{9,5},{13,9},{2,14},{6,2},{... | collective-permute-start | bytes 1179656 | tf_op jit(solution)/shard_map/ppermute | solution.py:25
  14.2 0.1 collective-permute-start
  14.3 34.9 %collective-permute-done.refs_0_ = bf16[384,256]{1,0:T(8,128)(2,1)S(1)} collective-permute-done((bf16[384,256]{1,0:T(8,128)(2,1)S(1)}, bf16[384,256]{1,0:T(8,128)(2,1)S(1)}, u32[]{:S(2)}, u32[]{:S(2)}) %collective-permute-start) | collective-permute-done | bytes 196640 | tf_op jit(solution)/shard_map/ppermute | solution.py:25
  49.2 0.7 %place.4.refs_0_ = bf16[1,3,384,768]{3,2,1,0:T(8,128)(2,1)} custom-call(bf16[384,256]{1,0:T(8,128)(2,1)S(1)} %collective-permute-done.refs_0_), custom_call_target="tpu_custom_call" | custom-call | bytes 393216 | tf_op jit(solution)/shard_map/place/pallas_call | solution.py:384
  49.9 0.0 collective-permute-done.1.refs_1_
  49.9 0.8 %place.5.refs_0_ = bf16[1,3,384,768]{3,2,1,0:T(8,128)(2,1)} custom-call(bf16[1,3,384,768]{3,2,1,0:T(8,128)(2,1)} %place.4.refs_0_, bf16[384,512]{1,0:T(8,128)(2,1)S(1)} %collective-permute-done.1.refs_1_), custom_call_target="tpu_custom_call", output_to_operand_aliasing={{}: (0, {})} | custom-call | bytes 786432 | tf_op jit(solution)/shard_map/place/pallas_call | solution.py:384
  50.7 1.3 %router_side.1 = f32[1,384]{1,0:T(1,128)S(1)} custom-call(s32[1,1,3]{2,1,0:T(1,128)S(4)} %get-tuple-element.17.refs_1_.blocks, bf16[512,768]{1,0:T(8,128)(2,1)S(1)} %get-tuple-element.18.refs_2_.q, bf16[512,768]{1,0:T(8,128)(2,1)S(1)} %get-tuple-element.19.refs_3_.k, bf16[512,768]{1,0:T(8,128)(2,1)S(1)} %get-tuple-element.20.refs_4_.v, ...), custom_call_target="tpu_custom_call" | custom-call | flops 226492416 | tf_op jit(solution)/shard_map/router_side/pallas_call | solution.py:361
  52.0 12.6 %psum.7 = f32[1,384]{1,0:T(1,128)} all-reduce(f32[1,384]{1,0:T(1,128)S(1)} %router_side.1), channel_id=1, replica_groups=mesh['seq'=2,'pipe'=4,'tp'=4] {'tp'}, use_global_device_ids=true, to_apply=%region_0.0 | all-reduce | flops 384 | bytes 3072 | tf_op jit(solution)/shard_map/psum | solution.py:489
  64.5 0.0 collective-permute-done.3.refs_1_
  64.5 0.8 %place.6.refs_0_ = bf16[1,3,384,768]{3,2,1,0:T(8,128)(2,1)} custom-call(bf16[1,3,384,768]{3,2,1,0:T(8,128)(2,1)} %place.5.refs_0_, bf16[384,768]{1,0:T(8,128)(2,1)S(1)} %collective-permute-done.3.refs_1_), custom_call_target="tpu_custom_call", output_to_operand_aliasing={{}: (0, {})} | custom-call | bytes 1179648 | tf_op jit(solution)/shard_map/place/pallas_call | solution.py:384
  65.4 0.0 collective-permute-done.4.refs_1_
  65.4 0.8 %place.7 = bf16[1,3,384,768]{3,2,1,0:T(8,128)(2,1)} custom-call(bf16[1,3,384,768]{3,2,1,0:T(8,128)(2,1)} %place.6.refs_0_, bf16[384,768]{1,0:T(8,128)(2,1)S(1)} %collective-permute-done.4.refs_1_), custom_call_target="tpu_custom_call", output_to_operand_aliasing={{}: (0, {})} | custom-call | bytes 1179648 | tf_op jit(solution)/shard_map/place/pallas_call | solution.py:384
Async XLA Ops:
  4.2 2.0 %collective-permute-start.2 = (f32[6,128,128]{2,1,0:T(8,128)S(1)}, f32[6,128,128]{2,1,0:T(8,128)S(1)}, u32[]{:S(2)}, u32[]{:S(2)}) collective-permute-start(f32[6,128,128]{2,1,0:T(8,128)S(1)} %get-tuple-element.24), channel_id=1, source_target_pairs={{0,16},{16,0},{1,17},{17,1},{2,18},{18,2},{3,19},{19,3},{4,20},{20... | collective-permute-start | bytes 1179656 | tf_op jit(solution)/shard_map/ppermute | solution.py:25
  7.3 57.3 %collective-permute-start.3 = (bf16[384,768]{1,0:T(8,128)(2,1)S(1)}, bf16[384,768]{1,0:T(8,128)(2,1)S(1)}, u32[]{:S(2)}, u32[]{:S(2)}) collective-permute-start(bf16[384,768]{1,0:T(8,128)(2,1)S(1)} %get-tuple-element.25), channel_id=1, source_target_pairs={{0,12},{4,0},{8,4},{12,8},{1,13},{5,1},{9,5},{13,9},{2,14},{6,2},{... | collective-permute-start | bytes 1769480 | tf_op jit(solution)/shard_map/ppermute | solution.py:25
  12.2 53.2 %collective-permute-start.4 = (bf16[384,768]{1,0:T(8,128)(2,1)S(1)}, bf16[384,768]{1,0:T(8,128)(2,1)S(1)}, u32[]{:S(2)}, u32[]{:S(2)}) collective-permute-start(bf16[384,768]{1,0:T(8,128)(2,1)S(1)} %value_side.1), channel_id=1, source_target_pairs={{0,12},{4,0},{8,4},{12,8},{1,13},{5,1},{9,5},{13,9},{2,14},{6,2},{... | collective-permute-start | bytes 1769480 | tf_op jit(solution)/shard_map/ppermute | solution.py:25
  12.8 37.1 %collective-permute-start.1 = (bf16[384,512]{1,0:T(8,128)(2,1)S(1)}, bf16[384,512]{1,0:T(8,128)(2,1)S(1)}, u32[]{:S(2)}, u32[]{:S(2)}) collective-permute-start(bf16[384,512]{1,0:T(8,128)(2,1)S(1)} %get-tuple-element.22), channel_id=1, source_target_pairs={{0,12},{4,0},{8,4},{12,8},{1,13},{5,1},{9,5},{13,9},{2,14},{6,2},{... | collective-permute-start | bytes 1179656 | tf_op jit(solution)/shard_map/ppermute | solution.py:25
  14.2 34.9 %collective-permute-start = (bf16[384,256]{1,0:T(8,128)(2,1)S(1)}, bf16[384,256]{1,0:T(8,128)(2,1)S(1)}, u32[]{:S(2)}, u32[]{:S(2)}) collective-permute-start(bf16[384,256]{1,0:T(8,128)(2,1)S(1)} %get-tuple-element.15), channel_id=1, source_target_pairs={{0,12},{4,0},{8,4},{12,8},{1,13},{5,1},{9,5},{13,9},{2,14},{6,2},{... | collective-permute-start | bytes 589832 | tf_op jit(solution)/shard_map/ppermute | solution.py:25

commit v3 on v2

--- a/solution.py
+++ b/solution.py
@@ -108,54 +108,52 @@
     return (weight * grad.astype(jnp.float32)).astype(jnp.bfloat16)
 
 
-def open_kernel(
-    factor, query_side, end, router, blocks, q, k, v, g, chunk, q_all, k_all, v_all, g_all,
-    router_all, blocks_all, acc, small_sem, head_sem, rest_sem,
-):
-    slots = blocks.shape[2]
-    heads = q_all.shape[1] // HEAD_SIZE
-    small = [
-        pltpu.make_async_copy(blocks, blocks_all, small_sem.at[0]),
-        pltpu.make_async_copy(router, router_all, small_sem.at[1]),
-    ]
-    pairs = ((g, g_all), (v, v_all), (k, k_all), (q, q_all))
-    first_loads = [
-        pltpu.make_async_copy(
-            source.at[0, :, lanes(0, end)], target.at[:, lanes(0, end)], head_sem.at[j]
-        )
+def head_loads(pairs, begin, count, sem):
+    return [
+        pltpu.make_async_copy(source.at[0, :, lanes(begin, count)], target, sem.at[j])
         for j, (source, target) in enumerate(pairs)
     ]
-    rest_loads = [
-        pltpu.make_async_copy(
-            source.at[0, :, lanes(end, heads - end)],
-            target.at[:, lanes(end, heads - end)],
-            rest_sem.at[j],
-        )
-        for j, (source, target) in enumerate(pairs)
+
+
+def open_kernel(
+    factor, query_side, end, router, blocks, q, k, v, g, chunk,
+    router_buf, blocks_buf, x_buf, v_buf, g_buf, acc, small_sem, load_sem,
+):
+    slots = blocks.shape[2]
+    small = [
+        pltpu.make_async_copy(blocks, blocks_buf, small_sem.at[0]),
+        pltpu.make_async_copy(router, router_buf, small_sem.at[1]),
     ]
-    for load in small + first_loads + rest_loads:
+    for copy in small:
+        copy.start()
+    shared = head_loads(((g, g_buf), (v, v_buf)), 0, end, load_sem)
+    for load in shared:
         load.start()
+
+    def start(query):
+        x = k if query else q
+        pltpu.make_async_copy(x.at[0, :, lanes(0, end)], x_buf, load_sem.at[2]).start()
+
+    by_role(query_side, start)
     difference = row_minus_column()
-    for load in small:
-        load.wait()
-    for load in first_loads:
-        load.wait()
+    for copy in small + shared:
+        copy.wait()
+    pltpu.make_async_copy(k.at[0, :, lanes(0, end)], x_buf, load_sem.at[2]).wait()
 
     def body(query):
         allowed = difference >= 0 if query else difference <= 0
-        x_all = k_all if query else q_all
         order = in_order(query, slots)
         for i, n in enumerate(order):
-            live = live_of(blocks_all, n)
-            block = blocks_all[0, 0, n]
+            live = live_of(blocks_buf, n)
+            block = blocks_buf[0, 0, n]
             rows = rows_of(block)
-            weight = jnp.where(live, down_rows(router_all, block), 0.0)
+            weight = jnp.where(live, down_rows(router_buf, block), 0.0)
             scale = jnp.where(live, factor, 0.0)
             for h in range(end):
-                c_h = weigh(weight, g_all[rows, lanes(h)])
-                v_h = v_all[rows, lanes(h)]
+                c_h = weigh(weight, g_buf[rows, lanes(h)])
+                v_h = v_buf[rows, lanes(h)]
                 l_h, r_h = (c_h, v_h) if query else (v_h, c_h)
-                x_h = x_all[rows, lanes(h)]
+                x_h = x_buf[rows, lanes(h)]
                 scores = jnp.where(allowed, dot_nt(l_h, r_h), 0.0).astype(jnp.bfloat16)
                 if i == 0:
                     out = dot(scores, x_h)
@@ -170,62 +168,78 @@
                     acc[h] = added if i == 0 else acc[h] + added
 
     by_role(query_side, body)
-    for load in rest_loads:
-        load.wait()
 
 
 def opened(factor, query_side, end, small, arrays):
     router, blocks = small
-    _, shard_rows, width = arrays[0].shape
-    slots = blocks.shape[2]
-    whole = pltpu.VMEM((shard_rows, width), jnp.bfloat16)
-    out_shape = [
-        pltpu.VMEM((slots * BLOCK_ROWS, end * HEAD_SIZE), jnp.bfloat16),
-        whole, whole, whole, whole,
-        pltpu.VMEM(router.shape, router.dtype),
-        pltpu.SMEM(blocks.shape, blocks.dtype),
-    ]
+    _, shard_rows, _ = arrays[0].shape
+    slots = blocks.shape[2]
+    part = pltpu.VMEM((shard_rows, end * HEAD_SIZE), jnp.bfloat16)
     return pl.pallas_call(
         functools.partial(open_kernel, factor, query_side, end),
         name="opened",
-        out_shape=out_shape,
+        out_shape=pltpu.VMEM((slots * BLOCK_ROWS, end * HEAD_SIZE), jnp.bfloat16),
         in_specs=[HBM] * 6,
-        out_specs=[VMEM] * 6 + [SMEM],
+        out_specs=VMEM,
         scratch_shapes=[
+            pltpu.VMEM(router.shape, router.dtype),
+            pltpu.SMEM(blocks.shape, blocks.dtype),
+            part, part, part,
             pltpu.VMEM((end, HEAD_SIZE, HEAD_SIZE), jnp.float32),
             pltpu.SemaphoreType.DMA((2,)),
-            pltpu.SemaphoreType.DMA((4,)),
-            pltpu.SemaphoreType.DMA((4,)),
+            pltpu.SemaphoreType.DMA((3,)),
         ],
         compiler_params=compiler_params(),
-        cost_estimate=cost(4 * slots * end, 8 * shard_rows * width),
+        cost_estimate=cost(4 * slots * end, 6 * shard_rows * end * HEAD_SIZE),
     )(router, blocks, *arrays)
 
 
-def side_kernel(factor, query_side, begin, make_c, *refs):
+def side_kernel(factor, query_side, begin, seeded, *refs):
     (router, blocks, q, k, v, g), refs = refs[:6], refs[6:]
-    if make_c:
-        chunk, states, total, c_all, scores_buf = refs
+    if seeded:
+        c_all, seed, chunk, states, scores_buf, total = refs
     else:
-        c_all, seed, chunk, states, scores_buf, total = refs
+        sources = (router, blocks, q, k, v, g)
+        chunk, states, total, c_all, *targets = refs[:10]
+        scores_buf, load_sem = refs[10:]
+        router, blocks, q, k, v, g = targets
     slots = blocks.shape[2]
     heads = states.shape[1]
     difference = row_minus_column()
+
+    if not seeded:
+        loads = [
+            pltpu.make_async_copy(source if j < 2 else source.at[0], target, load_sem.at[j])
+            for j, (source, target) in enumerate(zip(sources, targets))
+        ]
+        for j in (1, 0, 5, 4):
+            loads[j].start()
+
+        def start(query):
+            for j in (3, 2) if query else (2, 3):
+                loads[j].start()
+
+        by_role(query_side, start)
+        for j in (1, 0, 5):
+            loads[j].wait()
 
     def body(query):
         allowed = difference >= 0 if query else difference <= 0
         x_all = k if query else q
         order = in_order(query, slots)
+        if not seeded:
+            for n in order:
+                block = blocks[0, 0, n]
+                weight = jnp.where(live_of(blocks, n), down_rows(router, block), 0.0)
+                for h in range(heads):
+                    c_all[rows_of(n), lanes(h)] = weigh(weight, g[rows_of(block), lanes(h)])
+            for j in (4, 3 if query else 2):
+                loads[j].wait()
         for i, n in enumerate(order):
             live = live_of(blocks, n)
-            block = blocks[0, 0, n]
-            rows = rows_of(block)
+            rows = rows_of(blocks[0, 0, n])
             own = rows_of(n)
             scale = jnp.where(live, factor, 0.0)
-            if make_c:
-                weight = jnp.where(live, down_rows(router, block), 0.0)
-                for h in range(heads):
-                    c_all[own, lanes(h)] = weigh(weight, g[rows, lanes(h)])
 
             def sides(h):
                 c_h, v_h = c_all[own, lanes(h)], v[rows, lanes(h)]
@@ -237,12 +251,12 @@
             for h in range(heads):
                 if i > 0:
                     so_far = total[h]
-                elif make_c:
+                elif seeded:
+                    so_far = seed[h]
+                else:
                     so_far = jnp.zeros((HEAD_SIZE, HEAD_SIZE), jnp.float32)
-                else:
-                    so_far = seed[h]
                 states[n, h] = so_far.astype(jnp.bfloat16)
-                if make_c or i + 1 < slots:
+                if not seeded or i + 1 < slots:
                     added = dot_tn(sides(h)[1], x_all[rows, lanes(h)])
                     if query and n > 0:
                         added = jnp.where(live, added, 0.0)
@@ -250,7 +264,7 @@
             for h in range(begin, heads):
                 l_h, _ = sides(h)
                 x_h = x_all[rows, lanes(h)]
-                if i == 0 and make_c:
+                if i == 0 and not seeded:
                     out = dot(scores_buf[n, h], x_h)
                 else:
                     out = dot(
@@ -258,39 +272,48 @@
                         jnp.concatenate([x_h, states[n, h]], axis=0),
                     )
                 chunk[own, lanes(h - begin)] = (scale * out).astype(jnp.bfloat16)
+        if not seeded:
+            loads[2 if query else 3].wait()
 
     by_role(query_side, body)
 
 
-def side(factor, query_side, begin, loaded, c_all=None, seed=None):
-    blocks = loaded[1]
-    width = loaded[2].shape[1]
+def side(factor, query_side, begin, arrays, c_all=None, seed=None):
+    router, blocks = arrays[:2]
+    shard_rows, width = arrays[2].shape[-2:]
     heads = width // HEAD_SIZE
     slots = blocks.shape[2]
-    make_c = seed is None
     square = (HEAD_SIZE, HEAD_SIZE)
     total = pltpu.VMEM((heads,) + square, jnp.float32)
     out_shape = [
         pltpu.VMEM((slots * BLOCK_ROWS, (heads - begin) * HEAD_SIZE), jnp.bfloat16),
         pltpu.VMEM((slots, heads) + square, jnp.bfloat16),
     ]
+    out_specs = [VMEM] * 2
     scratch = [pltpu.VMEM((slots, heads) + square, jnp.bfloat16)]
-    if make_c:
-        out_shape += [total, pltpu.VMEM((slots * BLOCK_ROWS, width), jnp.bfloat16)]
-        extra = ()
-    else:
+    seeded = seed is not None
+    if seeded:
         scratch.append(total)
         extra = (c_all, seed)
+        in_specs = [VMEM, SMEM] + [VMEM] * 6
+    else:
+        out_shape += [total, pltpu.VMEM((slots * BLOCK_ROWS, width), jnp.bfloat16)]
+        out_shape += [pltpu.VMEM(router.shape, router.dtype), pltpu.SMEM(blocks.shape, blocks.dtype)]
+        out_shape += [pltpu.VMEM((shard_rows, width), jnp.bfloat16)] * 4
+        out_specs += [VMEM] * 3 + [SMEM] + [VMEM] * 4
+        scratch.append(pltpu.SemaphoreType.DMA((6,)))
+        extra = ()
+        in_specs = [HBM] * 6
     return pl.pallas_call(
-        functools.partial(side_kernel, factor, query_side, begin, make_c),
+        functools.partial(side_kernel, factor, query_side, begin, seeded),
         name="side",
         out_shape=out_shape,
-        in_specs=[VMEM, SMEM] + [VMEM] * (4 + len(extra)),
-        out_specs=[VMEM] * len(out_shape),
+        in_specs=in_specs,
+        out_specs=out_specs,
         scratch_shapes=scratch,
         compiler_params=compiler_params(),
-        cost_estimate=cost(4 * slots * heads, 0),
-    )(*loaded, *extra)
+        cost_estimate=cost(4 * slots * heads, 0 if seeded else 8 * shard_rows * width),
+    )(*arrays, *extra)
 
 
 def value_kernel(factor, take_one, blocks, q, k, c_all, one, two, chunk, scores_buf):
@@ -443,7 +466,7 @@
     arrays = (queries, keys, values, grad_out)
     shape = (1, 3, rows, width)
     if seq_count == 2:
-        head_start = max(1, heads // 3)
+        head_start = max(1, heads // 2)
         small = (in_hbm(router), in_hbm(blocks))
         arrays = tuple(in_hbm(x) for x in arrays)
 
@@ -453,10 +476,9 @@
         def kernel(call, *operands):
             return call(factor, *operands)
 
-        chunk_a, *loaded = kernel(opened, is_first, head_start, small, arrays)
-        loaded = (loaded[4], loaded[5], *loaded[:4])
+        chunk_a = kernel(opened, is_first, head_start, small, arrays)
         chunk_a = sent(chunk_a)
-        chunk_b, own, total, c_all = kernel(side, is_first, head_start, loaded)
+        chunk_b, own, total, c_all, *loaded = kernel(side, is_first, head_start, small + arrays)
         total = sent(total, "seq", 1)
         chunk_b = sent(chunk_b)
         chunk_c, other = kernel(side, is_last, 0, loaded, c_all, total)

time: 66.4 us -> 64.6 us (0.973)
  waiting for transfers between devices: 36.2 us -> 33 us
  Pallas kernels: 10.2 us -> 11.6 us
    ppermute x5, waiting for transfers between devices: 36.2 us -> 33 us  [from_behind(): return lax.ppermute(x, axis, [(i, (i + by) % count) for i in range(count)])]
    pallas_call x2, Pallas kernels: 2.01 us -> 3.53 us  [side(): pl.pallas_call(functools.partial(side_kernel, factor, query_side, begin,...]
  transfers between devices with their start and end apart: 5 -> 5, of which waited for: 2 -> 3; matrix products, arithmetic and copies ran while one was open for 0% -> 0% of each run, Pallas kernels for 7% -> 11%
where the time goes in v3:
time: 64.6 us; the launch traced here: 64.4 us
  waiting for transfers between devices  33 us (51%)
  blocking collectives  12.6 us (20%)
  Pallas kernels  11.6 us (18%)
  starting transfers between devices  6.56 us (10%)
  between operations  0.71 us (1%)
    ppermute x5, waiting for transfers between devices, from_behind(): return lax.ppermute(x, axis, [(i, (i + by) % count) for i in range(count)])  33 us
    psum x1, blocking collectives, on_device(): router_grad = lax.psum(partial, 'tp')  12.6 us
    ppermute x5, starting transfers between devices, from_behind(): return lax.ppermute(x, axis, [(i, (i + by) % count) for i in range(count)])  6.56 us
    pallas_call x2, Pallas kernels, side(): pl.pallas_call(functools.partial(side_kernel, factor, query_side, begin,...  3.53 us
    pallas_call x4, Pallas kernels, place(): pl.pallas_call(functools.partial(place_kernel, section_of, begin), name='...  3.09 us
    pallas_call x1, Pallas kernels, opened(): pl.pallas_call(functools.partial(open_kernel, factor, query_side, end), n...  2.46 us
    pallas_call x1, Pallas kernels, router_side(): pl.pallas_call(functools.partial(router_kernel, factor, take_one), name='...  1.3 us
  transfers between devices with their start and end apart: 5, of which 3 were waited for; matrix products, arithmetic and copies ran while one was open for 0% of the time, Pallas kernels for 11%

profile of v3, /device:TPU:0, one launch (start us, length us, event | category | flops | bytes accessed | tf_op | source)
XLA Modules:
  0.0 64.4 jit_solution(12151501875495913393)
XLA Ops:
  0.6 2.5 %side.2 = (bf16[384,384]{1,0:T(8,128)(2,1)S(1)}, bf16[3,6,128,128]{3,2,1,0:T(8,128)(2,1)S(1)}, f32[6,128,128]{2,1,0:T(8,128)S(1)}, bf16[384,768]{1,0:T(8,128)(2,...) custom-call(f32[1,512]{1,0:T(1,128)} %refs_0_.1, ...), custom_call_target="tpu_custom_call" | custom-call | flops 301989888 | bytes 3145728 | tf_op jit(solution)/shard_map/side/pallas_call | solution.py:307
  3.1 0.6 collective-permute-start.2
  3.7 1.3 %collective-permute-done.2.refs_7_ = f32[6,128,128]{2,1,0:T(8,128)S(1)} collective-permute-done((f32[6,128,128]{2,1,0:T(8,128)S(1)}, f32[6,128,128]{2,1,0:T(8,128)S(1)}, u32[]{:S(2)}, u32[]{:S(2)}) %collective-permute-start.2) | collective-permute-done | bytes 393248 | tf_op jit(solution)/shard_map/ppermute | solution.py:25
  5.0 1.0 %side.3 = (bf16[384,768]{1,0:T(8,128)(2,1)S(1)}, bf16[3,6,128,128]{3,2,1,0:T(8,128)(2,1)S(1)}) custom-call(f32[1,512]{1,0:T(1,128)S(1)} %get-tuple-element.15.refs_0_, s32[1,1,3]{2,1,0:T(1,128)S(4)} %get-tuple-element.16.refs_1_.blocks, bf16[512,768]{1,0:T(8,128)(2,1)S(1)} %get-tuple-element.17.refs_2_.q, bf16[512,768]{1,0:T(8,128)(2,1)S(1)} %get-tuple-element.18.refs_3_.k, ...), custom_call_target="tpu_custom_call" | custom-call | flops 301989888 | tf_op jit(solution)/shard_map/side/pallas_call | solution.py:307
  6.1 3.9 %collective-permute-start.3 = (bf16[384,768]{1,0:T(8,128)(2,1)S(1)}, bf16[384,768]{1,0:T(8,128)(2,1)S(1)}, u32[]{:S(2)}, u32[]{:S(2)}) collective-permute-start(bf16[384,768]{1,0:T(8,128)(2,1)S(1)} %get-tuple-element.23), channel_id=1, source_target_pairs={{0,12},{4,0},{8,4},{12,8},{1,13},{5,1},{9,5},{13,9},{2,14},{6,2},{... | collective-permute-start | bytes 1769480 | tf_op jit(solution)/shard_map/ppermute | solution.py:25
  10.0 1.2 %value_side.1 = bf16[384,768]{1,0:T(8,128)(2,1)S(1)} custom-call(s32[1,1,3]{2,1,0:T(1,128)S(4)} %get-tuple-element.16.refs_1_.blocks, bf16[512,768]{1,0:T(8,128)(2,1)S(1)} %get-tuple-element.17.refs_2_.q, bf16[512,768]{1,0:T(8,128)(2,1)S(1)} %get-tuple-element.18.refs_3_.k, bf16[384,768]{1,0:T(8,128)(2,1)S(1)} %get-tuple-element.21.refs_6_.c_all, ...), custom_call_target="tpu_custom_call" | custom-call | flops 226492416 | tf_op jit(solution)/shard_map/value_side/pallas_call | solution.py:345
  11.2 0.6 collective-permute-start.4
  11.7 2.5 %opened.1 = bf16[384,384]{1,0:T(8,128)(2,1)S(1)} custom-call(f32[1,512]{1,0:T(1,128)} %refs_0_.1, s32[1,1,3]{2,1,0:T(1,128)} %refs_1_.1, bf16[1,512,768]{2,1,0:T(8,128)(2,1)} %refs_2_.1, bf16[1,512,768]{2,1,0:T(8,128)(2,1)} %refs_3_.1, bf16[1,512,768]{2,1,0:T(8,128)(2,1)} %refs_4_.1, bf16[1,512,768]{2,1,0:T(8,128)(2,1)} %refs_5_.1), custom_call_target="tpu_custom_call" | custom-call | flops 150994944 | bytes 1179648 | tf_op jit(solution)/shard_map/opened/pallas_call | solution.py:178
  14.2 1.5 %collective-permute-start = (bf16[384,384]{1,0:T(8,128)(2,1)S(1)}, bf16[384,384]{1,0:T(8,128)(2,1)S(1)}, u32[]{:S(2)}, u32[]{:S(2)}) collective-permute-start(bf16[384,384]{1,0:T(8,128)(2,1)S(1)} %opened.1), channel_id=1, source_target_pairs={{0,12},{4,0},{8,4},{12,8},{1,13},{5,1},{9,5},{13,9},{2,14},{6,2},{... | collective-permute-start | bytes 884744 | tf_op jit(solution)/shard_map/ppermute | solution.py:25
  15.7 0.1 collective-permute-start.1
  15.8 26.9 %collective-permute-done.refs_0_ = bf16[384,384]{1,0:T(8,128)(2,1)S(1)} collective-permute-done((bf16[384,384]{1,0:T(8,128)(2,1)S(1)}, bf16[384,384]{1,0:T(8,128)(2,1)S(1)}, u32[]{:S(2)}, u32[]{:S(2)}) %collective-permute-start) | collective-permute-done | bytes 294944 | tf_op jit(solution)/shard_map/ppermute | solution.py:25
  42.6 0.7 %place.4.refs_0_ = bf16[1,3,384,768]{3,2,1,0:T(8,128)(2,1)} custom-call(bf16[384,384]{1,0:T(8,128)(2,1)S(1)} %collective-permute-done.refs_0_), custom_call_target="tpu_custom_call" | custom-call | bytes 589824 | tf_op jit(solution)/shard_map/place/pallas_call | solution.py:407
  43.4 4.8 %collective-permute-done.1.refs_1_ = bf16[384,384]{1,0:T(8,128)(2,1)S(1)} collective-permute-done((bf16[384,384]{1,0:T(8,128)(2,1)S(1)}, bf16[384,384]{1,0:T(8,128)(2,1)S(1)}, u32[]{:S(2)}, u32[]{:S(2)}) %collective-permute-start.1) | collective-permute-done | bytes 294944 | tf_op jit(solution)/shard_map/ppermute | solution.py:25
  48.1 0.7 %place.5.refs_0_ = bf16[1,3,384,768]{3,2,1,0:T(8,128)(2,1)} custom-call(bf16[1,3,384,768]{3,2,1,0:T(8,128)(2,1)} %place.4.refs_0_, bf16[384,384]{1,0:T(8,128)(2,1)S(1)} %collective-permute-done.1.refs_1_), custom_call_target="tpu_custom_call", output_to_operand_aliasing={{}: (0, {})} | custom-call | bytes 589824 | tf_op jit(solution)/shard_map/place/pallas_call | solution.py:407
  48.8 1.3 %router_side.1 = f32[1,384]{1,0:T(1,128)S(1)} custom-call(s32[1,1,3]{2,1,0:T(1,128)S(4)} %get-tuple-element.16.refs_1_.blocks, bf16[512,768]{1,0:T(8,128)(2,1)S(1)} %get-tuple-element.17.refs_2_.q, bf16[512,768]{1,0:T(8,128)(2,1)S(1)} %get-tuple-element.18.refs_3_.k, bf16[512,768]{1,0:T(8,128)(2,1)S(1)} %get-tuple-element.19.refs_4_.v, ...), custom_call_target="tpu_custom_call" | custom-call | flops 226492416 | tf_op jit(solution)/shard_map/router_side/pallas_call | solution.py:384
  50.2 12.6 %psum.7 = f32[1,384]{1,0:T(1,128)} all-reduce(f32[1,384]{1,0:T(1,128)S(1)} %router_side.1), channel_id=1, replica_groups=mesh['seq'=2,'pipe'=4,'tp'=4] {'tp'}, use_global_device_ids=true, to_apply=%region_0.0 | all-reduce | flops 384 | bytes 3072 | tf_op jit(solution)/shard_map/psum | solution.py:511
  62.7 0.0 collective-permute-done.3.refs_1_
  62.7 0.8 %place.6.refs_0_ = bf16[1,3,384,768]{3,2,1,0:T(8,128)(2,1)} custom-call(bf16[1,3,384,768]{3,2,1,0:T(8,128)(2,1)} %place.5.refs_0_, bf16[384,768]{1,0:T(8,128)(2,1)S(1)} %collective-permute-done.3.refs_1_), custom_call_target="tpu_custom_call", output_to_operand_aliasing={{}: (0, {})} | custom-call | bytes 1179648 | tf_op jit(solution)/shard_map/place/pallas_call | solution.py:407
  63.6 0.0 collective-permute-done.4.refs_1_
  63.6 0.8 %place.7 = bf16[1,3,384,768]{3,2,1,0:T(8,128)(2,1)} custom-call(bf16[1,3,384,768]{3,2,1,0:T(8,128)(2,1)} %place.6.refs_0_, bf16[384,768]{1,0:T(8,128)(2,1)S(1)} %collective-permute-done.4.refs_1_), custom_call_target="tpu_custom_call", output_to_operand_aliasing={{}: (0, {})} | custom-call | bytes 1179648 | tf_op jit(solution)/shard_map/place/pallas_call | solution.py:407
Async XLA Ops:
  3.1 1.9 %collective-permute-start.2 = (f32[6,128,128]{2,1,0:T(8,128)S(1)}, f32[6,128,128]{2,1,0:T(8,128)S(1)}, u32[]{:S(2)}, u32[]{:S(2)}) collective-permute-start(f32[6,128,128]{2,1,0:T(8,128)S(1)} %get-tuple-element.22), channel_id=1, source_target_pairs={{0,16},{16,0},{1,17},{17,1},{2,18},{18,2},{3,19},{19,3},{4,20},{20... | collective-permute-start | bytes 1179656 | tf_op jit(solution)/shard_map/ppermute | solution.py:25
  6.1 56.6 %collective-permute-start.3 = (bf16[384,768]{1,0:T(8,128)(2,1)S(1)}, bf16[384,768]{1,0:T(8,128)(2,1)S(1)}, u32[]{:S(2)}, u32[]{:S(2)}) collective-permute-start(bf16[384,768]{1,0:T(8,128)(2,1)S(1)} %get-tuple-element.23), channel_id=1, source_target_pairs={{0,12},{4,0},{8,4},{12,8},{1,13},{5,1},{9,5},{13,9},{2,14},{6,2},{... | collective-permute-start | bytes 1769480 | tf_op jit(solution)/shard_map/ppermute | solution.py:25
  11.2 52.4 %collective-permute-start.4 = (bf16[384,768]{1,0:T(8,128)(2,1)S(1)}, bf16[384,768]{1,0:T(8,128)(2,1)S(1)}, u32[]{:S(2)}, u32[]{:S(2)}) collective-permute-start(bf16[384,768]{1,0:T(8,128)(2,1)S(1)} %value_side.1), channel_id=1, source_target_pairs={{0,12},{4,0},{8,4},{12,8},{1,13},{5,1},{9,5},{13,9},{2,14},{6,2},{... | collective-permute-start | bytes 1769480 | tf_op jit(solution)/shard_map/ppermute | solution.py:25
  14.2 28.4 %collective-permute-start = (bf16[384,384]{1,0:T(8,128)(2,1)S(1)}, bf16[384,384]{1,0:T(8,128)(2,1)S(1)}, u32[]{:S(2)}, u32[]{:S(2)}) collective-permute-start(bf16[384,384]{1,0:T(8,128)(2,1)S(1)} %opened.1), channel_id=1, source_target_pairs={{0,12},{4,0},{8,4},{12,8},{1,13},{5,1},{9,5},{13,9},{2,14},{6,2},{... | collective-permute-start | bytes 884744 | tf_op jit(solution)/shard_map/ppermute | solution.py:25
  15.7 32.4 %collective-permute-start.1 = (bf16[384,384]{1,0:T(8,128)(2,1)S(1)}, bf16[384,384]{1,0:T(8,128)(2,1)S(1)}, u32[]{:S(2)}, u32[]{:S(2)}) collective-permute-start(bf16[384,384]{1,0:T(8,128)(2,1)S(1)} %get-tuple-element.14), channel_id=1, source_target_pairs={{0,12},{4,0},{8,4},{12,8},{1,13},{5,1},{9,5},{13,9},{2,14},{6,2},{... | collective-permute-start | bytes 884744 | tf_op jit(solution)/shard_map/ppermute | solution.py:25

commit v4 on v3

--- a/solution.py
+++ b/solution.py
@@ -1,4 +1,5 @@
 import functools
+import itertools
 import math
 
 import jax
@@ -108,6 +109,13 @@
     return (weight * grad.astype(jnp.float32)).astype(jnp.bfloat16)
 
 
+def put_rows(chunk, tail, n, columns, rows):
+    if tail is not None and n * BLOCK_ROWS == chunk.shape[0]:
+        tail[:, columns] = rows
+    else:
+        chunk[rows_of(n), columns] = rows
+
+
 def head_loads(pairs, begin, count, sem):
     return [
         pltpu.make_async_copy(source.at[0, :, lanes(begin, count)], target, sem.at[j])
@@ -116,8 +124,9 @@
 
 
 def open_kernel(
-    factor, query_side, end, router, blocks, q, k, v, g, chunk,
-    router_buf, blocks_buf, x_buf, v_buf, g_buf, acc, small_sem, load_sem,
+    factor, query_side, end, router, blocks, q, k, v, g, chunk, tail,
+    router_buf, blocks_buf, x_buf, v_buf, g_buf, c_buf, scores_buf, states_buf, acc,
+    small_sem, load_sem,
 ):
     slots = blocks.shape[2]
     small = [
@@ -136,38 +145,59 @@
 
     by_role(query_side, start)
     difference = row_minus_column()
-    for copy in small + shared:
+    for copy in small + shared[:1]:
         copy.wait()
+    for n in range(slots):
+        block = blocks_buf[0, 0, n]
+        weight = jnp.where(live_of(blocks_buf, n), down_rows(router_buf, block), 0.0)
+        for h in range(end):
+            c_buf[rows_of(n), lanes(h)] = weigh(weight, g_buf[rows_of(block), lanes(h)])
+    shared[1].wait()
     pltpu.make_async_copy(k.at[0, :, lanes(0, end)], x_buf, load_sem.at[2]).wait()
 
     def body(query):
         allowed = difference >= 0 if query else difference <= 0
         order = in_order(query, slots)
+
+        def sides(n, h):
+            c_h = c_buf[rows_of(n), lanes(h)]
+            v_h = v_buf[rows_of(blocks_buf[0, 0, n]), lanes(h)]
+            return (c_h, v_h) if query else (v_h, c_h)
+
+        def x_of(n, h):
+            return x_buf[rows_of(blocks_buf[0, 0, n]), lanes(h)]
+
+        for n in order:
+            for h in range(end):
+                l_h, r_h = sides(n, h)
+                scores_buf[n, h] = jnp.where(allowed, dot_nt(l_h, r_h), 0.0).astype(jnp.bfloat16)
+        for i, n in enumerate(order[:-1]):
+            for h in range(end):
+                added = dot_tn(sides(n, h)[1], x_of(n, h))
+                if i > 0:
+                    added = acc[h] + added
+                acc[h] = added
+                states_buf[order[i + 1], h] = added.astype(jnp.bfloat16)
         for i, n in enumerate(order):
-            live = live_of(blocks_buf, n)
-            block = blocks_buf[0, 0, n]
-            rows = rows_of(block)
-            weight = jnp.where(live, down_rows(router_buf, block), 0.0)
-            scale = jnp.where(live, factor, 0.0)
+            scale = jnp.where(live_of(blocks_buf, n), factor, 0.0)
             for h in range(end):
-                c_h = weigh(weight, g_buf[rows, lanes(h)])
-                v_h = v_buf[rows, lanes(h)]
-                l_h, r_h = (c_h, v_h) if query else (v_h, c_h)
-                x_h = x_buf[rows, lanes(h)]
-                scores = jnp.where(allowed, dot_nt(l_h, r_h), 0.0).astype(jnp.bfloat16)
                 if i == 0:
-                    out = dot(scores, x_h)
+                    out = dot(scores_buf[n, h], x_of(n, h))
                 else:
                     out = dot(
-                        jnp.concatenate([scores, l_h], axis=1),
-                        jnp.concatenate([x_h, acc[h].astype(jnp.bfloat16)], axis=0),
+                        jnp.concatenate([scores_buf[n, h], sides(n, h)[0]], axis=1),
+                        jnp.concatenate([x_of(n, h), states_buf[n, h]], axis=0),
                     )
-                chunk[rows_of(n), lanes(h)] = (scale * out).astype(jnp.bfloat16)
-                if i + 1 < slots:
-                    added = dot_tn(r_h, x_h)
-                    acc[h] = added if i == 0 else acc[h] + added
+                put_rows(chunk, tail, n, lanes(h), (scale * out).astype(jnp.bfloat16))
 
     by_role(query_side, body)
+
+
+def split_rows(slots, width):
+    return [
+        pltpu.VMEM(((slots - 1) * BLOCK_ROWS, width), jnp.bfloat16),
+        pltpu.VMEM((BLOCK_ROWS, width), jnp.bfloat16),
+    ]
 
 
 def opened(factor, query_side, end, small, arrays):
@@ -178,13 +208,16 @@
     return pl.pallas_call(
         functools.partial(open_kernel, factor, query_side, end),
         name="opened",
-        out_shape=pltpu.VMEM((slots * BLOCK_ROWS, end * HEAD_SIZE), jnp.bfloat16),
+        out_shape=split_rows(slots, end * HEAD_SIZE),
         in_specs=[HBM] * 6,
-        out_specs=VMEM,
+        out_specs=[VMEM] * 2,
         scratch_shapes=[
             pltpu.VMEM(router.shape, router.dtype),
             pltpu.SMEM(blocks.shape, blocks.dtype),
             part, part, part,
+            pltpu.VMEM((slots * BLOCK_ROWS, end * HEAD_SIZE), jnp.bfloat16),
+            pltpu.VMEM((slots, end, HEAD_SIZE, HEAD_SIZE), jnp.bfloat16),
+            pltpu.VMEM((slots, end, HEAD_SIZE, HEAD_SIZE), jnp.bfloat16),
             pltpu.VMEM((end, HEAD_SIZE, HEAD_SIZE), jnp.float32),
             pltpu.SemaphoreType.DMA((2,)),
             pltpu.SemaphoreType.DMA((3,)),
@@ -194,14 +227,17 @@
     )(router, blocks, *arrays)
 
 
-def side_kernel(factor, query_side, begin, seeded, *refs):
+def side_kernel(factor, query_side, begin, seeded, split, *refs):
     (router, blocks, q, k, v, g), refs = refs[:6], refs[6:]
-    if seeded:
+    tail = None
+    if seeded and split:
+        c_all, seed, chunk, tail, states, info, scores_buf, total = refs
+    elif seeded:
         c_all, seed, chunk, states, scores_buf, total = refs
     else:
         sources = (router, blocks, q, k, v, g)
-        chunk, states, total, c_all, *targets = refs[:10]
-        scores_buf, load_sem = refs[10:]
+        chunk, tail, states, total, c_all, *targets = refs[:11]
+        scores_buf, load_sem = refs[11:]
         router, blocks, q, k, v, g = targets
     slots = blocks.shape[2]
     heads = states.shape[1]
@@ -271,41 +307,52 @@
                         jnp.concatenate([scores_buf[n, h], l_h], axis=1),
                         jnp.concatenate([x_h, states[n, h]], axis=0),
                     )
-                chunk[own, lanes(h - begin)] = (scale * out).astype(jnp.bfloat16)
+                out = (scale * out).astype(jnp.bfloat16)
+                put_rows(chunk, tail, n, lanes(h - begin), out)
+        full = jnp.where(live_of(blocks, slots - 1), 1.0, 0.0)
         if not seeded:
+            total[heads] = jnp.full((HEAD_SIZE, HEAD_SIZE), full, jnp.float32)
             loads[2 if query else 3].wait()
+        elif split:
+            other = seed[heads, 0:8, :]
+            own_full = jnp.full(other.shape, full, jnp.float32)
+            info[...] = jnp.where(own_full + other > 1.5, 2.0, own_full if query else other)
 
     by_role(query_side, body)
 
 
-def side(factor, query_side, begin, arrays, c_all=None, seed=None):
+def side(factor, query_side, begin, split, arrays, c_all=None, seed=None):
     router, blocks = arrays[:2]
     shard_rows, width = arrays[2].shape[-2:]
     heads = width // HEAD_SIZE
     slots = blocks.shape[2]
     square = (HEAD_SIZE, HEAD_SIZE)
-    total = pltpu.VMEM((heads,) + square, jnp.float32)
-    out_shape = [
-        pltpu.VMEM((slots * BLOCK_ROWS, (heads - begin) * HEAD_SIZE), jnp.bfloat16),
-        pltpu.VMEM((slots, heads) + square, jnp.bfloat16),
-    ]
-    out_specs = [VMEM] * 2
+    out_width = (heads - begin) * HEAD_SIZE
+    if split:
+        out_shape = split_rows(slots, out_width)
+    else:
+        out_shape = [pltpu.VMEM((slots * BLOCK_ROWS, out_width), jnp.bfloat16)]
+    out_shape.append(pltpu.VMEM((slots, heads) + square, jnp.bfloat16))
     scratch = [pltpu.VMEM((slots, heads) + square, jnp.bfloat16)]
     seeded = seed is not None
     if seeded:
-        scratch.append(total)
+        if split:
+            out_shape.append(pltpu.VMEM((8, HEAD_SIZE), jnp.float32))
+        out_specs = [VMEM] * len(out_shape)
+        scratch.append(pltpu.VMEM((heads,) + square, jnp.float32))
         extra = (c_all, seed)
         in_specs = [VMEM, SMEM] + [VMEM] * 6
     else:
-        out_shape += [total, pltpu.VMEM((slots * BLOCK_ROWS, width), jnp.bfloat16)]
+        out_shape.append(pltpu.VMEM((heads + 1,) + square, jnp.float32))
+        out_shape.append(pltpu.VMEM((slots * BLOCK_ROWS, width), jnp.bfloat16))
         out_shape += [pltpu.VMEM(router.shape, router.dtype), pltpu.SMEM(blocks.shape, blocks.dtype)]
         out_shape += [pltpu.VMEM((shard_rows, width), jnp.bfloat16)] * 4
-        out_specs += [VMEM] * 3 + [SMEM] + [VMEM] * 4
+        out_specs = [VMEM] * 6 + [SMEM] + [VMEM] * 4
         scratch.append(pltpu.SemaphoreType.DMA((6,)))
         extra = ()
         in_specs = [HBM] * 6
     return pl.pallas_call(
-        functools.partial(side_kernel, factor, query_side, begin, seeded),
+        functools.partial(side_kernel, factor, query_side, begin, seeded, split),
         name="side",
         out_shape=out_shape,
         in_specs=in_specs,
@@ -316,7 +363,13 @@
     )(*arrays, *extra)
 
 
-def value_kernel(factor, take_one, blocks, q, k, c_all, one, two, chunk, scores_buf):
+def value_kernel(factor, take_one, split, blocks, q, k, c_all, one, two, *refs):
+    if split:
+        tail_a, tail_b, tail_c, chunk, tails, scores_buf = refs
+        tail = tails.at[2]
+    else:
+        chunk, scores_buf = refs
+        tail = None
     slots = blocks.shape[2]
     heads = q.shape[1] // HEAD_SIZE
     allowed = row_minus_column() <= 0
@@ -334,24 +387,38 @@
             for h in range(heads):
                 out = dot(scores_buf[n, h], c_all[own, lanes(h)])
                 out = out + dot_nt(k[rows, lanes(h)], states[n, h])
-                chunk[own, lanes(h)] = (scale * out).astype(jnp.bfloat16)
+                put_rows(chunk, tail, n, lanes(h), (scale * out).astype(jnp.bfloat16))
+        if split:
+            begin = tail_a.shape[1] // HEAD_SIZE
+            early, late = (1, 0) if pick else (0, 1)
+            tails[early, :, lanes(0, begin)] = tail_a[...]
+            tails[early, :, lanes(begin, heads - begin)] = tail_b[...]
+            tails[late] = tail_c[...]
 
     by_role(take_one, body)
 
 
-def value_side(factor, take_one, loaded, c_all, one, two):
+def value_side(factor, take_one, loaded, c_all, one, two, tails=()):
     _, blocks, q, k, _, _ = loaded
     slots, heads = one.shape[:2]
+    width = heads * HEAD_SIZE
+    split = len(tails) > 0
+    if split:
+        out_shape = [
+            split_rows(slots, width)[0], pltpu.VMEM((3, BLOCK_ROWS, width), jnp.bfloat16)
+        ]
+    else:
+        out_shape = [pltpu.VMEM((slots * BLOCK_ROWS, width), jnp.bfloat16)]
     return pl.pallas_call(
-        functools.partial(value_kernel, factor, take_one),
+        functools.partial(value_kernel, factor, take_one, split),
         name="value_side",
-        out_shape=pltpu.VMEM((slots * BLOCK_ROWS, heads * HEAD_SIZE), jnp.bfloat16),
-        in_specs=[SMEM] + [VMEM] * 5,
-        out_specs=VMEM,
+        out_shape=out_shape,
+        in_specs=[SMEM] + [VMEM] * (5 + len(tails)),
+        out_specs=[VMEM] * len(out_shape),
         scratch_shapes=[pltpu.VMEM(one.shape, jnp.bfloat16)],
         compiler_params=compiler_params(),
         cost_estimate=cost(3 * slots * heads, 0),
-    )(blocks, q, k, c_all, one, two)
+    )(blocks, q, k, c_all, one, two, *tails)
 
 
 def router_kernel(factor, take_one, blocks, q, k, v, g, one, two, partial, scores_buf):
@@ -395,26 +462,82 @@
 
 def place_kernel(section_of, begin, *refs):
     chunk, out, sem = refs[-3:]
-    width = chunk.shape[1] // HEAD_SIZE
-    copy = pltpu.make_async_copy(chunk, out.at[0, section_of(), :, lanes(begin, width)], sem)
+    rows, width = chunk.shape
+    target = out.at[0, section_of(), pl.ds(0, rows), lanes(begin, width // HEAD_SIZE)]
+    copy = pltpu.make_async_copy(chunk, target, sem)
     copy.start()
     copy.wait()
 
 
-def place(whole, chunk, shape, section_of, begin):
-    rows, width = chunk.shape
+def place_tail_kernel(whole, tails, out, sem):
+    del whole
+    rows = out.shape[2] - tails.shape[1]
+    copy = pltpu.make_async_copy(tails, out.at[0, :, pl.ds(rows, tails.shape[1])], sem)
+    copy.start()
+    copy.wait()
+
+
+def put(body, whole, chunk, shape):
     operands = (chunk,) if whole is None else (whole, chunk)
     return pl.pallas_call(
-        functools.partial(place_kernel, section_of, begin),
+        body,
         name="place",
-        out_shape=jax.ShapeDtypeStruct(shape, chunk.dtype),
+        out_shape=pltpu.HBM(shape, chunk.dtype),
         in_specs=[HBM] * (len(operands) - 1) + [ANY],
         out_specs=HBM,
         scratch_shapes=[pltpu.SemaphoreType.DMA],
         input_output_aliases={} if whole is None else {0: 0},
         compiler_params=pltpu.CompilerParams(vmem_limit_bytes=2**20),
-        cost_estimate=cost(0, 4 * rows * width),
+        cost_estimate=cost(0, 4 * chunk.size),
     )(*operands)
+
+
+def place(whole, chunk, shape, section_of, begin):
+    return put(functools.partial(place_kernel, section_of, begin), whole, chunk, shape)
+
+
+def pick_kernel(*refs):
+    infos, out = refs[:-1], refs[-1]
+    count = len(infos)
+    here = lax.axis_index("pipe")
+    both = jnp.bool_(False)
+    choice = jnp.int32(0)
+    for k, info in enumerate(infos):
+        code = jnp.max(info[...])
+        section = lax.rem(here + k, count)
+        weight = jnp.left_shift(jnp.int32(1), count - 1 - section)
+        both = jnp.logical_or(both, code > 1.5)
+        choice = choice + jnp.where(code > 0.5, weight, 0)
+    out[0, 0] = jnp.where(both, 0, 1 + choice)
+
+
+def pick(infos):
+    return pl.pallas_call(
+        pick_kernel,
+        name="pick",
+        out_shape=pltpu.SMEM((1, 1), jnp.int32),
+        in_specs=[VMEM] * len(infos),
+        out_specs=SMEM,
+        compiler_params=pltpu.CompilerParams(vmem_limit_bytes=2**20),
+    )(*infos)
+
+
+def third_pairs(pipe_count):
+    def pair(s, p):
+        return (s * pipe_count + p, s * pipe_count + (p - 1) % pipe_count)
+
+    every = [pair(s, p) for s in (0, 1) for p in range(pipe_count)]
+    return [every] + [
+        [pair(s, p) for p, s in enumerate(cores)]
+        for cores in itertools.product((0, 1), repeat=pipe_count)
+    ]
+
+
+def folded(parts):
+    while len(parts) > 1:
+        half = len(parts) // 2
+        parts = [parts[k] + parts[k + half] for k in range(half)]
+    return parts[0]
 
 
 def shard_states(queries, keys, values, grad_out, router, blocks, counts):
@@ -448,6 +571,10 @@
     return weighted.astype(jnp.bfloat16).reshape(slots * BLOCK_ROWS, -1)
 
 
+def fits(seq_count, pipe_count, tp_count, slots):
+    return seq_count == 2 and pipe_count <= 4 and tp_count in (1, 2, 4, 8) and slots > 1
+
+
 def own_side():
     return jnp.where(is_first(), 0, 1)
 
@@ -461,12 +588,12 @@
     rows = slots * BLOCK_ROWS
     width = queries.shape[2]
     heads = width // HEAD_SIZE
-    seq_count = lax.axis_size("seq")
+    seq_count, pipe_count, tp_count = (lax.axis_size(axis) for axis in ("seq", "pipe", "tp"))
     factor = 1.0 / math.sqrt(HEAD_SIZE * rows * seq_count)
     arrays = (queries, keys, values, grad_out)
     shape = (1, 3, rows, width)
-    if seq_count == 2:
-        head_start = max(1, heads // 2)
+    if fits(seq_count, pipe_count, tp_count, slots):
+        head_start = max(1, 2 * heads // 3)
         small = (in_hbm(router), in_hbm(blocks))
         arrays = tuple(in_hbm(x) for x in arrays)
 
@@ -476,19 +603,33 @@
         def kernel(call, *operands):
             return call(factor, *operands)
 
-        chunk_a = kernel(opened, is_first, head_start, small, arrays)
+        chunk_a, tail_a = kernel(opened, is_first, head_start, small, arrays)
         chunk_a = sent(chunk_a)
-        chunk_b, own, total, c_all, *loaded = kernel(side, is_first, head_start, small + arrays)
+        chunk_b, tail_b, own, total, c_all, *loaded = kernel(
+            side, is_first, head_start, True, small + arrays
+        )
         total = sent(total, "seq", 1)
         chunk_b = sent(chunk_b)
-        chunk_c, other = kernel(side, is_last, 0, loaded, c_all, total)
+        chunk_c, tail_c, other, info = kernel(side, is_last, 0, True, loaded, c_all, total)
         chunk_c = sent(chunk_c)
-        chunk_d = kernel(value_side, is_last, loaded, c_all, own, other)
+        infos = [info] + [sent(info, "pipe", -k) for k in range(1, pipe_count)]
+        chunk_d, tails = kernel(
+            value_side, is_last, loaded, c_all, own, other, (tail_a, tail_b, tail_c)
+        )
         chunk_d = sent(chunk_d)
         partial = kernel(router_side, is_first, loaded, own, other)
+        parts = [partial] + [sent(partial, "tp", -k) for k in range(1, tp_count)]
+        router_grad = folded(parts)
         handed = place(None, chunk_a, shape, own_side, 0)
         handed = place(handed, chunk_b, shape, own_side, head_start)
         handed = place(handed, chunk_c, shape, other_side, 0)
+        choice = pick(infos)[0, 0]
+
+        def third(pairs, whole, x):
+            return put(place_tail_kernel, whole, lax.ppermute(x, ("seq", "pipe"), pairs), shape)
+
+        branches = [functools.partial(third, pairs) for pairs in third_pairs(pipe_count)]
+        handed = lax.switch(choice, branches, handed, tails)
         handed = place(handed, chunk_d, shape, lambda: 2, 0)
     else:
         index = lax.axis_index("seq")
@@ -500,15 +641,15 @@
         later = jnp.sum(jnp.where(places > index, gathered, 0.0), axis=0)
         loaded = (router, blocks) + tuple(x[0] for x in arrays)
         c_all = gathered_gradient(grad_out, router, blocks, counts)
-        d_query, before = side(factor, always, 0, loaded, c_all, earlier)
-        d_key, after = side(factor, never, 0, loaded, c_all, later)
-        d_value = value_side(factor, always, loaded, c_all, after, after)
+        d_query, before = side(factor, always, 0, False, loaded, c_all, earlier)
+        d_key, after = side(factor, never, 0, False, loaded, c_all, later)
+        (d_value,) = value_side(factor, always, loaded, c_all, after, after)
         partial = router_side(factor, always, loaded, before, before)
         handed = None
         for section, chunk in enumerate((d_query, d_key, d_value)):
             chunk = from_behind(chunk, "pipe", -1)
             handed = place(handed, chunk, shape, functools.partial(int, section), 0)
-    router_grad = lax.psum(partial, "tp")
+        router_grad = lax.psum(partial, "tp")
     return (handed, router_grad)
 
 

time: 64.6 us -> 64.5 us (level)
  starting transfers between devices: 6.56 us -> 21.3 us
  blocking collectives: 12.6 us -> 0 us
  waiting for transfers between devices: 33 us -> 29.6 us
    ppermute x5 -> x11, waiting for transfers between devices: 33 us -> 19.1 us  [from_behind(): return lax.ppermute(x, axis, [(i, (i + by) % count) for i in range(count)])]
    ppermute x5 -> x11, starting transfers between devices: 6.56 us -> 19.2 us  [from_behind(): return lax.ppermute(x, axis, [(i, (i + by) % count) for i in range(count)])]
    psum x1 -> x0, blocking collectives: 12.6 us -> none  [on_device(): router_grad = lax.psum(partial, 'tp')]
    ppermute x0 -> x1, waiting for transfers between devices: none -> 10.5 us  [third(): lax.ppermute(x, ('seq', 'pipe'), pairs)]
    ppermute x0 -> x1, starting transfers between devices: none -> 2.07 us  [third(): lax.ppermute(x, ('seq', 'pipe'), pairs)]
    pallas_call x5 -> x7, Pallas kernels: 4.29 us -> 5.08 us  [the longest x5 3.74 us: put(): pl.pallas_call(body, name='place', out_shape=pltpu.HBM(shape, chunk.dtype...]
  transfers between devices with their start and end apart: 5 -> 12, of which waited for: 3 -> 5; matrix products, arithmetic and copies ran while one was open for 0% -> 1% of each run, Pallas kernels for 11% -> 14%
where the time goes in v4:
time: 64.5 us; the launch traced here: 64.3 us
  waiting for transfers between devices  29.6 us (46%)
  starting transfers between devices  21.3 us (33%)
  Pallas kernels  12 us (19%)
  between operations  0.75 us (1%)
    ppermute x11, starting transfers between devices, from_behind(): return lax.ppermute(x, axis, [(i, (i + by) % count) for i in range(count)])  19.2 us
    ppermute x11, waiting for transfers between devices, from_behind(): return lax.ppermute(x, axis, [(i, (i + by) % count) for i in range(count)])  19.1 us
    ppermute x1, waiting for transfers between devices, third(): lax.ppermute(x, ('seq', 'pipe'), pairs)  10.5 us
    pallas_call x5, Pallas kernels, put(): pl.pallas_call(body, name='place', out_shape=pltpu.HBM(shape, chunk.dtype...  3.74 us
    pallas_call x2, Pallas kernels, side(): pl.pallas_call(functools.partial(side_kernel, factor, query_side, begin,...  3.48 us
    pallas_call x1, Pallas kernels, opened(): pl.pallas_call(functools.partial(open_kernel, factor, query_side, end), n...  2.17 us
    ppermute x1, starting transfers between devices, third(): lax.ppermute(x, ('seq', 'pipe'), pairs)  2.07 us
    pallas_call x1, Pallas kernels, router_side(): pl.pallas_call(functools.partial(router_kernel, factor, take_one), name='...  1.3 us
  transfers between devices with their start and end apart: 12, of which 5 were waited for; matrix products, arithmetic and copies ran while one was open for 1% of the time, Pallas kernels for 14%

profile of v4, /device:TPU:0, one launch (start us, length us, event | category | flops | bytes accessed | tf_op | source)
XLA Modules:
  0.0 64.3 jit_solution(12913467926552556174)
XLA Ops:
  0.6 2.4 %side.2 = (bf16[256,256]{1,0:T(8,128)(2,1)S(1)}, bf16[128,256]{1,0:T(8,128)(2,1)S(1)}, bf16[3,6,128,128]{3,2,1,0:T(8,128)(2,1)S(1)}, f32[7,128,128]{2,1,0:T(8,12...) custom-call(f32[1,512]{1,0:T(1,128)} %router.1, ...), custom_call_target="tpu_custom_call" | custom-call | flops 301989888 | bytes 3145728 | tf_op jit(solution)/shard_map/side/pallas_call | solution.py:354
  3.0 0.6 collective-permute-start.17
  3.6 2.2 %opened.1 = (bf16[256,512]{1,0:T(8,128)(2,1)S(1)}, bf16[128,512]{1,0:T(8,128)(2,1)S(1)}) custom-call(f32[1,512]{1,0:T(1,128)} %router.1, s32[1,1,3]{2,1,0:T(1,128)} %blocks.1, bf16[1,512,768]{2,1,0:T(8,128)(2,1)} %q.1, bf16[1,512,768]{2,1,0:T(8,128)(2,1)} %k.1, bf16[1,512,768]{2,1,0:T(8,128)(2,1)} %v.1, bf16[1,512,768]{2,1,0:T(8,128)(2,1)} %g.1), custom_call_target="tpu_custom_call" | custom-call | flops 201326592 | bytes 1572864 | tf_op jit(solution)/shard_map/opened/pallas_call | solution.py:208
  5.8 3.5 %collective-permute-start.21 = (bf16[256,512]{1,0:T(8,128)(2,1)S(1)}, bf16[256,512]{1,0:T(8,128)(2,1)S(1)}, u32[]{:S(2)}, u32[]{:S(2)}) collective-permute-start(bf16[256,512]{1,0:T(8,128)(2,1)S(1)} %get-tuple-element.156), channel_id=1, source_target_pairs={{0,12},{4,0},{8,4},{12,8},{1,13},{5,1},{9,5},{13,9},{2,14},{6,2},{... | collective-permute-start | bytes 786440 | tf_op jit(solution)/shard_map/ppermute | solution.py:26
  9.3 0.0 collective-permute-done.17.refs_7_
  9.3 1.1 %side.3 = (bf16[256,768]{1,0:T(8,128)(2,1)S(1)}, bf16[128,768]{1,0:T(8,128)(2,1)S(1)}, bf16[3,6,128,128]{3,2,1,0:T(8,128)(2,1)S(1)}, f32[8,128]{1,0:T(8,128)S(1)}) custom-call(f32[1,512]{1,0:T(1,128)S(1)} %get-tuple-element.141.refs_0_, s32[1,1,3]{2,1,0:T(1,128)S(4)} %get-tuple-element.142.refs_1_.blocks, bf16[512,768]{1,0:T(8,128)(2,1)S(1)} %get-tuple-element.143.refs_2_.q, ...), custom_call_target="tpu_custom_call" | custom-call | flops 301989888 | tf_op jit(solution)/shard_map/side/pallas_call | solution.py:354
  10.4 0.6 collective-permute-start.23
  11.0 1.2 %value_side.1 = (bf16[256,768]{1,0:T(8,128)(2,1)S(1)}, bf16[3,128,768]{2,1,0:T(8,128)(2,1)S(1)}) custom-call(s32[1,1,3]{2,1,0:T(1,128)S(4)} %get-tuple-element.142.refs_1_.blocks, bf16[512,768]{1,0:T(8,128)(2,1)S(1)} %get-tuple-element.143.refs_2_.q, bf16[512,768]{1,0:T(8,128)(2,1)S(1)} %get-tuple-element.144.refs_3_.k, ...), custom_call_target="tpu_custom_call" | custom-call | flops 226492416 | tf_op jit(solution)/shard_map/value_side/pallas_call | solution.py:412
  12.2 1.5 %collective-permute-start.24 = (bf16[256,768]{1,0:T(8,128)(2,1)S(1)}, bf16[256,768]{1,0:T(8,128)(2,1)S(1)}, u32[]{:S(2)}, u32[]{:S(2)}) collective-permute-start(bf16[256,768]{1,0:T(8,128)(2,1)S(1)} %get-tuple-element.159), channel_id=1, source_target_pairs={{0,12},{4,0},{8,4},{12,8},{1,13},{5,1},{9,5},{13,9},{2,14},{6,2},{... | collective-permute-start | bytes 1179656 | tf_op jit(solution)/shard_map/ppermute | solution.py:26
  13.7 0.1 collective-permute-start.22
  13.7 1.3 %router_side.1 = f32[1,384]{1,0:T(1,128)S(1)} custom-call(s32[1,1,3]{2,1,0:T(1,128)S(4)} %get-tuple-element.142.refs_1_.blocks, bf16[512,768]{1,0:T(8,128)(2,1)S(1)} %get-tuple-element.143.refs_2_.q, bf16[512,768]{1,0:T(8,128)(2,1)S(1)} %get-tuple-element.144.refs_3_.k, bf16[512,768]{1,0:T(8,128)(2,1)S(1)} %get-tuple-element.145.refs_4_.v, ...), custom_call_target="tpu_custom_call" | custom-call | flops 226492416 | tf_op jit(solution)/shard_map/router_side/pallas_call | solution.py:451
  15.0 3.1 %collective-permute-start.25 = (f32[1,384]{1,0:T(1,128)S(1)}, f32[1,384]{1,0:T(1,128)S(1)}, u32[]{:S(2)}, u32[]{:S(2)}) collective-permute-start(f32[1,384]{1,0:T(1,128)S(1)} %router_side.1), channel_id=1, source_target_pairs={{0,2},{1,3},{2,0},{3,1},{4,6},{5,7},{6,4},{7,5},{8,10},{9,11},{10,... | collective-permute-start | bytes 4616 | tf_op jit(solution)/shard_map/ppermute | solution.py:26
  18.2 17.0 %collective-permute-done.22.refs_1_ = bf16[256,256]{1,0:T(8,128)(2,1)S(1)} collective-permute-done((bf16[256,256]{1,0:T(8,128)(2,1)S(1)}, bf16[256,256]{1,0:T(8,128)(2,1)S(1)}, u32[]{:S(2)}, u32[]{:S(2)}) %collective-permute-start.22) | collective-permute-done | bytes 131104 | tf_op jit(solution)/shard_map/ppermute | solution.py:26
  35.2 3.6 %collective-permute-start.26 = (f32[1,384]{1,0:T(1,128)S(1)}, f32[1,384]{1,0:T(1,128)S(1)}, u32[]{:S(2)}, u32[]{:S(2)}) collective-permute-start(f32[1,384]{1,0:T(1,128)S(1)} %router_side.1), channel_id=1, source_target_pairs={{0,3},{1,0},{2,1},{3,2},{4,7},{5,4},{6,5},{7,6},{8,11},{9,8},{10,9... | collective-permute-start | bytes 4616 | tf_op jit(solution)/shard_map/ppermute | solution.py:26
  38.8 0.0 collective-permute-done.21.refs_0_
  38.8 0.0 collective-permute-start.27
  38.8 0.7 %place.38.refs_0_ = bf16[1,3,384,768]{3,2,1,0:T(8,128)(2,1)} custom-call(bf16[256,512]{1,0:T(8,128)(2,1)S(1)} %collective-permute-done.21.refs_0_), custom_call_target="tpu_custom_call" | custom-call | bytes 524288 | tf_op jit(solution)/shard_map/place/pallas_call | solution.py:482
  39.5 0.7 %place.39.refs_0_ = bf16[1,3,384,768]{3,2,1,0:T(8,128)(2,1)} custom-call(bf16[1,3,384,768]{3,2,1,0:T(8,128)(2,1)} %place.38.refs_0_, bf16[256,256]{1,0:T(8,128)(2,1)S(1)} %collective-permute-done.22.refs_1_), custom_call_target="tpu_custom_call", output_to_operand_aliasing={{}: (0, {})} | custom-call | bytes 262144 | tf_op jit(solution)/shard_map/place/pallas_call | solution.py:482
  40.2 0.0 collective-permute-done.25
  40.2 3.4 %collective-permute-start.18 = (f32[8,128]{1,0:T(8,128)S(1)}, f32[8,128]{1,0:T(8,128)S(1)}, u32[]{:S(2)}, u32[]{:S(2)}) collective-permute-start(f32[8,128]{1,0:T(8,128)S(1)} %get-tuple-element.149.refs_0_), channel_id=1, source_target_pairs={{0,12},{4,0},{8,4},{12,8},{1,13},{5,1},{9,5},{13,9},{2,14},{6,2},{... | collective-permute-start | bytes 12296 | tf_op jit(solution)/shard_map/ppermute | solution.py:26
  43.6 0.0 collective-permute-done.26
  43.6 0.5 collective-permute-start.19
  44.1 0.1 collective-permute-done.27
  44.2 2.4 %collective-permute-start.20 = (f32[8,128]{1,0:T(8,128)S(1)}, f32[8,128]{1,0:T(8,128)S(1)}, u32[]{:S(2)}, u32[]{:S(2)}) collective-permute-start(f32[8,128]{1,0:T(8,128)S(1)} %get-tuple-element.149.refs_0_), channel_id=1, source_target_pairs={{0,4},{4,8},{8,12},{12,0},{1,5},{5,9},{9,13},{13,1},{2,6},{6,10},{... | collective-permute-start | bytes 12296 | tf_op jit(solution)/shard_map/ppermute | solution.py:26
  46.6 0.6 add_add_fusion
  47.1 0.0 collective-permute-done.18.refs_1_
  47.1 0.1 collective-permute-done.19.refs_2_
  47.2 1.9 %collective-permute-done.20.refs_3_ = f32[8,128]{1,0:T(8,128)S(1)} collective-permute-done((f32[8,128]{1,0:T(8,128)S(1)}, f32[8,128]{1,0:T(8,128)S(1)}, u32[]{:S(2)}, u32[]{:S(2)}) %collective-permute-start.20) | collective-permute-done | bytes 4128 | tf_op jit(solution)/shard_map/ppermute | solution.py:26
  49.1 0.1 pick.1
  49.2 0.0 collective-permute-done.23.refs_1_
  49.3 0.8 %place.40 = bf16[1,3,384,768]{3,2,1,0:T(8,128)(2,1)} custom-call(bf16[1,3,384,768]{3,2,1,0:T(8,128)(2,1)} %place.39.refs_0_, bf16[256,768]{1,0:T(8,128)(2,1)S(1)} %collective-permute-done.23.refs_1_), custom_call_target="tpu_custom_call", output_to_operand_aliasing={{}: (0, {})} | custom-call | bytes 786432 | tf_op jit(solution)/shard_map/place/pallas_call | solution.py:482
  50.0 13.5 %conditional.1 = (bf16[1,3,384,768]{3,2,1,0:T(8,128)(2,1)}) conditional(s32[]{:T(128)} %bitcast, (bf16[3,128,768]{2,1,0:T(8,128)(2,1)S(1)}, bf16[1,3,384,768]{3,2,1,0:T(8,128)(2,1)}) %tuple.59, (bf16[3,128,768]{2,1,0:T(8,128)(2,1)S(1)}, bf16[1,3,384,768]{3,2,1,0:T(8,128)(2,1)}) %tuple.59, ...), branch_computations={%region_0.0_spmd, %region_1.0_spmd, %region_2.0_spmd, %region_3.0_... | conditional | bytes 3538992 | solution.py:632
  50.1 2.1 %collective-permute-start = (bf16[3,128,768]{2,1,0:T(8,128)(2,1)S(1)}, bf16[3,128,768]{2,1,0:T(8,128)(2,1)S(1)}, u32[]{:S(2)}, u32[]{:S(2)}) collective-permute-start(bf16[3,128,768]{2,1,0:T(8,128)(2,1)S(1)} %get-tuple-element.72), channel_id=1, source_target_pairs={{0,12},{4,0},{8,4},{12,8},{16,28},{20,16},{24,20},{28,24},{1,13},{... | collective-permute-start | bytes 1769480 | tf_op jit(solution)/shard_map/cond/branch_0_fun/ppermute | solution.py:629
  52.1 10.5 %collective-permute-done.tails = bf16[3,128,768]{2,1,0:T(8,128)(2,1)S(1)} collective-permute-done((bf16[3,128,768]{2,1,0:T(8,128)(2,1)S(1)}, bf16[3,128,768]{2,1,0:T(8,128)(2,1)S(1)}, u32[]{:S(2)}, u32[]{:S(2)}) %collective-permute-start) | collective-permute-done | bytes 589856 | tf_op jit(solution)/shard_map/cond/branch_0_fun/ppermute | solution.py:629
  62.7 0.8 %place.21 = bf16[1,3,384,768]{3,2,1,0:T(8,128)(2,1)} custom-call(bf16[1,3,384,768]{3,2,1,0:T(8,128)(2,1)} %get-tuple-element.68.whole, bf16[3,128,768]{2,1,0:T(8,128)(2,1)S(1)} %collective-permute-done.tails), custom_call_target="tpu_custom_call", output_to_operand_aliasing={{}: (0, {})} | custom-call | bytes 1179648 | tf_op jit(solution)/shard_map/cond/branch_0_fun/place/pallas_call | solution.py:482
  63.6 0.0 collective-permute-done.24.refs_1_
  63.6 0.8 %place.41 = bf16[1,3,384,768]{3,2,1,0:T(8,128)(2,1)} custom-call(bf16[1,3,384,768]{3,2,1,0:T(8,128)(2,1)} %get-tuple-element.160.refs_0_, bf16[256,768]{1,0:T(8,128)(2,1)S(1)} %collective-permute-done.24.refs_1_), custom_call_target="tpu_custom_call", output_to_operand_aliasing={{}: (0, {})} | custom-call | bytes 786432 | tf_op jit(solution)/shard_map/place/pallas_call | solution.py:482
Async XLA Ops:
  3.0 6.2 %collective-permute-start.17 = (f32[7,128,128]{2,1,0:T(8,128)S(1)}, f32[7,128,128]{2,1,0:T(8,128)S(1)}, u32[]{:S(2)}, u32[]{:S(2)}) collective-permute-start(f32[7,128,128]{2,1,0:T(8,128)S(1)} %get-tuple-element.148), channel_id=1, source_target_pairs={{0,16},{16,0},{1,17},{17,1},{2,18},{18,2},{3,19},{19,3},{4,20},{20... | collective-permute-start | bytes 1376264 | tf_op jit(solution)/shard_map/ppermute | solution.py:26
  5.8 33.0 %collective-permute-start.21 = (bf16[256,512]{1,0:T(8,128)(2,1)S(1)}, bf16[256,512]{1,0:T(8,128)(2,1)S(1)}, u32[]{:S(2)}, u32[]{:S(2)}) collective-permute-start(bf16[256,512]{1,0:T(8,128)(2,1)S(1)} %get-tuple-element.156), channel_id=1, source_target_pairs={{0,12},{4,0},{8,4},{12,8},{1,13},{5,1},{9,5},{13,9},{2,14},{6,2},{... | collective-permute-start | bytes 786440 | tf_op jit(solution)/shard_map/ppermute | solution.py:26
  10.4 38.9 %collective-permute-start.23 = (bf16[256,768]{1,0:T(8,128)(2,1)S(1)}, bf16[256,768]{1,0:T(8,128)(2,1)S(1)}, u32[]{:S(2)}, u32[]{:S(2)}) collective-permute-start(bf16[256,768]{1,0:T(8,128)(2,1)S(1)} %get-tuple-element.158), channel_id=1, source_target_pairs={{0,12},{4,0},{8,4},{12,8},{1,13},{5,1},{9,5},{13,9},{2,14},{6,2},{... | collective-permute-start | bytes 1179656 | tf_op jit(solution)/shard_map/ppermute | solution.py:26
  12.2 51.4 %collective-permute-start.24 = (bf16[256,768]{1,0:T(8,128)(2,1)S(1)}, bf16[256,768]{1,0:T(8,128)(2,1)S(1)}, u32[]{:S(2)}, u32[]{:S(2)}) collective-permute-start(bf16[256,768]{1,0:T(8,128)(2,1)S(1)} %get-tuple-element.159), channel_id=1, source_target_pairs={{0,12},{4,0},{8,4},{12,8},{1,13},{5,1},{9,5},{13,9},{2,14},{6,2},{... | collective-permute-start | bytes 1179656 | tf_op jit(solution)/shard_map/ppermute | solution.py:26
  13.7 21.5 %collective-permute-start.22 = (bf16[256,256]{1,0:T(8,128)(2,1)S(1)}, bf16[256,256]{1,0:T(8,128)(2,1)S(1)}, u32[]{:S(2)}, u32[]{:S(2)}) collective-permute-start(bf16[256,256]{1,0:T(8,128)(2,1)S(1)} %get-tuple-element.157), channel_id=1, source_target_pairs={{0,12},{4,0},{8,4},{12,8},{1,13},{5,1},{9,5},{13,9},{2,14},{6,2},{... | collective-permute-start | bytes 393224 | tf_op jit(solution)/shard_map/ppermute | solution.py:26
  15.0 25.2 %collective-permute-start.25 = (f32[1,384]{1,0:T(1,128)S(1)}, f32[1,384]{1,0:T(1,128)S(1)}, u32[]{:S(2)}, u32[]{:S(2)}) collective-permute-start(f32[1,384]{1,0:T(1,128)S(1)} %router_side.1), channel_id=1, source_target_pairs={{0,2},{1,3},{2,0},{3,1},{4,6},{5,7},{6,4},{7,5},{8,10},{9,11},{10,... | collective-permute-start | bytes 4616 | tf_op jit(solution)/shard_map/ppermute | solution.py:26
  35.2 8.5 %collective-permute-start.26 = (f32[1,384]{1,0:T(1,128)S(1)}, f32[1,384]{1,0:T(1,128)S(1)}, u32[]{:S(2)}, u32[]{:S(2)}) collective-permute-start(f32[1,384]{1,0:T(1,128)S(1)} %router_side.1), channel_id=1, source_target_pairs={{0,3},{1,0},{2,1},{3,2},{4,7},{5,4},{6,5},{7,6},{8,11},{9,8},{10,9... | collective-permute-start | bytes 4616 | tf_op jit(solution)/shard_map/ppermute | solution.py:26
  38.8 5.4 %collective-permute-start.27 = (f32[1,384]{1,0:T(1,128)S(1)}, f32[1,384]{1,0:T(1,128)S(1)}, u32[]{:S(2)}, u32[]{:S(2)}) collective-permute-start(f32[1,384]{1,0:T(1,128)S(1)} %router_side.1), channel_id=1, source_target_pairs={{0,1},{1,2},{2,3},{3,0},{4,5},{5,6},{6,7},{7,4},{8,9},{9,10},{10,1... | collective-permute-start | bytes 4616 | tf_op jit(solution)/shard_map/ppermute | solution.py:26
  40.2 6.9 %collective-permute-start.18 = (f32[8,128]{1,0:T(8,128)S(1)}, f32[8,128]{1,0:T(8,128)S(1)}, u32[]{:S(2)}, u32[]{:S(2)}) collective-permute-start(f32[8,128]{1,0:T(8,128)S(1)} %get-tuple-element.149.refs_0_), channel_id=1, source_target_pairs={{0,12},{4,0},{8,4},{12,8},{1,13},{5,1},{9,5},{13,9},{2,14},{6,2},{... | collective-permute-start | bytes 12296 | tf_op jit(solution)/shard_map/ppermute | solution.py:26
  43.6 3.6 %collective-permute-start.19 = (f32[8,128]{1,0:T(8,128)S(1)}, f32[8,128]{1,0:T(8,128)S(1)}, u32[]{:S(2)}, u32[]{:S(2)}) collective-permute-start(f32[8,128]{1,0:T(8,128)S(1)} %get-tuple-element.149.refs_0_), channel_id=1, source_target_pairs={{0,8},{4,12},{8,0},{12,4},{1,9},{5,13},{9,1},{13,5},{2,10},{6,14},... | collective-permute-start | bytes 12296 | tf_op jit(solution)/shard_map/ppermute | solution.py:26
  44.2 4.9 %collective-permute-start.20 = (f32[8,128]{1,0:T(8,128)S(1)}, f32[8,128]{1,0:T(8,128)S(1)}, u32[]{:S(2)}, u32[]{:S(2)}) collective-permute-start(f32[8,128]{1,0:T(8,128)S(1)} %get-tuple-element.149.refs_0_), channel_id=1, source_target_pairs={{0,4},{4,8},{8,12},{12,0},{1,5},{5,9},{9,13},{13,1},{2,6},{6,10},{... | collective-permute-start | bytes 12296 | tf_op jit(solution)/shard_map/ppermute | solution.py:26
  50.1 12.6 %collective-permute-start = (bf16[3,128,768]{2,1,0:T(8,128)(2,1)S(1)}, bf16[3,128,768]{2,1,0:T(8,128)(2,1)S(1)}, u32[]{:S(2)}, u32[]{:S(2)}) collective-permute-start(bf16[3,128,768]{2,1,0:T(8,128)(2,1)S(1)} %get-tuple-element.72), channel_id=1, source_target_pairs={{0,12},{4,0},{8,4},{12,8},{16,28},{20,16},{24,20},{28,24},{1,13},{... | collective-permute-start | bytes 1769480 | tf_op jit(solution)/shard_map/cond/branch_0_fun/ppermute | solution.py:629

commit v5 on v4

--- a/solution.py
+++ b/solution.py
@@ -477,6 +477,32 @@
     copy.wait()
 
 
+def finish_kernel(section, whole, chunk, *refs):
+    del whole
+    parts, (out, total, sem) = refs[:-3], refs[-3:]
+    copy = pltpu.make_async_copy(chunk, out.at[0, section, pl.ds(0, chunk.shape[0])], sem)
+    copy.start()
+    total[...] = folded([part[...] for part in parts])
+    copy.wait()
+
+
+def finish(section, whole, chunk, parts):
+    return pl.pallas_call(
+        functools.partial(finish_kernel, section),
+        name="finish",
+        out_shape=[
+            pltpu.HBM(whole.shape, whole.dtype),
+            jax.ShapeDtypeStruct(parts[0].shape, parts[0].dtype),
+        ],
+        in_specs=[HBM, ANY] + [VMEM] * len(parts),
+        out_specs=[HBM, VMEM],
+        scratch_shapes=[pltpu.SemaphoreType.DMA],
+        input_output_aliases={0: 0},
+        compiler_params=pltpu.CompilerParams(vmem_limit_bytes=2**20),
+        cost_estimate=cost(0, 4 * chunk.size),
+    )(whole, chunk, *parts)
+
+
 def put(body, whole, chunk, shape):
     operands = (chunk,) if whole is None else (whole, chunk)
     return pl.pallas_call(
@@ -619,7 +645,6 @@
         chunk_d = sent(chunk_d)
         partial = kernel(router_side, is_first, loaded, own, other)
         parts = [partial] + [sent(partial, "tp", -k) for k in range(1, tp_count)]
-        router_grad = folded(parts)
         handed = place(None, chunk_a, shape, own_side, 0)
         handed = place(handed, chunk_b, shape, own_side, head_start)
         handed = place(handed, chunk_c, shape, other_side, 0)
@@ -630,7 +655,7 @@
 
         branches = [functools.partial(third, pairs) for pairs in third_pairs(pipe_count)]
         handed = lax.switch(choice, branches, handed, tails)
-        handed = place(handed, chunk_d, shape, lambda: 2, 0)
+        handed, router_grad = finish(2, handed, chunk_d, parts)
     else:
         index = lax.axis_index("seq")
         places = jnp.arange(seq_count)[:, None, None, None]

time: 64.5 us -> 64.4 us (level)
  starting transfers between devices: 21.3 us -> 18.9 us
  waiting for transfers between devices: 29.6 us -> 31.9 us
    ppermute x1, waiting for transfers between devices: 10.5 us -> 12.2 us  [third(): lax.ppermute(x, ('seq', 'pipe'), pairs)]
    ppermute x11, starting transfers between devices: 19.2 us -> 17.7 us  [from_behind(): return lax.ppermute(x, axis, [(i, (i + by) % count) for i in range(count)])]
    pallas_call x0 -> x1, Pallas kernels: none -> 1.32 us  [finish(): pl.pallas_call(functools.partial(finish_kernel, section), name='finish',...]
    ppermute x1, starting transfers between devices: 2.07 us -> 1.27 us  [third(): lax.ppermute(x, ('seq', 'pipe'), pairs)]
    pallas_call x5 -> x4, Pallas kernels: 3.74 us -> 2.98 us  [put(): pl.pallas_call(body, name='place', out_shape=pltpu.HBM(shape, chunk.dtype...]
  transfers between devices with their start and end apart: 12 -> 12, of which waited for: 5 -> 2; matrix products, arithmetic and copies ran while one was open for 1% -> 0% of each run, Pallas kernels for 14% -> 12%
where the time goes in v5:
time: 64.4 us; the launch traced here: 64.2 us
  waiting for transfers between devices  31.9 us (50%)
  starting transfers between devices  18.9 us (29%)
  Pallas kernels  12.6 us (20%)
  between operations  0.78 us (1%)
    ppermute x11, waiting for transfers between devices, from_behind(): return lax.ppermute(x, axis, [(i, (i + by) % count) for i in range(count)])  19.7 us
    ppermute x11, starting transfers between devices, from_behind(): return lax.ppermute(x, axis, [(i, (i + by) % count) for i in range(count)])  17.7 us
    ppermute x1, waiting for transfers between devices, third(): lax.ppermute(x, ('seq', 'pipe'), pairs)  12.2 us
    pallas_call x2, Pallas kernels, side(): pl.pallas_call(functools.partial(side_kernel, factor, query_side, begin,...  3.49 us
    pallas_call x4, Pallas kernels, put(): pl.pallas_call(body, name='place', out_shape=pltpu.HBM(shape, chunk.dtype...  2.98 us
    pallas_call x1, Pallas kernels, opened(): pl.pallas_call(functools.partial(open_kernel, factor, query_side, end), n...  2.17 us
    pallas_call x1, Pallas kernels, finish(): pl.pallas_call(functools.partial(finish_kernel, section), name='finish',...  1.32 us
    pallas_call x1, Pallas kernels, router_side(): pl.pallas_call(functools.partial(router_kernel, factor, take_one), name='...  1.29 us
  transfers between devices with their start and end apart: 12, of which 2 were waited for; matrix products, arithmetic and copies ran while one was open for 0% of the time, Pallas kernels for 12%

profile of v5, /device:TPU:0, one launch (start us, length us, event | category | flops | bytes accessed | tf_op | source)
XLA Modules:
  0.0 64.2 jit_solution(9626295958034876410)
XLA Ops:
  0.6 2.4 %side.2 = (bf16[256,256]{1,0:T(8,128)(2,1)S(1)}, bf16[128,256]{1,0:T(8,128)(2,1)S(1)}, bf16[3,6,128,128]{3,2,1,0:T(8,128)(2,1)S(1)}, f32[7,128,128]{2,1,0:T(8,12...) custom-call(f32[1,512]{1,0:T(1,128)} %router.1, ...), custom_call_target="tpu_custom_call" | custom-call | flops 301989888 | bytes 3145728 | tf_op jit(solution)/shard_map/side/pallas_call | solution.py:354
  3.0 0.6 collective-permute-start.17
  3.6 2.2 %opened.1 = (bf16[256,512]{1,0:T(8,128)(2,1)S(1)}, bf16[128,512]{1,0:T(8,128)(2,1)S(1)}) custom-call(f32[1,512]{1,0:T(1,128)} %router.1, s32[1,1,3]{2,1,0:T(1,128)} %blocks.1, bf16[1,512,768]{2,1,0:T(8,128)(2,1)} %q.1, bf16[1,512,768]{2,1,0:T(8,128)(2,1)} %k.1, bf16[1,512,768]{2,1,0:T(8,128)(2,1)} %v.1, bf16[1,512,768]{2,1,0:T(8,128)(2,1)} %g.1), custom_call_target="tpu_custom_call" | custom-call | flops 201326592 | bytes 1572864 | tf_op jit(solution)/shard_map/opened/pallas_call | solution.py:208
  5.8 0.0 collective-permute-done.17.refs_7_
  5.8 1.1 %side.3 = (bf16[256,768]{1,0:T(8,128)(2,1)S(1)}, bf16[128,768]{1,0:T(8,128)(2,1)S(1)}, bf16[3,6,128,128]{3,2,1,0:T(8,128)(2,1)S(1)}, f32[8,128]{1,0:T(8,128)S(1)}) custom-call(f32[1,512]{1,0:T(1,128)S(1)} %get-tuple-element.141.refs_0_, s32[1,1,3]{2,1,0:T(1,128)S(4)} %get-tuple-element.142.refs_1_.blocks, bf16[512,768]{1,0:T(8,128)(2,1)S(1)} %get-tuple-element.143.refs_2_.q, ...), custom_call_target="tpu_custom_call" | custom-call | flops 301989888 | tf_op jit(solution)/shard_map/side/pallas_call | solution.py:354
  6.9 3.5 %collective-permute-start.23 = (bf16[256,768]{1,0:T(8,128)(2,1)S(1)}, bf16[256,768]{1,0:T(8,128)(2,1)S(1)}, u32[]{:S(2)}, u32[]{:S(2)}) collective-permute-start(bf16[256,768]{1,0:T(8,128)(2,1)S(1)} %get-tuple-element.158), channel_id=1, source_target_pairs={{0,12},{4,0},{8,4},{12,8},{1,13},{5,1},{9,5},{13,9},{2,14},{6,2},{... | collective-permute-start | bytes 1179656 | tf_op jit(solution)/shard_map/ppermute | solution.py:26
  10.4 1.2 %value_side.1 = (bf16[256,768]{1,0:T(8,128)(2,1)S(1)}, bf16[3,128,768]{2,1,0:T(8,128)(2,1)S(1)}) custom-call(s32[1,1,3]{2,1,0:T(1,128)S(4)} %get-tuple-element.142.refs_1_.blocks, bf16[512,768]{1,0:T(8,128)(2,1)S(1)} %get-tuple-element.143.refs_2_.q, bf16[512,768]{1,0:T(8,128)(2,1)S(1)} %get-tuple-element.144.refs_3_.k, ...), custom_call_target="tpu_custom_call" | custom-call | flops 226492416 | tf_op jit(solution)/shard_map/value_side/pallas_call | solution.py:412
  11.6 0.6 collective-permute-start.24
  12.2 1.4 %collective-permute-start.21 = (bf16[256,512]{1,0:T(8,128)(2,1)S(1)}, bf16[256,512]{1,0:T(8,128)(2,1)S(1)}, u32[]{:S(2)}, u32[]{:S(2)}) collective-permute-start(bf16[256,512]{1,0:T(8,128)(2,1)S(1)} %get-tuple-element.156), channel_id=1, source_target_pairs={{0,12},{4,0},{8,4},{12,8},{1,13},{5,1},{9,5},{13,9},{2,14},{6,2},{... | collective-permute-start | bytes 786440 | tf_op jit(solution)/shard_map/ppermute | solution.py:26
  13.6 0.1 collective-permute-start.22
  13.7 2.9 %collective-permute-start.18 = (f32[8,128]{1,0:T(8,128)S(1)}, f32[8,128]{1,0:T(8,128)S(1)}, u32[]{:S(2)}, u32[]{:S(2)}) collective-permute-start(f32[8,128]{1,0:T(8,128)S(1)} %get-tuple-element.149.refs_0_), channel_id=1, source_target_pairs={{0,12},{4,0},{8,4},{12,8},{1,13},{5,1},{9,5},{13,9},{2,14},{6,2},{... | collective-permute-start | bytes 12296 | tf_op jit(solution)/shard_map/ppermute | solution.py:26
  16.6 19.7 %collective-permute-done.22.refs_1_ = bf16[256,256]{1,0:T(8,128)(2,1)S(1)} collective-permute-done((bf16[256,256]{1,0:T(8,128)(2,1)S(1)}, bf16[256,256]{1,0:T(8,128)(2,1)S(1)}, u32[]{:S(2)}, u32[]{:S(2)}) %collective-permute-start.22) | collective-permute-done | bytes 131104 | tf_op jit(solution)/shard_map/ppermute | solution.py:26
  36.3 1.6 %collective-permute-start.19 = (f32[8,128]{1,0:T(8,128)S(1)}, f32[8,128]{1,0:T(8,128)S(1)}, u32[]{:S(2)}, u32[]{:S(2)}) collective-permute-start(f32[8,128]{1,0:T(8,128)S(1)} %get-tuple-element.149.refs_0_), channel_id=1, source_target_pairs={{0,8},{4,12},{8,0},{12,4},{1,9},{5,13},{9,1},{13,5},{2,10},{6,14},... | collective-permute-start | bytes 12296 | tf_op jit(solution)/shard_map/ppermute | solution.py:26
  37.8 0.0 collective-permute-done.21.refs_0_
  37.8 2.4 %collective-permute-start.20 = (f32[8,128]{1,0:T(8,128)S(1)}, f32[8,128]{1,0:T(8,128)S(1)}, u32[]{:S(2)}, u32[]{:S(2)}) collective-permute-start(f32[8,128]{1,0:T(8,128)S(1)} %get-tuple-element.149.refs_0_), channel_id=1, source_target_pairs={{0,4},{4,8},{8,12},{12,0},{1,5},{5,9},{9,13},{13,1},{2,6},{6,10},{... | collective-permute-start | bytes 12296 | tf_op jit(solution)/shard_map/ppermute | solution.py:26
  40.2 1.3 %router_side.1.refs_0_ = f32[1,384]{1,0:T(1,128)S(1)} custom-call(s32[1,1,3]{2,1,0:T(1,128)S(4)} %get-tuple-element.142.refs_1_.blocks, bf16[512,768]{1,0:T(8,128)(2,1)S(1)} %get-tuple-element.143.refs_2_.q, bf16[512,768]{1,0:T(8,128)(2,1)S(1)} %get-tuple-element.144.refs_3_.k, bf16[512,768]{1,0:T(8,128)(2,1)S(1)} %get-tuple-element.145.refs_4_.v, ...), custom_call_target="tpu_custom_call" | custom-call | flops 226492416 | tf_op jit(solution)/shard_map/router_side/pallas_call | solution.py:451
  41.5 0.0 collective-permute-done.18.refs_1_
  41.5 3.7 %collective-permute-start.25 = (f32[1,384]{1,0:T(1,128)S(1)}, f32[1,384]{1,0:T(1,128)S(1)}, u32[]{:S(2)}, u32[]{:S(2)}) collective-permute-start(f32[1,384]{1,0:T(1,128)S(1)} %router_side.1.refs_0_), channel_id=1, source_target_pairs={{0,3},{1,0},{2,1},{3,2},{4,7},{5,4},{6,5},{7,6},{8,11},{9,8},{10,9... | collective-permute-start | bytes 4616 | tf_op jit(solution)/shard_map/ppermute | solution.py:26
  45.2 0.0 collective-permute-done.19.refs_2_
  45.2 0.0 collective-permute-start.26
  45.2 0.0 collective-permute-done.20.refs_3_
  45.2 1.0 %collective-permute-start.27 = (f32[1,384]{1,0:T(1,128)S(1)}, f32[1,384]{1,0:T(1,128)S(1)}, u32[]{:S(2)}, u32[]{:S(2)}) collective-permute-start(f32[1,384]{1,0:T(1,128)S(1)} %router_side.1.refs_0_), channel_id=1, source_target_pairs={{0,1},{1,2},{2,3},{3,0},{4,5},{5,6},{6,7},{7,4},{8,9},{9,10},{10,1... | collective-permute-start | bytes 4616 | tf_op jit(solution)/shard_map/ppermute | solution.py:26
  46.2 0.7 %place.37.refs_0_ = bf16[1,3,384,768]{3,2,1,0:T(8,128)(2,1)} custom-call(bf16[256,512]{1,0:T(8,128)(2,1)S(1)} %collective-permute-done.21.refs_0_), custom_call_target="tpu_custom_call" | custom-call | bytes 524288 | tf_op jit(solution)/shard_map/place/pallas_call | solution.py:508
  46.9 0.7 %place.38.refs_0_ = bf16[1,3,384,768]{3,2,1,0:T(8,128)(2,1)} custom-call(bf16[1,3,384,768]{3,2,1,0:T(8,128)(2,1)} %place.37.refs_0_, bf16[256,256]{1,0:T(8,128)(2,1)S(1)} %collective-permute-done.22.refs_1_), custom_call_target="tpu_custom_call", output_to_operand_aliasing={{}: (0, {})} | custom-call | bytes 262144 | tf_op jit(solution)/shard_map/place/pallas_call | solution.py:508
  47.6 0.1 pick.1
  47.8 0.0 collective-permute-done.23.refs_1_
  47.8 0.8 %place.39 = bf16[1,3,384,768]{3,2,1,0:T(8,128)(2,1)} custom-call(bf16[1,3,384,768]{3,2,1,0:T(8,128)(2,1)} %place.38.refs_0_, bf16[256,768]{1,0:T(8,128)(2,1)S(1)} %collective-permute-done.23.refs_1_), custom_call_target="tpu_custom_call", output_to_operand_aliasing={{}: (0, {})} | custom-call | bytes 786432 | tf_op jit(solution)/shard_map/place/pallas_call | solution.py:508
  48.5 14.3 %conditional.1 = (bf16[1,3,384,768]{3,2,1,0:T(8,128)(2,1)}) conditional(s32[]{:T(128)} %bitcast, (bf16[3,128,768]{2,1,0:T(8,128)(2,1)S(1)}, bf16[1,3,384,768]{3,2,1,0:T(8,128)(2,1)}) %tuple.58, (bf16[3,128,768]{2,1,0:T(8,128)(2,1)S(1)}, bf16[1,3,384,768]{3,2,1,0:T(8,128)(2,1)}) %tuple.58, ...), branch_computations={%region_0.0_spmd, %region_1.0_spmd, %region_2.0_spmd, %region_3.0_... | conditional | bytes 3538992 | solution.py:657
  48.6 1.3 %collective-permute-start = (bf16[3,128,768]{2,1,0:T(8,128)(2,1)S(1)}, bf16[3,128,768]{2,1,0:T(8,128)(2,1)S(1)}, u32[]{:S(2)}, u32[]{:S(2)}) collective-permute-start(bf16[3,128,768]{2,1,0:T(8,128)(2,1)S(1)} %get-tuple-element.72), channel_id=1, source_target_pairs={{0,12},{4,0},{8,4},{12,8},{16,28},{20,16},{24,20},{28,24},{1,13},{... | collective-permute-start | bytes 1769480 | tf_op jit(solution)/shard_map/cond/branch_0_fun/ppermute | solution.py:654
  49.9 12.2 %collective-permute-done.tails = bf16[3,128,768]{2,1,0:T(8,128)(2,1)S(1)} collective-permute-done((bf16[3,128,768]{2,1,0:T(8,128)(2,1)S(1)}, bf16[3,128,768]{2,1,0:T(8,128)(2,1)S(1)}, u32[]{:S(2)}, u32[]{:S(2)}) %collective-permute-start) | collective-permute-done | bytes 589856 | tf_op jit(solution)/shard_map/cond/branch_0_fun/ppermute | solution.py:654
  62.0 0.8 %place.20 = bf16[1,3,384,768]{3,2,1,0:T(8,128)(2,1)} custom-call(bf16[1,3,384,768]{3,2,1,0:T(8,128)(2,1)} %get-tuple-element.68.whole, bf16[3,128,768]{2,1,0:T(8,128)(2,1)S(1)} %collective-permute-done.tails), custom_call_target="tpu_custom_call", output_to_operand_aliasing={{}: (0, {})} | custom-call | bytes 1179648 | tf_op jit(solution)/shard_map/cond/branch_0_fun/place/pallas_call | solution.py:508
  62.9 0.0 collective-permute-done.25.refs_1_
  62.9 0.0 collective-permute-done.26.refs_2_
  62.9 0.0 collective-permute-done.27.refs_3_
  62.9 0.0 collective-permute-done.24.chunk
  62.9 1.3 %finish.1 = (bf16[1,3,384,768]{3,2,1,0:T(8,128)(2,1)}, f32[1,384]{1,0:T(1,128)}) custom-call(bf16[1,3,384,768]{3,2,1,0:T(8,128)(2,1)} %get-tuple-element.160.whole, bf16[256,768]{1,0:T(8,128)(2,1)S(1)} %collective-permute-done.24.chunk, f32[1,384]{1,0:T(1,128)S(1)} %router_side.1.refs_0_, ...), custom_call_target="tpu_custom_call", output_to_operand_aliasing={{0}: (0, {})} | custom-call | bytes 786432 | tf_op jit(solution)/shard_map/finish/pallas_call | solution.py:490
Async XLA Ops:
  3.0 2.7 %collective-permute-start.17 = (f32[7,128,128]{2,1,0:T(8,128)S(1)}, f32[7,128,128]{2,1,0:T(8,128)S(1)}, u32[]{:S(2)}, u32[]{:S(2)}) collective-permute-start(f32[7,128,128]{2,1,0:T(8,128)S(1)} %get-tuple-element.148), channel_id=1, source_target_pairs={{0,16},{16,0},{1,17},{17,1},{2,18},{18,2},{3,19},{19,3},{4,20},{20... | collective-permute-start | bytes 1376264 | tf_op jit(solution)/shard_map/ppermute | solution.py:26
  6.9 40.9 %collective-permute-start.23 = (bf16[256,768]{1,0:T(8,128)(2,1)S(1)}, bf16[256,768]{1,0:T(8,128)(2,1)S(1)}, u32[]{:S(2)}, u32[]{:S(2)}) collective-permute-start(bf16[256,768]{1,0:T(8,128)(2,1)S(1)} %get-tuple-element.158), channel_id=1, source_target_pairs={{0,12},{4,0},{8,4},{12,8},{1,13},{5,1},{9,5},{13,9},{2,14},{6,2},{... | collective-permute-start | bytes 1179656 | tf_op jit(solution)/shard_map/ppermute | solution.py:26
  11.6 51.3 %collective-permute-start.24 = (bf16[256,768]{1,0:T(8,128)(2,1)S(1)}, bf16[256,768]{1,0:T(8,128)(2,1)S(1)}, u32[]{:S(2)}, u32[]{:S(2)}) collective-permute-start(bf16[256,768]{1,0:T(8,128)(2,1)S(1)} %get-tuple-element.159), channel_id=1, source_target_pairs={{0,12},{4,0},{8,4},{12,8},{1,13},{5,1},{9,5},{13,9},{2,14},{6,2},{... | collective-permute-start | bytes 1179656 | tf_op jit(solution)/shard_map/ppermute | solution.py:26
  12.2 25.7 %collective-permute-start.21 = (bf16[256,512]{1,0:T(8,128)(2,1)S(1)}, bf16[256,512]{1,0:T(8,128)(2,1)S(1)}, u32[]{:S(2)}, u32[]{:S(2)}) collective-permute-start(bf16[256,512]{1,0:T(8,128)(2,1)S(1)} %get-tuple-element.156), channel_id=1, source_target_pairs={{0,12},{4,0},{8,4},{12,8},{1,13},{5,1},{9,5},{13,9},{2,14},{6,2},{... | collective-permute-start | bytes 786440 | tf_op jit(solution)/shard_map/ppermute | solution.py:26
  13.6 22.6 %collective-permute-start.22 = (bf16[256,256]{1,0:T(8,128)(2,1)S(1)}, bf16[256,256]{1,0:T(8,128)(2,1)S(1)}, u32[]{:S(2)}, u32[]{:S(2)}) collective-permute-start(bf16[256,256]{1,0:T(8,128)(2,1)S(1)} %get-tuple-element.157), channel_id=1, source_target_pairs={{0,12},{4,0},{8,4},{12,8},{1,13},{5,1},{9,5},{13,9},{2,14},{6,2},{... | collective-permute-start | bytes 393224 | tf_op jit(solution)/shard_map/ppermute | solution.py:26
  13.7 27.8 %collective-permute-start.18 = (f32[8,128]{1,0:T(8,128)S(1)}, f32[8,128]{1,0:T(8,128)S(1)}, u32[]{:S(2)}, u32[]{:S(2)}) collective-permute-start(f32[8,128]{1,0:T(8,128)S(1)} %get-tuple-element.149.refs_0_), channel_id=1, source_target_pairs={{0,12},{4,0},{8,4},{12,8},{1,13},{5,1},{9,5},{13,9},{2,14},{6,2},{... | collective-permute-start | bytes 12296 | tf_op jit(solution)/shard_map/ppermute | solution.py:26
  36.3 8.9 %collective-permute-start.19 = (f32[8,128]{1,0:T(8,128)S(1)}, f32[8,128]{1,0:T(8,128)S(1)}, u32[]{:S(2)}, u32[]{:S(2)}) collective-permute-start(f32[8,128]{1,0:T(8,128)S(1)} %get-tuple-element.149.refs_0_), channel_id=1, source_target_pairs={{0,8},{4,12},{8,0},{12,4},{1,9},{5,13},{9,1},{13,5},{2,10},{6,14},... | collective-permute-start | bytes 12296 | tf_op jit(solution)/shard_map/ppermute | solution.py:26
  37.8 7.4 %collective-permute-start.20 = (f32[8,128]{1,0:T(8,128)S(1)}, f32[8,128]{1,0:T(8,128)S(1)}, u32[]{:S(2)}, u32[]{:S(2)}) collective-permute-start(f32[8,128]{1,0:T(8,128)S(1)} %get-tuple-element.149.refs_0_), channel_id=1, source_target_pairs={{0,4},{4,8},{8,12},{12,0},{1,5},{5,9},{9,13},{13,1},{2,6},{6,10},{... | collective-permute-start | bytes 12296 | tf_op jit(solution)/shard_map/ppermute | solution.py:26
  41.5 21.4 %collective-permute-start.25 = (f32[1,384]{1,0:T(1,128)S(1)}, f32[1,384]{1,0:T(1,128)S(1)}, u32[]{:S(2)}, u32[]{:S(2)}) collective-permute-start(f32[1,384]{1,0:T(1,128)S(1)} %router_side.1.refs_0_), channel_id=1, source_target_pairs={{0,3},{1,0},{2,1},{3,2},{4,7},{5,4},{6,5},{7,6},{8,11},{9,8},{10,9... | collective-permute-start | bytes 4616 | tf_op jit(solution)/shard_map/ppermute | solution.py:26
  45.2 17.7 %collective-permute-start.26 = (f32[1,384]{1,0:T(1,128)S(1)}, f32[1,384]{1,0:T(1,128)S(1)}, u32[]{:S(2)}, u32[]{:S(2)}) collective-permute-start(f32[1,384]{1,0:T(1,128)S(1)} %router_side.1.refs_0_), channel_id=1, source_target_pairs={{0,2},{1,3},{2,0},{3,1},{4,6},{5,7},{6,4},{7,5},{8,10},{9,11},{10,... | collective-permute-start | bytes 4616 | tf_op jit(solution)/shard_map/ppermute | solution.py:26
  45.2 17.7 %collective-permute-start.27 = (f32[1,384]{1,0:T(1,128)S(1)}, f32[1,384]{1,0:T(1,128)S(1)}, u32[]{:S(2)}, u32[]{:S(2)}) collective-permute-start(f32[1,384]{1,0:T(1,128)S(1)} %router_side.1.refs_0_), channel_id=1, source_target_pairs={{0,1},{1,2},{2,3},{3,0},{4,5},{5,6},{6,7},{7,4},{8,9},{9,10},{10,1... | collective-permute-start | bytes 4616 | tf_op jit(solution)/shard_map/ppermute | solution.py:26
  48.6 13.4 %collective-permute-start = (bf16[3,128,768]{2,1,0:T(8,128)(2,1)S(1)}, bf16[3,128,768]{2,1,0:T(8,128)(2,1)S(1)}, u32[]{:S(2)}, u32[]{:S(2)}) collective-permute-start(bf16[3,128,768]{2,1,0:T(8,128)(2,1)S(1)} %get-tuple-element.72), channel_id=1, source_target_pairs={{0,12},{4,0},{8,4},{12,8},{16,28},{20,16},{24,20},{28,24},{1,13},{... | collective-permute-start | bytes 1769480 | tf_op jit(solution)/shard_map/cond/branch_0_fun/ppermute | solution.py:654

commit v6 on v4

--- a/solution.py
+++ b/solution.py
@@ -469,18 +469,65 @@
     copy.wait()
 
 
-def place_tail_kernel(whole, tails, out, sem):
+def keep_kernel(old, new, out):
+    del old
+    out[...] = new[...]
+
+
+def third(pairs, tails):
+    received = lax.ppermute(tails, ("seq", "pipe"), pairs)
+    return pl.pallas_call(
+        keep_kernel,
+        name="keep",
+        out_shape=pltpu.VMEM(tails.shape, tails.dtype),
+        in_specs=[VMEM] * 2,
+        out_specs=VMEM,
+        input_output_aliases={0: 0},
+        compiler_params=pltpu.CompilerParams(vmem_limit_bytes=2**20),
+    )(tails, received)
+
+
+def finish_kernel(section, whole, chunk, tails, *refs):
     del whole
-    rows = out.shape[2] - tails.shape[1]
-    copy = pltpu.make_async_copy(tails, out.at[0, :, pl.ds(rows, tails.shape[1])], sem)
-    copy.start()
-    copy.wait()
-
-
-def put(body, whole, chunk, shape):
+    parts, (out, total, total_buf, sem) = refs[:-4], refs[-4:]
+    rows = chunk.shape[0]
+    copies = [
+        pltpu.make_async_copy(tails, out.at[0, :, pl.ds(rows, tails.shape[1])], sem.at[0]),
+        pltpu.make_async_copy(chunk, out.at[0, section, pl.ds(0, rows)], sem.at[1]),
+        pltpu.make_async_copy(total_buf, total, sem.at[2]),
+    ]
+    copies[0].start()
+    copies[1].start()
+    total_buf[...] = folded([part[...] for part in parts])
+    copies[2].start()
+    for copy in copies:
+        copy.wait()
+
+
+def finish(section, whole, chunk, tails, parts):
+    return pl.pallas_call(
+        functools.partial(finish_kernel, section),
+        name="finish",
+        out_shape=[
+            pltpu.HBM(whole.shape, whole.dtype),
+            pltpu.HBM(parts[0].shape, parts[0].dtype),
+        ],
+        in_specs=[HBM, ANY, ANY] + [VMEM] * len(parts),
+        out_specs=[HBM, HBM],
+        scratch_shapes=[
+            pltpu.VMEM(parts[0].shape, parts[0].dtype),
+            pltpu.SemaphoreType.DMA((3,)),
+        ],
+        input_output_aliases={0: 0},
+        compiler_params=pltpu.CompilerParams(vmem_limit_bytes=2**20),
+        cost_estimate=cost(0, 4 * (chunk.size + tails.size)),
+    )(whole, chunk, tails, *parts)
+
+
+def place(whole, chunk, shape, section_of, begin):
     operands = (chunk,) if whole is None else (whole, chunk)
     return pl.pallas_call(
-        body,
+        functools.partial(place_kernel, section_of, begin),
         name="place",
         out_shape=pltpu.HBM(shape, chunk.dtype),
         in_specs=[HBM] * (len(operands) - 1) + [ANY],
@@ -490,10 +537,6 @@
         compiler_params=pltpu.CompilerParams(vmem_limit_bytes=2**20),
         cost_estimate=cost(0, 4 * chunk.size),
     )(*operands)
-
-
-def place(whole, chunk, shape, section_of, begin):
-    return put(functools.partial(place_kernel, section_of, begin), whole, chunk, shape)
 
 
 def pick_kernel(*refs):
@@ -619,18 +662,15 @@
         chunk_d = sent(chunk_d)
         partial = kernel(router_side, is_first, loaded, own, other)
         parts = [partial] + [sent(partial, "tp", -k) for k in range(1, tp_count)]
-        router_grad = folded(parts)
         handed = place(None, chunk_a, shape, own_side, 0)
         handed = place(handed, chunk_b, shape, own_side, head_start)
         handed = place(handed, chunk_c, shape, other_side, 0)
         choice = pick(infos)[0, 0]
 
-        def third(pairs, whole, x):
-            return put(place_tail_kernel, whole, lax.ppermute(x, ("seq", "pipe"), pairs), shape)
-
         branches = [functools.partial(third, pairs) for pairs in third_pairs(pipe_count)]
-        handed = lax.switch(choice, branches, handed, tails)
-        handed = place(handed, chunk_d, shape, lambda: 2, 0)
+        handed, tails = lax.optimization_barrier((handed, tails))
+        tails = lax.switch(choice, branches, tails)
+        handed, router_grad = finish(2, handed, chunk_d, tails, parts)
     else:
         index = lax.axis_index("seq")
         places = jnp.arange(seq_count)[:, None, None, None]

time: 64.5 us -> 63.3 us (0.981)
  starting transfers between devices: 21.3 us -> 18.9 us
  waiting for transfers between devices: 29.6 us -> 31.9 us
    ppermute x1, waiting for transfers between devices: 10.5 us -> 12.2 us  [third(): received = lax.ppermute(tails, ('seq', 'pipe'), pairs)]
    ppermute x11, starting transfers between devices: 19.2 us -> 17.7 us  [from_behind(): return lax.ppermute(x, axis, [(i, (i + by) % count) for i in range(count)])]
    ppermute x1, starting transfers between devices: 2.07 us -> 1.27 us  [third(): received = lax.ppermute(tails, ('seq', 'pipe'), pairs)]
    ppermute x11, waiting for transfers between devices: 19.1 us -> 19.7 us  [from_behind(): return lax.ppermute(x, axis, [(i, (i + by) % count) for i in range(count)])]
  transfers between devices with their start and end apart: 12 -> 12, of which waited for: 5 -> 2; matrix products, arithmetic and copies ran while one was open for 1% -> 0% of each run, Pallas kernels for 14% -> 11%
where the time goes in v6:
time: 63.3 us; the launch traced here: 63.2 us
  waiting for transfers between devices  31.9 us (50%)
  starting transfers between devices  18.9 us (30%)
  Pallas kernels  11.5 us (18%)
  between operations  0.78 us (1%)
    ppermute x11, waiting for transfers between devices, from_behind(): return lax.ppermute(x, axis, [(i, (i + by) % count) for i in range(count)])  19.7 us
    ppermute x11, starting transfers between devices, from_behind(): return lax.ppermute(x, axis, [(i, (i + by) % count) for i in range(count)])  17.7 us
    ppermute x1, waiting for transfers between devices, third(): received = lax.ppermute(tails, ('seq', 'pipe'), pairs)  12.2 us
    pallas_call x2, Pallas kernels, side(): pl.pallas_call(functools.partial(side_kernel, factor, query_side, begin,...  3.5 us
    pallas_call x1, Pallas kernels, opened(): pl.pallas_call(functools.partial(open_kernel, factor, query_side, end), n...  2.16 us
    pallas_call x3, Pallas kernels, place(): pl.pallas_call(functools.partial(place_kernel, section_of, begin), name='...  2.16 us
    pallas_call x1, Pallas kernels, router_side(): pl.pallas_call(functools.partial(router_kernel, factor, take_one), name='...  1.3 us
    ppermute x1, starting transfers between devices, third(): received = lax.ppermute(tails, ('seq', 'pipe'), pairs)  1.27 us
  transfers between devices with their start and end apart: 12, of which 2 were waited for; matrix products, arithmetic and copies ran while one was open for 0% of the time, Pallas kernels for 11%

profile of v6, /device:TPU:0, one launch (start us, length us, event | category | flops | bytes accessed | tf_op | source)
XLA Modules:
  0.0 63.2 jit_solution(10942703819380039125)
XLA Ops:
  0.6 2.4 %side.2 = (bf16[256,256]{1,0:T(8,128)(2,1)S(1)}, bf16[128,256]{1,0:T(8,128)(2,1)S(1)}, bf16[3,6,128,128]{3,2,1,0:T(8,128)(2,1)S(1)}, f32[7,128,128]{2,1,0:T(8,12...) custom-call(f32[1,512]{1,0:T(1,128)} %refs_0_.1, ...), custom_call_target="tpu_custom_call" | custom-call | flops 301989888 | bytes 3145728 | tf_op jit(solution)/shard_map/side/pallas_call | solution.py:354
  3.0 0.5 collective-permute-start.19
  3.6 2.2 %opened.1 = (bf16[256,512]{1,0:T(8,128)(2,1)S(1)}, bf16[128,512]{1,0:T(8,128)(2,1)S(1)}) custom-call(f32[1,512]{1,0:T(1,128)} %refs_0_.1, s32[1,1,3]{2,1,0:T(1,128)} %refs_1_.1, bf16[1,512,768]{2,1,0:T(8,128)(2,1)} %refs_2_.1, bf16[1,512,768]{2,1,0:T(8,128)(2,1)} %refs_3_.1, bf16[1,512,768]{2,1,0:T(8,128)(2,1)} %refs_4_.1, bf16[1,512,768]{2,1,0:T(8,128)(2,1)} %refs_5_.1), custom_call_target="tpu_custom_call" | custom-call | flops 201326592 | bytes 1572864 | tf_op jit(solution)/shard_map/opened/pallas_call | solution.py:208
  5.8 0.0 collective-permute-done.19.refs_7_
  5.8 1.1 %side.3 = (bf16[256,768]{1,0:T(8,128)(2,1)S(1)}, bf16[128,768]{1,0:T(8,128)(2,1)S(1)}, bf16[3,6,128,128]{3,2,1,0:T(8,128)(2,1)S(1)}, f32[8,128]{1,0:T(8,128)S(1)}) custom-call(f32[1,512]{1,0:T(1,128)S(1)} %get-tuple-element.60.refs_0_, s32[1,1,3]{2,1,0:T(1,128)S(4)} %get-tuple-element.61.refs_1_.blocks, bf16[512,768]{1,0:T(8,128)(2,1)S(1)} %get-tuple-element.62.refs_2_.q, ...), custom_call_target="tpu_custom_call" | custom-call | flops 301989888 | tf_op jit(solution)/shard_map/side/pallas_call | solution.py:354
  6.9 3.5 %collective-permute-start.20 = (bf16[256,768]{1,0:T(8,128)(2,1)S(1)}, bf16[256,768]{1,0:T(8,128)(2,1)S(1)}, u32[]{:S(2)}, u32[]{:S(2)}) collective-permute-start(bf16[256,768]{1,0:T(8,128)(2,1)S(1)} %get-tuple-element.68), channel_id=1, source_target_pairs={{0,12},{4,0},{8,4},{12,8},{1,13},{5,1},{9,5},{13,9},{2,14},{6,2},{... | collective-permute-start | bytes 1179656 | tf_op jit(solution)/shard_map/ppermute | solution.py:26
  10.4 1.2 %value_side.1 = (bf16[256,768]{1,0:T(8,128)(2,1)S(1)}, bf16[3,128,768]{2,1,0:T(8,128)(2,1)S(1)}) custom-call(s32[1,1,3]{2,1,0:T(1,128)S(4)} %get-tuple-element.61.refs_1_.blocks, bf16[512,768]{1,0:T(8,128)(2,1)S(1)} %get-tuple-element.62.refs_2_.q, bf16[512,768]{1,0:T(8,128)(2,1)S(1)} %get-tuple-element.63.refs_3_.k, ...), custom_call_target="tpu_custom_call" | custom-call | flops 226492416 | tf_op jit(solution)/shard_map/value_side/pallas_call | solution.py:412
  11.6 0.6 collective-permute-start.21
  12.2 1.4 %collective-permute-start.17 = (bf16[256,512]{1,0:T(8,128)(2,1)S(1)}, bf16[256,512]{1,0:T(8,128)(2,1)S(1)}, u32[]{:S(2)}, u32[]{:S(2)}) collective-permute-start(bf16[256,512]{1,0:T(8,128)(2,1)S(1)} %get-tuple-element.58), channel_id=1, source_target_pairs={{0,12},{4,0},{8,4},{12,8},{1,13},{5,1},{9,5},{13,9},{2,14},{6,2},{... | collective-permute-start | bytes 786440 | tf_op jit(solution)/shard_map/ppermute | solution.py:26
  13.6 0.1 collective-permute-start.18
  13.7 2.9 %collective-permute-start.22 = (f32[8,128]{1,0:T(8,128)S(1)}, f32[8,128]{1,0:T(8,128)S(1)}, u32[]{:S(2)}, u32[]{:S(2)}) collective-permute-start(f32[8,128]{1,0:T(8,128)S(1)} %get-tuple-element.77.refs_0_), channel_id=1, source_target_pairs={{0,12},{4,0},{8,4},{12,8},{1,13},{5,1},{9,5},{13,9},{2,14},{6,2},{... | collective-permute-start | bytes 12296 | tf_op jit(solution)/shard_map/ppermute | solution.py:26
  16.6 19.7 %collective-permute-done.18.refs_1_ = bf16[256,256]{1,0:T(8,128)(2,1)S(1)} collective-permute-done((bf16[256,256]{1,0:T(8,128)(2,1)S(1)}, bf16[256,256]{1,0:T(8,128)(2,1)S(1)}, u32[]{:S(2)}, u32[]{:S(2)}) %collective-permute-start.18) | collective-permute-done | bytes 131104 | tf_op jit(solution)/shard_map/ppermute | solution.py:26
  36.3 1.6 %collective-permute-start.23 = (f32[8,128]{1,0:T(8,128)S(1)}, f32[8,128]{1,0:T(8,128)S(1)}, u32[]{:S(2)}, u32[]{:S(2)}) collective-permute-start(f32[8,128]{1,0:T(8,128)S(1)} %get-tuple-element.77.refs_0_), channel_id=1, source_target_pairs={{0,8},{4,12},{8,0},{12,4},{1,9},{5,13},{9,1},{13,5},{2,10},{6,14},... | collective-permute-start | bytes 12296 | tf_op jit(solution)/shard_map/ppermute | solution.py:26
  37.9 0.0 collective-permute-done.17.refs_0_
  37.9 2.4 %collective-permute-start.24 = (f32[8,128]{1,0:T(8,128)S(1)}, f32[8,128]{1,0:T(8,128)S(1)}, u32[]{:S(2)}, u32[]{:S(2)}) collective-permute-start(f32[8,128]{1,0:T(8,128)S(1)} %get-tuple-element.77.refs_0_), channel_id=1, source_target_pairs={{0,4},{4,8},{8,12},{12,0},{1,5},{5,9},{9,13},{13,1},{2,6},{6,10},{... | collective-permute-start | bytes 12296 | tf_op jit(solution)/shard_map/ppermute | solution.py:26
  40.2 1.3 %router_side.1.refs_0_ = f32[1,384]{1,0:T(1,128)S(1)} custom-call(s32[1,1,3]{2,1,0:T(1,128)S(4)} %get-tuple-element.61.refs_1_.blocks, bf16[512,768]{1,0:T(8,128)(2,1)S(1)} %get-tuple-element.62.refs_2_.q, bf16[512,768]{1,0:T(8,128)(2,1)S(1)} %get-tuple-element.63.refs_3_.k, bf16[512,768]{1,0:T(8,128)(2,1)S(1)} %get-tuple-element.64.refs_4_.v, ...), custom_call_target="tpu_custom_call" | custom-call | flops 226492416 | tf_op jit(solution)/shard_map/router_side/pallas_call | solution.py:451
  41.6 0.0 collective-permute-done.22.refs_1_
  41.6 3.7 %collective-permute-start.25 = (f32[1,384]{1,0:T(1,128)S(1)}, f32[1,384]{1,0:T(1,128)S(1)}, u32[]{:S(2)}, u32[]{:S(2)}) collective-permute-start(f32[1,384]{1,0:T(1,128)S(1)} %router_side.1.refs_0_), channel_id=1, source_target_pairs={{0,3},{1,0},{2,1},{3,2},{4,7},{5,4},{6,5},{7,6},{8,11},{9,8},{10,9... | collective-permute-start | bytes 4616 | tf_op jit(solution)/shard_map/ppermute | solution.py:26
  45.2 0.0 collective-permute-done.23.refs_2_
  45.2 0.0 collective-permute-start.26
  45.2 0.0 collective-permute-done.24.refs_3_
  45.2 1.0 %collective-permute-start.27 = (f32[1,384]{1,0:T(1,128)S(1)}, f32[1,384]{1,0:T(1,128)S(1)}, u32[]{:S(2)}, u32[]{:S(2)}) collective-permute-start(f32[1,384]{1,0:T(1,128)S(1)} %router_side.1.refs_0_), channel_id=1, source_target_pairs={{0,1},{1,2},{2,3},{3,0},{4,5},{5,6},{6,7},{7,4},{8,9},{9,10},{10,1... | collective-permute-start | bytes 4616 | tf_op jit(solution)/shard_map/ppermute | solution.py:26
  46.2 0.7 %place.3.refs_0_ = bf16[1,3,384,768]{3,2,1,0:T(8,128)(2,1)} custom-call(bf16[256,512]{1,0:T(8,128)(2,1)S(1)} %collective-permute-done.17.refs_0_), custom_call_target="tpu_custom_call" | custom-call | bytes 524288 | tf_op jit(solution)/shard_map/place/pallas_call | solution.py:529
  47.0 0.7 %place.4.refs_0_ = bf16[1,3,384,768]{3,2,1,0:T(8,128)(2,1)} custom-call(bf16[1,3,384,768]{3,2,1,0:T(8,128)(2,1)} %place.3.refs_0_, bf16[256,256]{1,0:T(8,128)(2,1)S(1)} %collective-permute-done.18.refs_1_), custom_call_target="tpu_custom_call", output_to_operand_aliasing={{}: (0, {})} | custom-call | bytes 262144 | tf_op jit(solution)/shard_map/place/pallas_call | solution.py:529
  47.7 0.1 pick.1
  47.8 0.0 collective-permute-done.20.refs_1_
  47.8 0.8 %place.5.whole = bf16[1,3,384,768]{3,2,1,0:T(8,128)(2,1)} custom-call(bf16[1,3,384,768]{3,2,1,0:T(8,128)(2,1)} %place.4.refs_0_, bf16[256,768]{1,0:T(8,128)(2,1)S(1)} %collective-permute-done.20.refs_1_), custom_call_target="tpu_custom_call", output_to_operand_aliasing={{}: (0, {})} | custom-call | bytes 786432 | tf_op jit(solution)/shard_map/place/pallas_call | solution.py:529
  48.6 13.6 %conditional.1 = (bf16[3,128,768]{2,1,0:T(8,128)(2,1)S(1)}) conditional(s32[]{:T(128)} %bitcast, bf16[3,128,768]{2,1,0:T(8,128)(2,1)S(1)} %get-tuple-element.78, bf16[3,128,768]{2,1,0:T(8,128)(2,1)S(1)} %get-tuple-element.78, bf16[3,128,768]{2,1,0:T(8,128)(2,1)S(1)} %get-tuple-element.78, ...), branch_computations={%region_0.0_spmd, %region_1.0_spmd, %region_2.0_spmd, %region_3.0_... | conditional | bytes 2359344 | solution.py:672
  48.6 1.3 %collective-permute-start = (bf16[3,128,768]{2,1,0:T(8,128)(2,1)S(1)}, bf16[3,128,768]{2,1,0:T(8,128)(2,1)S(1)}, u32[]{:S(2)}, u32[]{:S(2)}) collective-permute-start(bf16[3,128,768]{2,1,0:T(8,128)(2,1)S(1)} %old), channel_id=1, source_target_pairs={{0,12},{4,0},{8,4},{12,8},{16,28},{20,16},{24,20},{28,24},{1,13},{... | collective-permute-start | bytes 1769480 | tf_op jit(solution)/shard_map/cond/branch_0_fun/ppermute | solution.py:478
  49.9 12.2 %collective-permute-done.new = bf16[3,128,768]{2,1,0:T(8,128)(2,1)S(1)} collective-permute-done((bf16[3,128,768]{2,1,0:T(8,128)(2,1)S(1)}, bf16[3,128,768]{2,1,0:T(8,128)(2,1)S(1)}, u32[]{:S(2)}, u32[]{:S(2)}) %collective-permute-start) | collective-permute-done | bytes 589856 | tf_op jit(solution)/shard_map/cond/branch_0_fun/ppermute | solution.py:478
  62.1 0.0 collective-permute-done.25.refs_1_
  62.2 0.0 collective-permute-done.26.refs_2_
  62.2 0.0 collective-permute-done.27.refs_3_
  62.2 0.0 collective-permute-done.21.chunk
  62.2 1.0 %finish.1 = (bf16[1,3,384,768]{3,2,1,0:T(8,128)(2,1)}, f32[1,384]{1,0:T(1,128)}) custom-call(bf16[1,3,384,768]{3,2,1,0:T(8,128)(2,1)} %place.5.whole, bf16[256,768]{1,0:T(8,128)(2,1)S(1)} %collective-permute-done.21.chunk, bf16[3,128,768]{2,1,0:T(8,128)(2,1)S(1)} %get-tuple-element.79.tails, ...), custom_call_target="tpu_custom_call", output_to_operand_aliasing={{0}: (0, {})} | custom-call | bytes 1966080 | tf_op jit(solution)/shard_map/finish/pallas_call | solution.py:508
  (1 shorter events, 0.0 us)
Async XLA Ops:
  3.0 2.7 %collective-permute-start.19 = (f32[7,128,128]{2,1,0:T(8,128)S(1)}, f32[7,128,128]{2,1,0:T(8,128)S(1)}, u32[]{:S(2)}, u32[]{:S(2)}) collective-permute-start(f32[7,128,128]{2,1,0:T(8,128)S(1)} %get-tuple-element.67), channel_id=1, source_target_pairs={{0,16},{16,0},{1,17},{17,1},{2,18},{18,2},{3,19},{19,3},{4,20},{20... | collective-permute-start | bytes 1376264 | tf_op jit(solution)/shard_map/ppermute | solution.py:26
  6.9 40.9 %collective-permute-start.20 = (bf16[256,768]{1,0:T(8,128)(2,1)S(1)}, bf16[256,768]{1,0:T(8,128)(2,1)S(1)}, u32[]{:S(2)}, u32[]{:S(2)}) collective-permute-start(bf16[256,768]{1,0:T(8,128)(2,1)S(1)} %get-tuple-element.68), channel_id=1, source_target_pairs={{0,12},{4,0},{8,4},{12,8},{1,13},{5,1},{9,5},{13,9},{2,14},{6,2},{... | collective-permute-start | bytes 1179656 | tf_op jit(solution)/shard_map/ppermute | solution.py:26
  11.6 50.6 %collective-permute-start.21 = (bf16[256,768]{1,0:T(8,128)(2,1)S(1)}, bf16[256,768]{1,0:T(8,128)(2,1)S(1)}, u32[]{:S(2)}, u32[]{:S(2)}) collective-permute-start(bf16[256,768]{1,0:T(8,128)(2,1)S(1)} %get-tuple-element.76), channel_id=1, source_target_pairs={{0,12},{4,0},{8,4},{12,8},{1,13},{5,1},{9,5},{13,9},{2,14},{6,2},{... | collective-permute-start | bytes 1179656 | tf_op jit(solution)/shard_map/ppermute | solution.py:26
  12.2 25.7 %collective-permute-start.17 = (bf16[256,512]{1,0:T(8,128)(2,1)S(1)}, bf16[256,512]{1,0:T(8,128)(2,1)S(1)}, u32[]{:S(2)}, u32[]{:S(2)}) collective-permute-start(bf16[256,512]{1,0:T(8,128)(2,1)S(1)} %get-tuple-element.58), channel_id=1, source_target_pairs={{0,12},{4,0},{8,4},{12,8},{1,13},{5,1},{9,5},{13,9},{2,14},{6,2},{... | collective-permute-start | bytes 786440 | tf_op jit(solution)/shard_map/ppermute | solution.py:26
  13.6 22.7 %collective-permute-start.18 = (bf16[256,256]{1,0:T(8,128)(2,1)S(1)}, bf16[256,256]{1,0:T(8,128)(2,1)S(1)}, u32[]{:S(2)}, u32[]{:S(2)}) collective-permute-start(bf16[256,256]{1,0:T(8,128)(2,1)S(1)} %get-tuple-element.59), channel_id=1, source_target_pairs={{0,12},{4,0},{8,4},{12,8},{1,13},{5,1},{9,5},{13,9},{2,14},{6,2},{... | collective-permute-start | bytes 393224 | tf_op jit(solution)/shard_map/ppermute | solution.py:26
  13.7 27.9 %collective-permute-start.22 = (f32[8,128]{1,0:T(8,128)S(1)}, f32[8,128]{1,0:T(8,128)S(1)}, u32[]{:S(2)}, u32[]{:S(2)}) collective-permute-start(f32[8,128]{1,0:T(8,128)S(1)} %get-tuple-element.77.refs_0_), channel_id=1, source_target_pairs={{0,12},{4,0},{8,4},{12,8},{1,13},{5,1},{9,5},{13,9},{2,14},{6,2},{... | collective-permute-start | bytes 12296 | tf_op jit(solution)/shard_map/ppermute | solution.py:26
  36.3 8.9 %collective-permute-start.23 = (f32[8,128]{1,0:T(8,128)S(1)}, f32[8,128]{1,0:T(8,128)S(1)}, u32[]{:S(2)}, u32[]{:S(2)}) collective-permute-start(f32[8,128]{1,0:T(8,128)S(1)} %get-tuple-element.77.refs_0_), channel_id=1, source_target_pairs={{0,8},{4,12},{8,0},{12,4},{1,9},{5,13},{9,1},{13,5},{2,10},{6,14},... | collective-permute-start | bytes 12296 | tf_op jit(solution)/shard_map/ppermute | solution.py:26
  37.9 7.4 %collective-permute-start.24 = (f32[8,128]{1,0:T(8,128)S(1)}, f32[8,128]{1,0:T(8,128)S(1)}, u32[]{:S(2)}, u32[]{:S(2)}) collective-permute-start(f32[8,128]{1,0:T(8,128)S(1)} %get-tuple-element.77.refs_0_), channel_id=1, source_target_pairs={{0,4},{4,8},{8,12},{12,0},{1,5},{5,9},{9,13},{13,1},{2,6},{6,10},{... | collective-permute-start | bytes 12296 | tf_op jit(solution)/shard_map/ppermute | solution.py:26
  41.6 20.6 %collective-permute-start.25 = (f32[1,384]{1,0:T(1,128)S(1)}, f32[1,384]{1,0:T(1,128)S(1)}, u32[]{:S(2)}, u32[]{:S(2)}) collective-permute-start(f32[1,384]{1,0:T(1,128)S(1)} %router_side.1.refs_0_), channel_id=1, source_target_pairs={{0,3},{1,0},{2,1},{3,2},{4,7},{5,4},{6,5},{7,6},{8,11},{9,8},{10,9... | collective-permute-start | bytes 4616 | tf_op jit(solution)/shard_map/ppermute | solution.py:26
  45.2 16.9 %collective-permute-start.26 = (f32[1,384]{1,0:T(1,128)S(1)}, f32[1,384]{1,0:T(1,128)S(1)}, u32[]{:S(2)}, u32[]{:S(2)}) collective-permute-start(f32[1,384]{1,0:T(1,128)S(1)} %router_side.1.refs_0_), channel_id=1, source_target_pairs={{0,2},{1,3},{2,0},{3,1},{4,6},{5,7},{6,4},{7,5},{8,10},{9,11},{10,... | collective-permute-start | bytes 4616 | tf_op jit(solution)/shard_map/ppermute | solution.py:26
  45.2 16.9 %collective-permute-start.27 = (f32[1,384]{1,0:T(1,128)S(1)}, f32[1,384]{1,0:T(1,128)S(1)}, u32[]{:S(2)}, u32[]{:S(2)}) collective-permute-start(f32[1,384]{1,0:T(1,128)S(1)} %router_side.1.refs_0_), channel_id=1, source_target_pairs={{0,1},{1,2},{2,3},{3,0},{4,5},{5,6},{6,7},{7,4},{8,9},{9,10},{10,1... | collective-permute-start | bytes 4616 | tf_op jit(solution)/shard_map/ppermute | solution.py:26
  48.6 13.5 %collective-permute-start = (bf16[3,128,768]{2,1,0:T(8,128)(2,1)S(1)}, bf16[3,128,768]{2,1,0:T(8,128)(2,1)S(1)}, u32[]{:S(2)}, u32[]{:S(2)}) collective-permute-start(bf16[3,128,768]{2,1,0:T(8,128)(2,1)S(1)} %old), channel_id=1, source_target_pairs={{0,12},{4,0},{8,4},{12,8},{16,28},{20,16},{24,20},{28,24},{1,13},{... | collective-permute-start | bytes 1769480 | tf_op jit(solution)/shard_map/cond/branch_0_fun/ppermute | solution.py:478

commit v7 on v6

--- a/solution.py
+++ b/solution.py
@@ -124,8 +124,8 @@
 
 
 def open_kernel(
-    factor, query_side, end, router, blocks, q, k, v, g, chunk, tail,
-    router_buf, blocks_buf, x_buf, v_buf, g_buf, c_buf, scores_buf, states_buf, acc,
+    factor, query_side, end, router, blocks, q, k, v, g, chunk, tail, router_buf, blocks_buf,
+    x_buf, v_buf, g_buf, c_buf, scores_buf, states_buf, acc,
     small_sem, load_sem,
 ):
     slots = blocks.shape[2]
@@ -208,12 +208,11 @@
     return pl.pallas_call(
         functools.partial(open_kernel, factor, query_side, end),
         name="opened",
-        out_shape=split_rows(slots, end * HEAD_SIZE),
+        out_shape=split_rows(slots, end * HEAD_SIZE)
+        + [pltpu.VMEM(router.shape, router.dtype), pltpu.SMEM(blocks.shape, blocks.dtype)],
         in_specs=[HBM] * 6,
-        out_specs=[VMEM] * 2,
+        out_specs=[VMEM] * 3 + [SMEM],
         scratch_shapes=[
-            pltpu.VMEM(router.shape, router.dtype),
-            pltpu.SMEM(blocks.shape, blocks.dtype),
             part, part, part,
             pltpu.VMEM((slots * BLOCK_ROWS, end * HEAD_SIZE), jnp.bfloat16),
             pltpu.VMEM((slots, end, HEAD_SIZE, HEAD_SIZE), jnp.bfloat16),
@@ -235,29 +234,10 @@
     elif seeded:
         c_all, seed, chunk, states, scores_buf, total = refs
     else:
-        sources = (router, blocks, q, k, v, g)
-        chunk, tail, states, total, c_all, *targets = refs[:11]
-        scores_buf, load_sem = refs[11:]
-        router, blocks, q, k, v, g = targets
+        chunk, tail, states, total, c_all, scores_buf = refs
     slots = blocks.shape[2]
     heads = states.shape[1]
     difference = row_minus_column()
-
-    if not seeded:
-        loads = [
-            pltpu.make_async_copy(source if j < 2 else source.at[0], target, load_sem.at[j])
-            for j, (source, target) in enumerate(zip(sources, targets))
-        ]
-        for j in (1, 0, 5, 4):
-            loads[j].start()
-
-        def start(query):
-            for j in (3, 2) if query else (2, 3):
-                loads[j].start()
-
-        by_role(query_side, start)
-        for j in (1, 0, 5):
-            loads[j].wait()
 
     def body(query):
         allowed = difference >= 0 if query else difference <= 0
@@ -269,8 +249,6 @@
                 weight = jnp.where(live_of(blocks, n), down_rows(router, block), 0.0)
                 for h in range(heads):
                     c_all[rows_of(n), lanes(h)] = weigh(weight, g[rows_of(block), lanes(h)])
-            for j in (4, 3 if query else 2):
-                loads[j].wait()
         for i, n in enumerate(order):
             live = live_of(blocks, n)
             rows = rows_of(blocks[0, 0, n])
@@ -312,7 +290,6 @@
         full = jnp.where(live_of(blocks, slots - 1), 1.0, 0.0)
         if not seeded:
             total[heads] = jnp.full((HEAD_SIZE, HEAD_SIZE), full, jnp.float32)
-            loads[2 if query else 3].wait()
         elif split:
             other = seed[heads, 0:8, :]
             own_full = jnp.full(other.shape, full, jnp.float32)
@@ -322,8 +299,8 @@
 
 
 def side(factor, query_side, begin, split, arrays, c_all=None, seed=None):
-    router, blocks = arrays[:2]
-    shard_rows, width = arrays[2].shape[-2:]
+    _, blocks = arrays[:2]
+    width = arrays[2].shape[1]
     heads = width // HEAD_SIZE
     slots = blocks.shape[2]
     square = (HEAD_SIZE, HEAD_SIZE)
@@ -338,28 +315,21 @@
     if seeded:
         if split:
             out_shape.append(pltpu.VMEM((8, HEAD_SIZE), jnp.float32))
-        out_specs = [VMEM] * len(out_shape)
         scratch.append(pltpu.VMEM((heads,) + square, jnp.float32))
         extra = (c_all, seed)
-        in_specs = [VMEM, SMEM] + [VMEM] * 6
     else:
         out_shape.append(pltpu.VMEM((heads + 1,) + square, jnp.float32))
         out_shape.append(pltpu.VMEM((slots * BLOCK_ROWS, width), jnp.bfloat16))
-        out_shape += [pltpu.VMEM(router.shape, router.dtype), pltpu.SMEM(blocks.shape, blocks.dtype)]
-        out_shape += [pltpu.VMEM((shard_rows, width), jnp.bfloat16)] * 4
-        out_specs = [VMEM] * 6 + [SMEM] + [VMEM] * 4
-        scratch.append(pltpu.SemaphoreType.DMA((6,)))
         extra = ()
-        in_specs = [HBM] * 6
     return pl.pallas_call(
         functools.partial(side_kernel, factor, query_side, begin, seeded, split),
         name="side",
         out_shape=out_shape,
-        in_specs=in_specs,
-        out_specs=out_specs,
+        in_specs=[VMEM, SMEM] + [VMEM] * (4 + len(extra)),
+        out_specs=[VMEM] * len(out_shape),
         scratch_shapes=scratch,
         compiler_params=compiler_params(),
-        cost_estimate=cost(4 * slots * heads, 0 if seeded else 8 * shard_rows * width),
+        cost_estimate=cost(4 * slots * heads, 0),
     )(*arrays, *extra)
 
 
@@ -469,59 +439,56 @@
     copy.wait()
 
 
-def keep_kernel(old, new, out):
+def keep_kernel(old, new, *refs):
     del old
+    parts, (out, total) = refs[:-2], refs[-2:]
     out[...] = new[...]
-
-
-def third(pairs, tails):
+    total[...] = folded([part[...] for part in parts])
+
+
+def third(pairs, tails, partial):
     received = lax.ppermute(tails, ("seq", "pipe"), pairs)
+    parts = [partial]
+    parts += [from_behind(partial, "tp", -k) for k in range(1, lax.axis_size("tp"))]
     return pl.pallas_call(
         keep_kernel,
         name="keep",
-        out_shape=pltpu.VMEM(tails.shape, tails.dtype),
-        in_specs=[VMEM] * 2,
-        out_specs=VMEM,
-        input_output_aliases={0: 0},
+        out_shape=[
+            pltpu.VMEM(tails.shape, tails.dtype), pltpu.VMEM(partial.shape, partial.dtype)
+        ],
+        in_specs=[VMEM] * (2 + len(parts)),
+        out_specs=[VMEM] * 2,
+        input_output_aliases={0: 0, 2: 1},
         compiler_params=pltpu.CompilerParams(vmem_limit_bytes=2**20),
-    )(tails, received)
-
-
-def finish_kernel(section, whole, chunk, tails, *refs):
+    )(tails, received, *parts)
+
+
+def finish_kernel(section, whole, chunk, tails, part, out, total, sem):
     del whole
-    parts, (out, total, total_buf, sem) = refs[:-4], refs[-4:]
     rows = chunk.shape[0]
     copies = [
         pltpu.make_async_copy(tails, out.at[0, :, pl.ds(rows, tails.shape[1])], sem.at[0]),
         pltpu.make_async_copy(chunk, out.at[0, section, pl.ds(0, rows)], sem.at[1]),
-        pltpu.make_async_copy(total_buf, total, sem.at[2]),
+        pltpu.make_async_copy(part, total, sem.at[2]),
     ]
-    copies[0].start()
-    copies[1].start()
-    total_buf[...] = folded([part[...] for part in parts])
-    copies[2].start()
+    for copy in copies:
+        copy.start()
     for copy in copies:
         copy.wait()
 
 
-def finish(section, whole, chunk, tails, parts):
+def finish(section, whole, chunk, tails, total):
     return pl.pallas_call(
         functools.partial(finish_kernel, section),
         name="finish",
-        out_shape=[
-            pltpu.HBM(whole.shape, whole.dtype),
-            pltpu.HBM(parts[0].shape, parts[0].dtype),
-        ],
-        in_specs=[HBM, ANY, ANY] + [VMEM] * len(parts),
+        out_shape=[pltpu.HBM(whole.shape, whole.dtype), pltpu.HBM(total.shape, total.dtype)],
+        in_specs=[HBM, ANY, ANY, ANY],
         out_specs=[HBM, HBM],
-        scratch_shapes=[
-            pltpu.VMEM(parts[0].shape, parts[0].dtype),
-            pltpu.SemaphoreType.DMA((3,)),
-        ],
+        scratch_shapes=[pltpu.SemaphoreType.DMA((3,))],
         input_output_aliases={0: 0},
         compiler_params=pltpu.CompilerParams(vmem_limit_bytes=2**20),
         cost_estimate=cost(0, 4 * (chunk.size + tails.size)),
-    )(whole, chunk, tails, *parts)
+    )(whole, chunk, tails, total)
 
 
 def place(whole, chunk, shape, section_of, begin):
@@ -565,6 +532,13 @@
     )(*infos)
 
 
+def other_core(pipe_count, by):
+    return [
+        (s * pipe_count + p, (1 - s) * pipe_count + (p - by) % pipe_count)
+        for s in (0, 1) for p in range(pipe_count)
+    ]
+
+
 def third_pairs(pipe_count):
     def pair(s, p):
         return (s * pipe_count + p, s * pipe_count + (p - 1) % pipe_count)
@@ -636,41 +610,46 @@
     arrays = (queries, keys, values, grad_out)
     shape = (1, 3, rows, width)
     if fits(seq_count, pipe_count, tp_count, slots):
-        head_start = max(1, 2 * heads // 3)
+        head_start = max(1, heads // 2)
         small = (in_hbm(router), in_hbm(blocks))
-        arrays = tuple(in_hbm(x) for x in arrays)
+        held = tuple(in_hbm(x) for x in arrays)
 
         def sent(x, axis="pipe", by=-1):
             return from_behind(x, axis, by)
 
+        def across(x, pairs):
+            return lax.ppermute(x, ("seq", "pipe"), pairs)
+
         def kernel(call, *operands):
             return call(factor, *operands)
 
-        chunk_a, tail_a = kernel(opened, is_first, head_start, small, arrays)
+        chunk_a, tail_a, *loaded = kernel(opened, is_first, head_start, small, held)
+        loaded += [x[0] for x in arrays]
         chunk_a = sent(chunk_a)
-        chunk_b, tail_b, own, total, c_all, *loaded = kernel(
-            side, is_first, head_start, True, small + arrays
-        )
+        chunk_b, tail_b, own, total, c_all = kernel(side, is_first, head_start, True, loaded)
         total = sent(total, "seq", 1)
         chunk_b = sent(chunk_b)
         chunk_c, tail_c, other, info = kernel(side, is_last, 0, True, loaded, c_all, total)
         chunk_c = sent(chunk_c)
-        infos = [info] + [sent(info, "pipe", -k) for k in range(1, pipe_count)]
+        infos = [info] + [across(info, other_core(pipe_count, k)) for k in range(1, pipe_count)]
         chunk_d, tails = kernel(
             value_side, is_last, loaded, c_all, own, other, (tail_a, tail_b, tail_c)
         )
         chunk_d = sent(chunk_d)
         partial = kernel(router_side, is_first, loaded, own, other)
-        parts = [partial] + [sent(partial, "tp", -k) for k in range(1, tp_count)]
-        handed = place(None, chunk_a, shape, own_side, 0)
-        handed = place(handed, chunk_b, shape, own_side, head_start)
-        handed = place(handed, chunk_c, shape, other_side, 0)
         choice = pick(infos)[0, 0]
 
-        branches = [functools.partial(third, pairs) for pairs in third_pairs(pipe_count)]
-        handed, tails = lax.optimization_barrier((handed, tails))
-        tails = lax.switch(choice, branches, tails)
-        handed, router_grad = finish(2, handed, chunk_d, tails, parts)
+        def branch(pairs, tails, partial, a, b, c):
+            handed = place(None, a, shape, own_side, 0)
+            handed = place(handed, b, shape, own_side, head_start)
+            handed = place(handed, c, shape, other_side, 0)
+            return handed, *third(pairs, tails, partial)
+
+        branches = [functools.partial(branch, pairs) for pairs in third_pairs(pipe_count)]
+        handed, tails, router_grad = lax.switch(
+            choice, branches, tails, partial, chunk_a, chunk_b, chunk_c
+        )
+        handed, router_grad = finish(2, handed, chunk_d, tails, router_grad)
     else:
         index = lax.axis_index("seq")
         places = jnp.arange(seq_count)[:, None, None, None]

time: 63.3 us -> 60.9 us (0.962)
  Pallas kernels: 11.5 us -> 9.76 us
  starting transfers between devices: 18.9 us -> 17.4 us
    ppermute x0 -> x3, waiting for transfers between devices: none -> 24.5 us  [across(): return lax.ppermute(x, ('seq', 'pipe'), pairs)]
    ppermute x11 -> x8, waiting for transfers between devices: 19.7 us -> 1.49 us  [from_behind(): return lax.ppermute(x, axis, [(i, (i + by) % count) for i in range(count)])]
    ppermute x1, waiting for transfers between devices: 12.2 us -> 6.12 us  [third(): received = lax.ppermute(tails, ('seq', 'pipe'), pairs)]
    ppermute x11 -> x8, starting transfers between devices: 17.7 us -> 12 us  [from_behind(): return lax.ppermute(x, axis, [(i, (i + by) % count) for i in range(count)])]
    ppermute x0 -> x3, starting transfers between devices: none -> 3.03 us  [across(): return lax.ppermute(x, ('seq', 'pipe'), pairs)]
    pallas_call x2, Pallas kernels: 3.5 us -> 1.92 us  [side(): pl.pallas_call(functools.partial(side_kernel, factor, query_side, begin,...]
    ppermute x1, starting transfers between devices: 1.27 us -> 2.37 us  [third(): received = lax.ppermute(tails, ('seq', 'pipe'), pairs)]
  transfers between devices with their start and end apart: 12 -> 12, of which waited for: 2 -> 4; matrix products, arithmetic and copies ran while one was open for 0% -> 0% of each run, Pallas kernels for 11% -> 8%
where the time goes in v7:
time: 60.9 us; the launch traced here: 60.6 us
  waiting for transfers between devices  32.1 us (53%)
  starting transfers between devices  17.4 us (29%)
  Pallas kernels  9.76 us (16%)
  between operations  0.95 us (2%)
    ppermute x3, waiting for transfers between devices, across(): return lax.ppermute(x, ('seq', 'pipe'), pairs)  24.5 us
    ppermute x8, starting transfers between devices, from_behind(): return lax.ppermute(x, axis, [(i, (i + by) % count) for i in range(count)])  12 us
    ppermute x1, waiting for transfers between devices, third(): received = lax.ppermute(tails, ('seq', 'pipe'), pairs)  6.12 us
    ppermute x3, starting transfers between devices, across(): return lax.ppermute(x, ('seq', 'pipe'), pairs)  3.03 us
    ppermute x1, starting transfers between devices, third(): received = lax.ppermute(tails, ('seq', 'pipe'), pairs)  2.37 us
    pallas_call x3, Pallas kernels, place(): pl.pallas_call(functools.partial(place_kernel, section_of, begin), name='...  2.15 us
    pallas_call x1, Pallas kernels, opened(): pl.pallas_call(functools.partial(open_kernel, factor, query_side, end), n...  2.05 us
    pallas_call x2, Pallas kernels, side(): pl.pallas_call(functools.partial(side_kernel, factor, query_side, begin,...  1.92 us
  transfers between devices with their start and end apart: 12, of which 4 were waited for; matrix products, arithmetic and copies ran while one was open for 0% of the time, Pallas kernels for 8%

profile of v7, /device:TPU:0, one launch (start us, length us, event | category | flops | bytes accessed | tf_op | source)
XLA Modules:
  0.0 60.6 jit_solution(75850165332802229)
XLA Ops:
  0.6 0.0 copy-start.3
  0.6 0.0 copy-start.2
  0.7 0.0 copy-start.1
  0.7 0.0 copy-start
  0.7 2.0 %opened.1 = (bf16[256,384]{1,0:T(8,128)(2,1)S(1)}, bf16[128,384]{1,0:T(8,128)(2,1)S(1)}, f32[1,512]{1,0:T(1,128)S(1)}, s32[1,1,3]{2,1,0:T(1,128)S(4)}) custom-call(f32[1,512]{1,0:T(1,128)} %router.1, s32[1,1,3]{2,1,0:T(1,128)} %blocks.1, bf16[1,512,768]{2,1,0:T(8,128)(2,1)} %q.1, bf16[1,512,768]{2,1,0:T(8,128)(2,1)} %k.1, bf16[1,512,768]{2,1,0:T(8,128)(2,1)} %v.1, ...), custom_call_target="tpu_custom_call" | custom-call | flops 150994944 | bytes 1179648 | tf_op jit(solution)/shard_map/opened/pallas_call | solution.py:208
  2.7 0.0 copy-done.3
  2.7 0.0 copy-done.2
  2.7 0.0 copy-done.1
  2.8 0.1 copy-done
  2.9 0.9 %side.2 = (bf16[256,384]{1,0:T(8,128)(2,1)S(1)}, bf16[128,384]{1,0:T(8,128)(2,1)S(1)}, bf16[3,6,128,128]{3,2,1,0:T(8,128)(2,1)S(1)}, f32[7,128,128]{2,1,0:T(8,128)S(1)}, bf16[384,768]{1,0:T(8,128)(2,1)S(1)}) custom-call(f32[1,512]{1,0:T(1,128)S(1)} %get-tuple-element.309.refs_0_, s32[1,1,3]{2,1,0:T(1,128)S(4)} %get-tuple-element.310.refs_1_.blocks, ...), custom_call_target="tpu_custom_call" | custom-call | flops 301989888 | tf_op jit(solution)/shard_map/side/pallas_call | solution.py:324
  3.7 0.6 %collective-permute-start.68 = (f32[7,128,128]{2,1,0:T(8,128)S(1)}, f32[7,128,128]{2,1,0:T(8,128)S(1)}, u32[]{:S(2)}, u32[]{:S(2)}) collective-permute-start(f32[7,128,128]{2,1,0:T(8,128)S(1)} %get-tuple-element.312), channel_id=1, source_target_pairs={{0,16},{16,0},{1,17},{17,1},{2,18},{18,2},{3,19},{19,3},{4,20},{20... | collective-permute-start | bytes 1376264 | tf_op jit(solution)/shard_map/ppermute | solution.py:26
  4.4 1.4 %collective-permute-done.68.refs_7_ = f32[7,128,128]{2,1,0:T(8,128)S(1)} collective-permute-done((f32[7,128,128]{2,1,0:T(8,128)S(1)}, f32[7,128,128]{2,1,0:T(8,128)S(1)}, u32[]{:S(2)}, u32[]{:S(2)}) %collective-permute-start.68) | collective-permute-done | bytes 458784 | tf_op jit(solution)/shard_map/ppermute | solution.py:26
  5.8 1.0 %side.3 = (bf16[256,768]{1,0:T(8,128)(2,1)S(1)}, bf16[128,768]{1,0:T(8,128)(2,1)S(1)}, bf16[3,6,128,128]{3,2,1,0:T(8,128)(2,1)S(1)}, f32[8,128]{1,0:T(8,128)S(1)}) custom-call(f32[1,512]{1,0:T(1,128)S(1)} %get-tuple-element.309.refs_0_, s32[1,1,3]{2,1,0:T(1,128)S(4)} %get-tuple-element.310.refs_1_.blocks, bf16[512,768]{1,0:T(8,128)(2,1)S(1)} %bitcast.6, ...), custom_call_target="tpu_custom_call" | custom-call | flops 301989888 | tf_op jit(solution)/shard_map/side/pallas_call | solution.py:324
  6.9 3.8 %collective-permute-start.74 = (bf16[256,768]{1,0:T(8,128)(2,1)S(1)}, bf16[256,768]{1,0:T(8,128)(2,1)S(1)}, u32[]{:S(2)}, u32[]{:S(2)}) collective-permute-start(bf16[256,768]{1,0:T(8,128)(2,1)S(1)} %get-tuple-element.316), channel_id=1, source_target_pairs={{0,12},{4,0},{8,4},{12,8},{1,13},{5,1},{9,5},{13,9},{2,14},{6,2},{... | collective-permute-start | bytes 1179656 | tf_op jit(solution)/shard_map/ppermute | solution.py:26
  10.7 1.2 %value_side.1 = (bf16[256,768]{1,0:T(8,128)(2,1)S(1)}, bf16[3,128,768]{2,1,0:T(8,128)(2,1)S(1)}) custom-call(s32[1,1,3]{2,1,0:T(1,128)S(4)} %get-tuple-element.310.refs_1_.blocks, bf16[512,768]{1,0:T(8,128)(2,1)S(1)} %bitcast.7, bf16[512,768]{1,0:T(8,128)(2,1)S(1)} %bitcast.11, bf16[384,768]{1,0:T(8,128)(2,1)S(1)} %get-tuple-element.311.refs_6_.c_all, ...), custom_call_target="tpu_custom_call" | custom-call | flops 226492416 | tf_op jit(solution)/shard_map/value_side/pallas_call | solution.py:382
  11.9 0.6 collective-permute-start.75
  12.5 1.4 %collective-permute-start.72 = (bf16[256,384]{1,0:T(8,128)(2,1)S(1)}, bf16[256,384]{1,0:T(8,128)(2,1)S(1)}, u32[]{:S(2)}, u32[]{:S(2)}) collective-permute-start(bf16[256,384]{1,0:T(8,128)(2,1)S(1)} %get-tuple-element.314), channel_id=1, source_target_pairs={{0,12},{4,0},{8,4},{12,8},{1,13},{5,1},{9,5},{13,9},{2,14},{6,2},{... | collective-permute-start | bytes 589832 | tf_op jit(solution)/shard_map/ppermute | solution.py:26
  13.9 0.1 collective-permute-start.73
  14.0 0.6 collective-permute-start.71
  14.5 21.9 %collective-permute-done.71.refs_3_ = f32[8,128]{1,0:T(8,128)S(1)} collective-permute-done((f32[8,128]{1,0:T(8,128)S(1)}, f32[8,128]{1,0:T(8,128)S(1)}, u32[]{:S(2)}, u32[]{:S(2)}) %collective-permute-start.71) | collective-permute-done | bytes 4128 | tf_op jit(solution)/shard_map/ppermute | solution.py:621
  36.5 0.5 collective-permute-start.70
  37.0 2.5 %collective-permute-done.70.refs_2_ = f32[8,128]{1,0:T(8,128)S(1)} collective-permute-done((f32[8,128]{1,0:T(8,128)S(1)}, f32[8,128]{1,0:T(8,128)S(1)}, u32[]{:S(2)}, u32[]{:S(2)}) %collective-permute-start.70) | collective-permute-done | bytes 4128 | tf_op jit(solution)/shard_map/ppermute | solution.py:621
  39.5 2.0 %collective-permute-start.69 = (f32[8,128]{1,0:T(8,128)S(1)}, f32[8,128]{1,0:T(8,128)S(1)}, u32[]{:S(2)}, u32[]{:S(2)}) collective-permute-start(f32[8,128]{1,0:T(8,128)S(1)} %get-tuple-element.313.refs_0_), channel_id=1, source_target_pairs={{0,28},{4,16},{8,20},{12,24},{16,12},{20,0},{24,4},{28,8},{1,29},{... | collective-permute-start | bytes 12296 | tf_op jit(solution)/shard_map/ppermute | solution.py:621
  41.5 1.3 %router_side.1 = f32[1,384]{1,0:T(1,128)S(1)} custom-call(s32[1,1,3]{2,1,0:T(1,128)S(4)} %get-tuple-element.310.refs_1_.blocks, bf16[512,768]{1,0:T(8,128)(2,1)S(1)} %bitcast.8, bf16[512,768]{1,0:T(8,128)(2,1)S(1)} %bitcast.12, bf16[512,768]{1,0:T(8,128)(2,1)S(1)} %bitcast.15, bf16[512,768]{1,0:T(8,128)(2,1)S(1)} %bitcast.18, ...), custom_call_target="tpu_custom_call" | custom-call | flops 226492416 | tf_op jit(solution)/shard_map/router_side/pallas_call | solution.py:421
  42.8 0.0 collective-permute-done.69.refs_1_
  42.8 0.1 pick.1
  42.9 0.0 collective-permute-done.72
  42.9 0.0 collective-permute-done.73
  43.0 0.0 collective-permute-done.74
  43.0 16.5 %conditional.1 = (bf16[1,3,384,768]{3,2,1,0:T(8,128)(2,1)}, bf16[3,128,768]{2,1,0:T(8,128)(2,1)S(1)}, f32[1,384]{1,0:T(1,128)S(1)}) conditional(s32[]{:T(128)} %bitcast.4, (bf16[256,384]{1,0:T(8,128)(2,1)S(1)}, bf16[256,384]{1,0:T(8,128)(2,1)S(1)}, bf16[256,768]{1,0:T(8,128)(2,1)S(1)}, ...), branch_computations={%region_0.0_spmd, %region_1.0_spmd, %region_2.0_spmd, %region_3.0_... | conditional | bytes 3950776 | solution.py:649
  43.0 2.4 %collective-permute-start = (bf16[3,128,768]{2,1,0:T(8,128)(2,1)S(1)}, bf16[3,128,768]{2,1,0:T(8,128)(2,1)S(1)}, u32[]{:S(2)}, u32[]{:S(2)}) collective-permute-start(bf16[3,128,768]{2,1,0:T(8,128)(2,1)S(1)} %get-tuple-element.173.old), channel_id=1, source_target_pairs={{0,12},{4,0},{8,4},{12,8},{16,28},{20,16},{24,20},{28,24},{1,13},{... | collective-permute-start | bytes 1769480 | tf_op jit(solution)/shard_map/cond/branch_0_fun/ppermute | solution.py:450
  45.4 1.6 %collective-permute-start.3 = (f32[1,384]{1,0:T(1,128)S(1)}, f32[1,384]{1,0:T(1,128)S(1)}, u32[]{:S(2)}, u32[]{:S(2)}) collective-permute-start(f32[1,384]{1,0:T(1,128)S(1)} %get-tuple-element.174.refs_0_), channel_id=1, source_target_pairs={{0,1},{1,2},{2,3},{3,0},{4,5},{5,6},{6,7},{7,4},{8,9},{9,10},{10,1... | collective-permute-start | bytes 4616 | tf_op jit(solution)/shard_map/cond/branch_0_fun/ppermute | solution.py:26
  46.9 2.6 %collective-permute-start.2 = (f32[1,384]{1,0:T(1,128)S(1)}, f32[1,384]{1,0:T(1,128)S(1)}, u32[]{:S(2)}, u32[]{:S(2)}) collective-permute-start(f32[1,384]{1,0:T(1,128)S(1)} %get-tuple-element.174.refs_0_), channel_id=1, source_target_pairs={{0,2},{1,3},{2,0},{3,1},{4,6},{5,7},{6,4},{7,5},{8,10},{9,11},{10,... | collective-permute-start | bytes 4616 | tf_op jit(solution)/shard_map/cond/branch_0_fun/ppermute | solution.py:26
  49.5 1.3 %collective-permute-start.1 = (f32[1,384]{1,0:T(1,128)S(1)}, f32[1,384]{1,0:T(1,128)S(1)}, u32[]{:S(2)}, u32[]{:S(2)}) collective-permute-start(f32[1,384]{1,0:T(1,128)S(1)} %get-tuple-element.174.refs_0_), channel_id=1, source_target_pairs={{0,3},{1,0},{2,1},{3,2},{4,7},{5,4},{6,5},{7,6},{8,11},{9,8},{10,9... | collective-permute-start | bytes 4616 | tf_op jit(solution)/shard_map/cond/branch_0_fun/ppermute | solution.py:26
  50.9 0.7 %place.51.refs_0_ = bf16[1,3,384,768]{3,2,1,0:T(8,128)(2,1)} custom-call(bf16[256,384]{1,0:T(8,128)(2,1)S(1)} %get-tuple-element.170.refs_0_), custom_call_target="tpu_custom_call" | custom-call | bytes 393216 | tf_op jit(solution)/shard_map/cond/branch_0_fun/place/pallas_call | solution.py:496
  51.6 0.7 %place.52.refs_0_ = bf16[1,3,384,768]{3,2,1,0:T(8,128)(2,1)} custom-call(bf16[1,3,384,768]{3,2,1,0:T(8,128)(2,1)} %place.51.refs_0_, bf16[256,384]{1,0:T(8,128)(2,1)S(1)} %get-tuple-element.171.refs_1_), custom_call_target="tpu_custom_call", output_to_operand_aliasing={{}: (0, {})} | custom-call | bytes 393216 | tf_op jit(solution)/shard_map/cond/branch_0_fun/place/pallas_call | solution.py:496
  52.3 0.8 %place.53 = bf16[1,3,384,768]{3,2,1,0:T(8,128)(2,1)} custom-call(bf16[1,3,384,768]{3,2,1,0:T(8,128)(2,1)} %place.52.refs_0_, bf16[256,768]{1,0:T(8,128)(2,1)S(1)} %get-tuple-element.172.refs_1_), custom_call_target="tpu_custom_call", output_to_operand_aliasing={{}: (0, {})} | custom-call | bytes 786432 | tf_op jit(solution)/shard_map/cond/branch_0_fun/place/pallas_call | solution.py:496
  53.1 0.0 collective-permute-done.3.refs_3_
  53.1 0.0 collective-permute-done.2.refs_2_
  53.1 0.0 collective-permute-done.1.refs_1_
  53.1 6.1 %collective-permute-done.new = bf16[3,128,768]{2,1,0:T(8,128)(2,1)S(1)} collective-permute-done((bf16[3,128,768]{2,1,0:T(8,128)(2,1)S(1)}, bf16[3,128,768]{2,1,0:T(8,128)(2,1)S(1)}, u32[]{:S(2)}, u32[]{:S(2)}) %collective-permute-start) | collective-permute-done | bytes 589856 | tf_op jit(solution)/shard_map/cond/branch_0_fun/ppermute | solution.py:450
  59.5 0.0 collective-permute-done.75.chunk
  59.5 1.0 %finish.1 = (bf16[1,3,384,768]{3,2,1,0:T(8,128)(2,1)}, f32[1,384]{1,0:T(1,128)}) custom-call(bf16[1,3,384,768]{3,2,1,0:T(8,128)(2,1)} %get-tuple-element.323.whole, bf16[256,768]{1,0:T(8,128)(2,1)S(1)} %collective-permute-done.75.chunk, bf16[3,128,768]{2,1,0:T(8,128)(2,1)S(1)} %get-tuple-element.325.tails, ...), custom_call_target="tpu_custom_call", output_to_operand_aliasing={{0}: (0, {})} | custom-call | bytes 1966080 | tf_op jit(solution)/shard_map/finish/pallas_call | solution.py:481
  (1 shorter events, 0.0 us)
Async XLA Ops:
  0.6 2.1 %copy-start.3 = (bf16[1,512,768]{2,1,0:T(8,128)(2,1)S(1)}, bf16[1,512,768]{2,1,0:T(8,128)(2,1)}, u32[]{:S(2)}) copy-start(bf16[1,512,768]{2,1,0:T(8,128)(2,1)} %g.1) | copy-start | bytes 2359300
  0.6 2.1 %copy-start.2 = (bf16[1,512,768]{2,1,0:T(8,128)(2,1)S(1)}, bf16[1,512,768]{2,1,0:T(8,128)(2,1)}, u32[]{:S(2)}) copy-start(bf16[1,512,768]{2,1,0:T(8,128)(2,1)} %v.1) | copy-start | bytes 2359300
  0.7 2.1 %copy-start.1 = (bf16[1,512,768]{2,1,0:T(8,128)(2,1)S(1)}, bf16[1,512,768]{2,1,0:T(8,128)(2,1)}, u32[]{:S(2)}) copy-start(bf16[1,512,768]{2,1,0:T(8,128)(2,1)} %k.1) | copy-start | bytes 2359300
  0.7 2.2 %copy-start = (bf16[1,512,768]{2,1,0:T(8,128)(2,1)S(1)}, bf16[1,512,768]{2,1,0:T(8,128)(2,1)}, u32[]{:S(2)}) copy-start(bf16[1,512,768]{2,1,0:T(8,128)(2,1)} %q.1) | copy-start | bytes 2359300
  3.7 2.1 %collective-permute-start.68 = (f32[7,128,128]{2,1,0:T(8,128)S(1)}, f32[7,128,128]{2,1,0:T(8,128)S(1)}, u32[]{:S(2)}, u32[]{:S(2)}) collective-permute-start(f32[7,128,128]{2,1,0:T(8,128)S(1)} %get-tuple-element.312), channel_id=1, source_target_pairs={{0,16},{16,0},{1,17},{17,1},{2,18},{18,2},{3,19},{19,3},{4,20},{20... | collective-permute-start | bytes 1376264 | tf_op jit(solution)/shard_map/ppermute | solution.py:26
  6.9 36.1 %collective-permute-start.74 = (bf16[256,768]{1,0:T(8,128)(2,1)S(1)}, bf16[256,768]{1,0:T(8,128)(2,1)S(1)}, u32[]{:S(2)}, u32[]{:S(2)}) collective-permute-start(bf16[256,768]{1,0:T(8,128)(2,1)S(1)} %get-tuple-element.316), channel_id=1, source_target_pairs={{0,12},{4,0},{8,4},{12,8},{1,13},{5,1},{9,5},{13,9},{2,14},{6,2},{... | collective-permute-start | bytes 1179656 | tf_op jit(solution)/shard_map/ppermute | solution.py:26
  11.9 47.6 %collective-permute-start.75 = (bf16[256,768]{1,0:T(8,128)(2,1)S(1)}, bf16[256,768]{1,0:T(8,128)(2,1)S(1)}, u32[]{:S(2)}, u32[]{:S(2)}) collective-permute-start(bf16[256,768]{1,0:T(8,128)(2,1)S(1)} %get-tuple-element.324), channel_id=1, source_target_pairs={{0,12},{4,0},{8,4},{12,8},{1,13},{5,1},{9,5},{13,9},{2,14},{6,2},{... | collective-permute-start | bytes 1179656 | tf_op jit(solution)/shard_map/ppermute | solution.py:26
  12.5 30.5 %collective-permute-start.72 = (bf16[256,384]{1,0:T(8,128)(2,1)S(1)}, bf16[256,384]{1,0:T(8,128)(2,1)S(1)}, u32[]{:S(2)}, u32[]{:S(2)}) collective-permute-start(bf16[256,384]{1,0:T(8,128)(2,1)S(1)} %get-tuple-element.314), channel_id=1, source_target_pairs={{0,12},{4,0},{8,4},{12,8},{1,13},{5,1},{9,5},{13,9},{2,14},{6,2},{... | collective-permute-start | bytes 589832 | tf_op jit(solution)/shard_map/ppermute | solution.py:26
  13.9 29.0 %collective-permute-start.73 = (bf16[256,384]{1,0:T(8,128)(2,1)S(1)}, bf16[256,384]{1,0:T(8,128)(2,1)S(1)}, u32[]{:S(2)}, u32[]{:S(2)}) collective-permute-start(bf16[256,384]{1,0:T(8,128)(2,1)S(1)} %get-tuple-element.315), channel_id=1, source_target_pairs={{0,12},{4,0},{8,4},{12,8},{1,13},{5,1},{9,5},{13,9},{2,14},{6,2},{... | collective-permute-start | bytes 589832 | tf_op jit(solution)/shard_map/ppermute | solution.py:26
  14.0 22.5 %collective-permute-start.71 = (f32[8,128]{1,0:T(8,128)S(1)}, f32[8,128]{1,0:T(8,128)S(1)}, u32[]{:S(2)}, u32[]{:S(2)}) collective-permute-start(f32[8,128]{1,0:T(8,128)S(1)} %get-tuple-element.313.refs_0_), channel_id=1, source_target_pairs={{0,20},{4,24},{8,28},{12,16},{16,4},{20,8},{24,12},{28,0},{1,21},{... | collective-permute-start | bytes 12296 | tf_op jit(solution)/shard_map/ppermute | solution.py:621
  36.5 3.0 %collective-permute-start.70 = (f32[8,128]{1,0:T(8,128)S(1)}, f32[8,128]{1,0:T(8,128)S(1)}, u32[]{:S(2)}, u32[]{:S(2)}) collective-permute-start(f32[8,128]{1,0:T(8,128)S(1)} %get-tuple-element.313.refs_0_), channel_id=1, source_target_pairs={{0,24},{4,28},{8,16},{12,20},{16,8},{20,12},{24,0},{28,4},{1,25},{... | collective-permute-start | bytes 12296 | tf_op jit(solution)/shard_map/ppermute | solution.py:621
  39.5 3.3 %collective-permute-start.69 = (f32[8,128]{1,0:T(8,128)S(1)}, f32[8,128]{1,0:T(8,128)S(1)}, u32[]{:S(2)}, u32[]{:S(2)}) collective-permute-start(f32[8,128]{1,0:T(8,128)S(1)} %get-tuple-element.313.refs_0_), channel_id=1, source_target_pairs={{0,28},{4,16},{8,20},{12,24},{16,12},{20,0},{24,4},{28,8},{1,29},{... | collective-permute-start | bytes 12296 | tf_op jit(solution)/shard_map/ppermute | solution.py:621
  43.0 16.2 %collective-permute-start = (bf16[3,128,768]{2,1,0:T(8,128)(2,1)S(1)}, bf16[3,128,768]{2,1,0:T(8,128)(2,1)S(1)}, u32[]{:S(2)}, u32[]{:S(2)}) collective-permute-start(bf16[3,128,768]{2,1,0:T(8,128)(2,1)S(1)} %get-tuple-element.173.old), channel_id=1, source_target_pairs={{0,12},{4,0},{8,4},{12,8},{16,28},{20,16},{24,20},{28,24},{1,13},{... | collective-permute-start | bytes 1769480 | tf_op jit(solution)/shard_map/cond/branch_0_fun/ppermute | solution.py:450
  45.4 7.7 %collective-permute-start.3 = (f32[1,384]{1,0:T(1,128)S(1)}, f32[1,384]{1,0:T(1,128)S(1)}, u32[]{:S(2)}, u32[]{:S(2)}) collective-permute-start(f32[1,384]{1,0:T(1,128)S(1)} %get-tuple-element.174.refs_0_), channel_id=1, source_target_pairs={{0,1},{1,2},{2,3},{3,0},{4,5},{5,6},{6,7},{7,4},{8,9},{9,10},{10,1... | collective-permute-start | bytes 4616 | tf_op jit(solution)/shard_map/cond/branch_0_fun/ppermute | solution.py:26
  46.9 6.1 %collective-permute-start.2 = (f32[1,384]{1,0:T(1,128)S(1)}, f32[1,384]{1,0:T(1,128)S(1)}, u32[]{:S(2)}, u32[]{:S(2)}) collective-permute-start(f32[1,384]{1,0:T(1,128)S(1)} %get-tuple-element.174.refs_0_), channel_id=1, source_target_pairs={{0,2},{1,3},{2,0},{3,1},{4,6},{5,7},{6,4},{7,5},{8,10},{9,11},{10,... | collective-permute-start | bytes 4616 | tf_op jit(solution)/shard_map/cond/branch_0_fun/ppermute | solution.py:26
  49.5 3.6 %collective-permute-start.1 = (f32[1,384]{1,0:T(1,128)S(1)}, f32[1,384]{1,0:T(1,128)S(1)}, u32[]{:S(2)}, u32[]{:S(2)}) collective-permute-start(f32[1,384]{1,0:T(1,128)S(1)} %get-tuple-element.174.refs_0_), channel_id=1, source_target_pairs={{0,3},{1,0},{2,1},{3,2},{4,7},{5,4},{6,5},{7,6},{8,11},{9,8},{10,9... | collective-permute-start | bytes 4616 | tf_op jit(solution)/shard_map/cond/branch_0_fun/ppermute | solution.py:26

commit v8 on v7

--- a/solution.py
+++ b/solution.py
@@ -13,6 +13,7 @@
 HEAD_SIZE = 128
 BLOCK_ROWS = 128
 GRANT = 16 * 2**20
+PIECES = 8
 
 
 ANY = pl.BlockSpec(memory_space=pl.ANY)
@@ -124,7 +125,7 @@
 
 
 def open_kernel(
-    factor, query_side, end, router, blocks, q, k, v, g, chunk, tail, router_buf, blocks_buf,
+    factor, query_side, end, router, blocks, q, k, v, g, chunk, router_buf, blocks_buf,
     x_buf, v_buf, g_buf, c_buf, scores_buf, states_buf, acc,
     small_sem, load_sem,
 ):
@@ -136,28 +137,37 @@
     for copy in small:
         copy.start()
     shared = head_loads(((g, g_buf), (v, v_buf)), 0, end, load_sem)
-    for load in shared:
-        load.start()
+    rows = q.shape[1] // PIECES
+
+    def start_pieces(source, target, sem):
+        for i in range(PIECES):
+            at = pl.ds(i * rows, rows)
+            pltpu.make_async_copy(
+                source.at[0, at, lanes(0, end)], target.at[at], load_sem.at[sem]
+            ).start()
+
+    start_pieces(g, g_buf, 0)
+    start_pieces(v, v_buf, 1)
 
     def start(query):
-        x = k if query else q
-        pltpu.make_async_copy(x.at[0, :, lanes(0, end)], x_buf, load_sem.at[2]).start()
+        start_pieces(k if query else q, x_buf, 2)
 
     by_role(query_side, start)
     difference = row_minus_column()
     for copy in small + shared[:1]:
         copy.wait()
-    for n in range(slots):
-        block = blocks_buf[0, 0, n]
-        weight = jnp.where(live_of(blocks_buf, n), down_rows(router_buf, block), 0.0)
-        for h in range(end):
-            c_buf[rows_of(n), lanes(h)] = weigh(weight, g_buf[rows_of(block), lanes(h)])
-    shared[1].wait()
-    pltpu.make_async_copy(k.at[0, :, lanes(0, end)], x_buf, load_sem.at[2]).wait()
 
     def body(query):
         allowed = difference >= 0 if query else difference <= 0
         order = in_order(query, slots)
+        sent = range(slots - 1)
+        for n in sent if query else order:
+            block = blocks_buf[0, 0, n]
+            weight = jnp.where(live_of(blocks_buf, n), down_rows(router_buf, block), 0.0)
+            for h in range(end):
+                c_buf[rows_of(n), lanes(h)] = weigh(weight, g_buf[rows_of(block), lanes(h)])
+        shared[1].wait()
+        pltpu.make_async_copy(k.at[0, :, lanes(0, end)], x_buf, load_sem.at[2]).wait()
 
         def sides(n, h):
             c_h = c_buf[rows_of(n), lanes(h)]
@@ -167,11 +177,13 @@
         def x_of(n, h):
             return x_buf[rows_of(blocks_buf[0, 0, n]), lanes(h)]
 
-        for n in order:
+        for n in sent:
             for h in range(end):
                 l_h, r_h = sides(n, h)
                 scores_buf[n, h] = jnp.where(allowed, dot_nt(l_h, r_h), 0.0).astype(jnp.bfloat16)
         for i, n in enumerate(order[:-1]):
+            if order[i + 1] not in sent:
+                break
             for h in range(end):
                 added = dot_tn(sides(n, h)[1], x_of(n, h))
                 if i > 0:
@@ -179,6 +191,8 @@
                 acc[h] = added
                 states_buf[order[i + 1], h] = added.astype(jnp.bfloat16)
         for i, n in enumerate(order):
+            if n not in sent:
+                continue
             scale = jnp.where(live_of(blocks_buf, n), factor, 0.0)
             for h in range(end):
                 if i == 0:
@@ -188,7 +202,7 @@
                         jnp.concatenate([scores_buf[n, h], sides(n, h)[0]], axis=1),
                         jnp.concatenate([x_of(n, h), states_buf[n, h]], axis=0),
                     )
-                put_rows(chunk, tail, n, lanes(h), (scale * out).astype(jnp.bfloat16))
+                chunk[rows_of(n), lanes(h)] = (scale * out).astype(jnp.bfloat16)
 
     by_role(query_side, body)
 
@@ -208,10 +222,10 @@
     return pl.pallas_call(
         functools.partial(open_kernel, factor, query_side, end),
         name="opened",
-        out_shape=split_rows(slots, end * HEAD_SIZE)
+        out_shape=split_rows(slots, end * HEAD_SIZE)[:1]
         + [pltpu.VMEM(router.shape, router.dtype), pltpu.SMEM(blocks.shape, blocks.dtype)],
         in_specs=[HBM] * 6,
-        out_specs=[VMEM] * 3 + [SMEM],
+        out_specs=[VMEM] * 2 + [SMEM],
         scratch_shapes=[
             part, part, part,
             pltpu.VMEM((slots * BLOCK_ROWS, end * HEAD_SIZE), jnp.bfloat16),
@@ -259,7 +273,8 @@
                 c_h, v_h = c_all[own, lanes(h)], v[rows, lanes(h)]
                 return (c_h, v_h) if query else (v_h, c_h)
 
-            for h in range(begin, heads):
+            low = 0 if split and n == slots - 1 else begin
+            for h in range(low, heads):
                 l_h, r_h = sides(h)
                 scores_buf[n, h] = jnp.where(allowed, dot_nt(l_h, r_h), 0.0).astype(jnp.bfloat16)
             for h in range(heads):
@@ -275,7 +290,7 @@
                     if query and n > 0:
                         added = jnp.where(live, added, 0.0)
                     total[h] = so_far + added
-            for h in range(begin, heads):
+            for h in range(low, heads):
                 l_h, _ = sides(h)
                 x_h = x_all[rows, lanes(h)]
                 if i == 0 and not seeded:
@@ -286,7 +301,7 @@
                         jnp.concatenate([x_h, states[n, h]], axis=0),
                     )
                 out = (scale * out).astype(jnp.bfloat16)
-                put_rows(chunk, tail, n, lanes(h - begin), out)
+                put_rows(chunk, tail, n, lanes(h - low), out)
         full = jnp.where(live_of(blocks, slots - 1), 1.0, 0.0)
         if not seeded:
             total[heads] = jnp.full((HEAD_SIZE, HEAD_SIZE), full, jnp.float32)
@@ -306,7 +321,7 @@
     square = (HEAD_SIZE, HEAD_SIZE)
     out_width = (heads - begin) * HEAD_SIZE
     if split:
-        out_shape = split_rows(slots, out_width)
+        out_shape = [split_rows(slots, out_width)[0], split_rows(slots, width)[1]]
     else:
         out_shape = [pltpu.VMEM((slots * BLOCK_ROWS, out_width), jnp.bfloat16)]
     out_shape.append(pltpu.VMEM((slots, heads) + square, jnp.bfloat16))
@@ -335,7 +350,7 @@
 
 def value_kernel(factor, take_one, split, blocks, q, k, c_all, one, two, *refs):
     if split:
-        tail_a, tail_b, tail_c, chunk, tails, scores_buf = refs
+        tail_b, tail_c, chunk, tails, scores_buf = refs
         tail = tails.at[2]
     else:
         chunk, scores_buf = refs
@@ -359,11 +374,8 @@
                 out = out + dot_nt(k[rows, lanes(h)], states[n, h])
                 put_rows(chunk, tail, n, lanes(h), (scale * out).astype(jnp.bfloat16))
         if split:
-            begin = tail_a.shape[1] // HEAD_SIZE
-            early, late = (1, 0) if pick else (0, 1)
-            tails[early, :, lanes(0, begin)] = tail_a[...]
-            tails[early, :, lanes(begin, heads - begin)] = tail_b[...]
-            tails[late] = tail_c[...]
+            tails[1 if pick else 0] = tail_b[...]
+            tails[0 if pick else 1] = tail_c[...]
 
     by_role(take_one, body)
 
@@ -623,7 +635,7 @@
         def kernel(call, *operands):
             return call(factor, *operands)
 
-        chunk_a, tail_a, *loaded = kernel(opened, is_first, head_start, small, held)
+        chunk_a, *loaded = kernel(opened, is_first, head_start, small, held)
         loaded += [x[0] for x in arrays]
         chunk_a = sent(chunk_a)
         chunk_b, tail_b, own, total, c_all = kernel(side, is_first, head_start, True, loaded)
@@ -632,9 +644,7 @@
         chunk_c, tail_c, other, info = kernel(side, is_last, 0, True, loaded, c_all, total)
         chunk_c = sent(chunk_c)
         infos = [info] + [across(info, other_core(pipe_count, k)) for k in range(1, pipe_count)]
-        chunk_d, tails = kernel(
-            value_side, is_last, loaded, c_all, own, other, (tail_a, tail_b, tail_c)
-        )
+        chunk_d, tails = kernel(value_side, is_last, loaded, c_all, own, other, (tail_b, tail_c))
         chunk_d = sent(chunk_d)
         partial = kernel(router_side, is_first, loaded, own, other)
         choice = pick(infos)[0, 0]

time: 60.9 us -> 61 us (level)
  no operation moved by 1% of the time
where the time goes in v8:
time: 61 us; the launch traced here: 60.8 us
  waiting for transfers between devices  32 us (52%)
  starting transfers between devices  17.4 us (29%)
  Pallas kernels  9.74 us (16%)
  between operations  0.94 us (2%)
    ppermute x3, waiting for transfers between devices, across(): return lax.ppermute(x, ('seq', 'pipe'), pairs)  24.5 us
    ppermute x8, starting transfers between devices, from_behind(): return lax.ppermute(x, axis, [(i, (i + by) % count) for i in range(count)])  12 us
    ppermute x1, waiting for transfers between devices, third(): received = lax.ppermute(tails, ('seq', 'pipe'), pairs)  6.09 us
    ppermute x3, starting transfers between devices, across(): return lax.ppermute(x, ('seq', 'pipe'), pairs)  3.06 us
    ppermute x1, starting transfers between devices, third(): received = lax.ppermute(tails, ('seq', 'pipe'), pairs)  2.37 us
    pallas_call x3, Pallas kernels, place(): pl.pallas_call(functools.partial(place_kernel, section_of, begin), name='...  2.15 us
    pallas_call x2, Pallas kernels, side(): pl.pallas_call(functools.partial(side_kernel, factor, query_side, begin,...  2.02 us
    pallas_call x1, Pallas kernels, opened(): pl.pallas_call(functools.partial(open_kernel, factor, query_side, end), n...  1.92 us
  transfers between devices with their start and end apart: 12, of which 4 were waited for; matrix products, arithmetic and copies ran while one was open for 0% of the time, Pallas kernels for 8%

profile of v8, /device:TPU:0, one launch (start us, length us, event | category | flops | bytes accessed | tf_op | source)
XLA Modules:
  0.0 60.8 jit_solution(16530314717153856785)
XLA Ops:
  0.6 0.0 copy-start.3
  0.6 0.0 copy-start.2
  0.7 0.0 copy-start.1
  0.7 0.0 copy-start
  0.7 1.9 %opened.1 = (bf16[256,384]{1,0:T(8,128)(2,1)S(1)}, f32[1,512]{1,0:T(1,128)S(1)}, s32[1,1,3]{2,1,0:T(1,128)S(4)}) custom-call(f32[1,512]{1,0:T(1,128)} %router.1, s32[1,1,3]{2,1,0:T(1,128)} %blocks.1, bf16[1,512,768]{2,1,0:T(8,128)(2,1)} %q.1, bf16[1,512,768]{2,1,0:T(8,128)(2,1)} %k.1, bf16[1,512,768]{2,1,0:T(8,128)(2,1)} %v.1, bf16[1,512,768]{2,1,0:T(8,128)(2,1)} %g.1), custom_call_target="tpu_custom_call" | custom-call | flops 150994944 | bytes 1179648 | tf_op jit(solution)/shard_map/opened/pallas_call | solution.py:222
  2.6 0.0 copy-done.3
  2.6 0.0 copy-done.2
  2.6 0.1 copy-done.1
  2.7 0.2 copy-done
  2.9 1.0 %side.2 = (bf16[256,384]{1,0:T(8,128)(2,1)S(1)}, bf16[128,768]{1,0:T(8,128)(2,1)S(1)}, bf16[3,6,128,128]{3,2,1,0:T(8,128)(2,1)S(1)}, f32[7,128,128]{2,1,0:T(8,128)S(1)}, bf16[384,768]{1,0:T(8,128)(2,1)S(1)}) custom-call(f32[1,512]{1,0:T(1,128)S(1)} %get-tuple-element.308.refs_0_, s32[1,1,3]{2,1,0:T(1,128)S(4)} %get-tuple-element.309.refs_1_.blocks, ...), custom_call_target="tpu_custom_call" | custom-call | flops 301989888 | tf_op jit(solution)/shard_map/side/pallas_call | solution.py:339
  3.9 0.6 collective-permute-start.68
  4.5 1.4 %collective-permute-done.68.refs_7_ = f32[7,128,128]{2,1,0:T(8,128)S(1)} collective-permute-done((f32[7,128,128]{2,1,0:T(8,128)S(1)}, f32[7,128,128]{2,1,0:T(8,128)S(1)}, u32[]{:S(2)}, u32[]{:S(2)}) %collective-permute-start.68) | collective-permute-done | bytes 458784 | tf_op jit(solution)/shard_map/ppermute | solution.py:27
  5.9 1.1 %side.3 = (bf16[256,768]{1,0:T(8,128)(2,1)S(1)}, bf16[128,768]{1,0:T(8,128)(2,1)S(1)}, bf16[3,6,128,128]{3,2,1,0:T(8,128)(2,1)S(1)}, f32[8,128]{1,0:T(8,128)S(1)}) custom-call(f32[1,512]{1,0:T(1,128)S(1)} %get-tuple-element.308.refs_0_, s32[1,1,3]{2,1,0:T(1,128)S(4)} %get-tuple-element.309.refs_1_.blocks, bf16[512,768]{1,0:T(8,128)(2,1)S(1)} %bitcast.6, ...), custom_call_target="tpu_custom_call" | custom-call | flops 301989888 | tf_op jit(solution)/shard_map/side/pallas_call | solution.py:339
  7.0 3.8 %collective-permute-start.74 = (bf16[256,768]{1,0:T(8,128)(2,1)S(1)}, bf16[256,768]{1,0:T(8,128)(2,1)S(1)}, u32[]{:S(2)}, u32[]{:S(2)}) collective-permute-start(bf16[256,768]{1,0:T(8,128)(2,1)S(1)} %get-tuple-element.315), channel_id=1, source_target_pairs={{0,12},{4,0},{8,4},{12,8},{1,13},{5,1},{9,5},{13,9},{2,14},{6,2},{... | collective-permute-start | bytes 1179656 | tf_op jit(solution)/shard_map/ppermute | solution.py:27
  10.8 1.2 %value_side.1 = (bf16[256,768]{1,0:T(8,128)(2,1)S(1)}, bf16[3,128,768]{2,1,0:T(8,128)(2,1)S(1)}) custom-call(s32[1,1,3]{2,1,0:T(1,128)S(4)} %get-tuple-element.309.refs_1_.blocks, bf16[512,768]{1,0:T(8,128)(2,1)S(1)} %bitcast.7, bf16[512,768]{1,0:T(8,128)(2,1)S(1)} %bitcast.11, bf16[384,768]{1,0:T(8,128)(2,1)S(1)} %get-tuple-element.310.refs_6_.c_all, ...), custom_call_target="tpu_custom_call" | custom-call | flops 226492416 | tf_op jit(solution)/shard_map/value_side/pallas_call | solution.py:394
  12.0 0.6 collective-permute-start.75
  12.6 1.4 %collective-permute-start.72 = (bf16[256,384]{1,0:T(8,128)(2,1)S(1)}, bf16[256,384]{1,0:T(8,128)(2,1)S(1)}, u32[]{:S(2)}, u32[]{:S(2)}) collective-permute-start(bf16[256,384]{1,0:T(8,128)(2,1)S(1)} %get-tuple-element.313), channel_id=1, source_target_pairs={{0,12},{4,0},{8,4},{12,8},{1,13},{5,1},{9,5},{13,9},{2,14},{6,2},{... | collective-permute-start | bytes 589832 | tf_op jit(solution)/shard_map/ppermute | solution.py:27
  14.1 0.1 collective-permute-start.73
  14.1 0.6 collective-permute-start.71
  14.7 21.9 %collective-permute-done.71.refs_3_ = f32[8,128]{1,0:T(8,128)S(1)} collective-permute-done((f32[8,128]{1,0:T(8,128)S(1)}, f32[8,128]{1,0:T(8,128)S(1)}, u32[]{:S(2)}, u32[]{:S(2)}) %collective-permute-start.71) | collective-permute-done | bytes 4128 | tf_op jit(solution)/shard_map/ppermute | solution.py:633
  36.6 0.5 collective-permute-start.70
  37.1 2.5 %collective-permute-done.70.refs_2_ = f32[8,128]{1,0:T(8,128)S(1)} collective-permute-done((f32[8,128]{1,0:T(8,128)S(1)}, f32[8,128]{1,0:T(8,128)S(1)}, u32[]{:S(2)}, u32[]{:S(2)}) %collective-permute-start.70) | collective-permute-done | bytes 4128 | tf_op jit(solution)/shard_map/ppermute | solution.py:633
  39.7 2.0 %collective-permute-start.69 = (f32[8,128]{1,0:T(8,128)S(1)}, f32[8,128]{1,0:T(8,128)S(1)}, u32[]{:S(2)}, u32[]{:S(2)}) collective-permute-start(f32[8,128]{1,0:T(8,128)S(1)} %get-tuple-element.312.refs_0_), channel_id=1, source_target_pairs={{0,28},{4,16},{8,20},{12,24},{16,12},{20,0},{24,4},{28,8},{1,29},{... | collective-permute-start | bytes 12296 | tf_op jit(solution)/shard_map/ppermute | solution.py:633
  41.6 1.3 %router_side.1 = f32[1,384]{1,0:T(1,128)S(1)} custom-call(s32[1,1,3]{2,1,0:T(1,128)S(4)} %get-tuple-element.309.refs_1_.blocks, bf16[512,768]{1,0:T(8,128)(2,1)S(1)} %bitcast.8, bf16[512,768]{1,0:T(8,128)(2,1)S(1)} %bitcast.12, bf16[512,768]{1,0:T(8,128)(2,1)S(1)} %bitcast.15, bf16[512,768]{1,0:T(8,128)(2,1)S(1)} %bitcast.18, ...), custom_call_target="tpu_custom_call" | custom-call | flops 226492416 | tf_op jit(solution)/shard_map/router_side/pallas_call | solution.py:433
  42.9 0.0 collective-permute-done.69.refs_1_
  43.0 0.1 pick.1
  43.1 0.0 collective-permute-done.72
  43.1 0.0 collective-permute-done.73
  43.1 0.0 collective-permute-done.74
  43.1 16.5 %conditional.1 = (bf16[1,3,384,768]{3,2,1,0:T(8,128)(2,1)}, bf16[3,128,768]{2,1,0:T(8,128)(2,1)S(1)}, f32[1,384]{1,0:T(1,128)S(1)}) conditional(s32[]{:T(128)} %bitcast.4, (bf16[256,384]{1,0:T(8,128)(2,1)S(1)}, bf16[256,384]{1,0:T(8,128)(2,1)S(1)}, bf16[256,768]{1,0:T(8,128)(2,1)S(1)}, ...), branch_computations={%region_0.0_spmd, %region_1.0_spmd, %region_2.0_spmd, %region_3.0_... | conditional | bytes 3950776 | solution.py:659
  43.2 2.4 %collective-permute-start = (bf16[3,128,768]{2,1,0:T(8,128)(2,1)S(1)}, bf16[3,128,768]{2,1,0:T(8,128)(2,1)S(1)}, u32[]{:S(2)}, u32[]{:S(2)}) collective-permute-start(bf16[3,128,768]{2,1,0:T(8,128)(2,1)S(1)} %get-tuple-element.173.old), channel_id=1, source_target_pairs={{0,12},{4,0},{8,4},{12,8},{16,28},{20,16},{24,20},{28,24},{1,13},{... | collective-permute-start | bytes 1769480 | tf_op jit(solution)/shard_map/cond/branch_0_fun/ppermute | solution.py:462
  45.5 1.6 %collective-permute-start.3 = (f32[1,384]{1,0:T(1,128)S(1)}, f32[1,384]{1,0:T(1,128)S(1)}, u32[]{:S(2)}, u32[]{:S(2)}) collective-permute-start(f32[1,384]{1,0:T(1,128)S(1)} %get-tuple-element.174.refs_0_), channel_id=1, source_target_pairs={{0,1},{1,2},{2,3},{3,0},{4,5},{5,6},{6,7},{7,4},{8,9},{9,10},{10,1... | collective-permute-start | bytes 4616 | tf_op jit(solution)/shard_map/cond/branch_0_fun/ppermute | solution.py:27
  47.1 2.6 %collective-permute-start.2 = (f32[1,384]{1,0:T(1,128)S(1)}, f32[1,384]{1,0:T(1,128)S(1)}, u32[]{:S(2)}, u32[]{:S(2)}) collective-permute-start(f32[1,384]{1,0:T(1,128)S(1)} %get-tuple-element.174.refs_0_), channel_id=1, source_target_pairs={{0,2},{1,3},{2,0},{3,1},{4,6},{5,7},{6,4},{7,5},{8,10},{9,11},{10,... | collective-permute-start | bytes 4616 | tf_op jit(solution)/shard_map/cond/branch_0_fun/ppermute | solution.py:27
  49.7 1.3 %collective-permute-start.1 = (f32[1,384]{1,0:T(1,128)S(1)}, f32[1,384]{1,0:T(1,128)S(1)}, u32[]{:S(2)}, u32[]{:S(2)}) collective-permute-start(f32[1,384]{1,0:T(1,128)S(1)} %get-tuple-element.174.refs_0_), channel_id=1, source_target_pairs={{0,3},{1,0},{2,1},{3,2},{4,7},{5,4},{6,5},{7,6},{8,11},{9,8},{10,9... | collective-permute-start | bytes 4616 | tf_op jit(solution)/shard_map/cond/branch_0_fun/ppermute | solution.py:27
  51.0 0.7 %place.51.refs_0_ = bf16[1,3,384,768]{3,2,1,0:T(8,128)(2,1)} custom-call(bf16[256,384]{1,0:T(8,128)(2,1)S(1)} %get-tuple-element.170.refs_0_), custom_call_target="tpu_custom_call" | custom-call | bytes 393216 | tf_op jit(solution)/shard_map/cond/branch_0_fun/place/pallas_call | solution.py:508
  51.7 0.7 %place.52.refs_0_ = bf16[1,3,384,768]{3,2,1,0:T(8,128)(2,1)} custom-call(bf16[1,3,384,768]{3,2,1,0:T(8,128)(2,1)} %place.51.refs_0_, bf16[256,384]{1,0:T(8,128)(2,1)S(1)} %get-tuple-element.171.refs_1_), custom_call_target="tpu_custom_call", output_to_operand_aliasing={{}: (0, {})} | custom-call | bytes 393216 | tf_op jit(solution)/shard_map/cond/branch_0_fun/place/pallas_call | solution.py:508
  52.4 0.8 %place.53 = bf16[1,3,384,768]{3,2,1,0:T(8,128)(2,1)} custom-call(bf16[1,3,384,768]{3,2,1,0:T(8,128)(2,1)} %place.52.refs_0_, bf16[256,768]{1,0:T(8,128)(2,1)S(1)} %get-tuple-element.172.refs_1_), custom_call_target="tpu_custom_call", output_to_operand_aliasing={{}: (0, {})} | custom-call | bytes 786432 | tf_op jit(solution)/shard_map/cond/branch_0_fun/place/pallas_call | solution.py:508
  53.2 0.0 collective-permute-done.3.refs_3_
  53.2 0.0 collective-permute-done.2.refs_2_
  53.2 0.0 collective-permute-done.1.refs_1_
  53.3 6.1 %collective-permute-done.new = bf16[3,128,768]{2,1,0:T(8,128)(2,1)S(1)} collective-permute-done((bf16[3,128,768]{2,1,0:T(8,128)(2,1)S(1)}, bf16[3,128,768]{2,1,0:T(8,128)(2,1)S(1)}, u32[]{:S(2)}, u32[]{:S(2)}) %collective-permute-start) | collective-permute-done | bytes 589856 | tf_op jit(solution)/shard_map/cond/branch_0_fun/ppermute | solution.py:462
  59.6 0.0 collective-permute-done.75.chunk
  59.6 1.0 %finish.1 = (bf16[1,3,384,768]{3,2,1,0:T(8,128)(2,1)}, f32[1,384]{1,0:T(1,128)}) custom-call(bf16[1,3,384,768]{3,2,1,0:T(8,128)(2,1)} %get-tuple-element.321.whole, bf16[256,768]{1,0:T(8,128)(2,1)S(1)} %collective-permute-done.75.chunk, bf16[3,128,768]{2,1,0:T(8,128)(2,1)S(1)} %get-tuple-element.323.tails, ...), custom_call_target="tpu_custom_call", output_to_operand_aliasing={{0}: (0, {})} | custom-call | bytes 1966080 | tf_op jit(solution)/shard_map/finish/pallas_call | solution.py:493
  (1 shorter events, 0.0 us)
Async XLA Ops:
  0.6 2.0 %copy-start.3 = (bf16[1,512,768]{2,1,0:T(8,128)(2,1)S(1)}, bf16[1,512,768]{2,1,0:T(8,128)(2,1)}, u32[]{:S(2)}) copy-start(bf16[1,512,768]{2,1,0:T(8,128)(2,1)} %g.1) | copy-start | bytes 2359300
  0.6 2.0 %copy-start.2 = (bf16[1,512,768]{2,1,0:T(8,128)(2,1)S(1)}, bf16[1,512,768]{2,1,0:T(8,128)(2,1)}, u32[]{:S(2)}) copy-start(bf16[1,512,768]{2,1,0:T(8,128)(2,1)} %v.1) | copy-start | bytes 2359300
  0.7 2.0 %copy-start.1 = (bf16[1,512,768]{2,1,0:T(8,128)(2,1)S(1)}, bf16[1,512,768]{2,1,0:T(8,128)(2,1)}, u32[]{:S(2)}) copy-start(bf16[1,512,768]{2,1,0:T(8,128)(2,1)} %k.1) | copy-start | bytes 2359300
  0.7 2.3 %copy-start = (bf16[1,512,768]{2,1,0:T(8,128)(2,1)S(1)}, bf16[1,512,768]{2,1,0:T(8,128)(2,1)}, u32[]{:S(2)}) copy-start(bf16[1,512,768]{2,1,0:T(8,128)(2,1)} %q.1) | copy-start | bytes 2359300
  3.9 2.0 %collective-permute-start.68 = (f32[7,128,128]{2,1,0:T(8,128)S(1)}, f32[7,128,128]{2,1,0:T(8,128)S(1)}, u32[]{:S(2)}, u32[]{:S(2)}) collective-permute-start(f32[7,128,128]{2,1,0:T(8,128)S(1)} %get-tuple-element.311), channel_id=1, source_target_pairs={{0,16},{16,0},{1,17},{17,1},{2,18},{18,2},{3,19},{19,3},{4,20},{20... | collective-permute-start | bytes 1376264 | tf_op jit(solution)/shard_map/ppermute | solution.py:27
  7.0 36.1 %collective-permute-start.74 = (bf16[256,768]{1,0:T(8,128)(2,1)S(1)}, bf16[256,768]{1,0:T(8,128)(2,1)S(1)}, u32[]{:S(2)}, u32[]{:S(2)}) collective-permute-start(bf16[256,768]{1,0:T(8,128)(2,1)S(1)} %get-tuple-element.315), channel_id=1, source_target_pairs={{0,12},{4,0},{8,4},{12,8},{1,13},{5,1},{9,5},{13,9},{2,14},{6,2},{... | collective-permute-start | bytes 1179656 | tf_op jit(solution)/shard_map/ppermute | solution.py:27
  12.0 47.6 %collective-permute-start.75 = (bf16[256,768]{1,0:T(8,128)(2,1)S(1)}, bf16[256,768]{1,0:T(8,128)(2,1)S(1)}, u32[]{:S(2)}, u32[]{:S(2)}) collective-permute-start(bf16[256,768]{1,0:T(8,128)(2,1)S(1)} %get-tuple-element.322), channel_id=1, source_target_pairs={{0,12},{4,0},{8,4},{12,8},{1,13},{5,1},{9,5},{13,9},{2,14},{6,2},{... | collective-permute-start | bytes 1179656 | tf_op jit(solution)/shard_map/ppermute | solution.py:27
  12.6 30.5 %collective-permute-start.72 = (bf16[256,384]{1,0:T(8,128)(2,1)S(1)}, bf16[256,384]{1,0:T(8,128)(2,1)S(1)}, u32[]{:S(2)}, u32[]{:S(2)}) collective-permute-start(bf16[256,384]{1,0:T(8,128)(2,1)S(1)} %get-tuple-element.313), channel_id=1, source_target_pairs={{0,12},{4,0},{8,4},{12,8},{1,13},{5,1},{9,5},{13,9},{2,14},{6,2},{... | collective-permute-start | bytes 589832 | tf_op jit(solution)/shard_map/ppermute | solution.py:27
  14.1 29.0 %collective-permute-start.73 = (bf16[256,384]{1,0:T(8,128)(2,1)S(1)}, bf16[256,384]{1,0:T(8,128)(2,1)S(1)}, u32[]{:S(2)}, u32[]{:S(2)}) collective-permute-start(bf16[256,384]{1,0:T(8,128)(2,1)S(1)} %get-tuple-element.314), channel_id=1, source_target_pairs={{0,12},{4,0},{8,4},{12,8},{1,13},{5,1},{9,5},{13,9},{2,14},{6,2},{... | collective-permute-start | bytes 589832 | tf_op jit(solution)/shard_map/ppermute | solution.py:27
  14.1 22.5 %collective-permute-start.71 = (f32[8,128]{1,0:T(8,128)S(1)}, f32[8,128]{1,0:T(8,128)S(1)}, u32[]{:S(2)}, u32[]{:S(2)}) collective-permute-start(f32[8,128]{1,0:T(8,128)S(1)} %get-tuple-element.312.refs_0_), channel_id=1, source_target_pairs={{0,20},{4,24},{8,28},{12,16},{16,4},{20,8},{24,12},{28,0},{1,21},{... | collective-permute-start | bytes 12296 | tf_op jit(solution)/shard_map/ppermute | solution.py:633
  36.6 3.0 %collective-permute-start.70 = (f32[8,128]{1,0:T(8,128)S(1)}, f32[8,128]{1,0:T(8,128)S(1)}, u32[]{:S(2)}, u32[]{:S(2)}) collective-permute-start(f32[8,128]{1,0:T(8,128)S(1)} %get-tuple-element.312.refs_0_), channel_id=1, source_target_pairs={{0,24},{4,28},{8,16},{12,20},{16,8},{20,12},{24,0},{28,4},{1,25},{... | collective-permute-start | bytes 12296 | tf_op jit(solution)/shard_map/ppermute | solution.py:633
  39.7 3.3 %collective-permute-start.69 = (f32[8,128]{1,0:T(8,128)S(1)}, f32[8,128]{1,0:T(8,128)S(1)}, u32[]{:S(2)}, u32[]{:S(2)}) collective-permute-start(f32[8,128]{1,0:T(8,128)S(1)} %get-tuple-element.312.refs_0_), channel_id=1, source_target_pairs={{0,28},{4,16},{8,20},{12,24},{16,12},{20,0},{24,4},{28,8},{1,29},{... | collective-permute-start | bytes 12296 | tf_op jit(solution)/shard_map/ppermute | solution.py:633
  43.2 16.2 %collective-permute-start = (bf16[3,128,768]{2,1,0:T(8,128)(2,1)S(1)}, bf16[3,128,768]{2,1,0:T(8,128)(2,1)S(1)}, u32[]{:S(2)}, u32[]{:S(2)}) collective-permute-start(bf16[3,128,768]{2,1,0:T(8,128)(2,1)S(1)} %get-tuple-element.173.old), channel_id=1, source_target_pairs={{0,12},{4,0},{8,4},{12,8},{16,28},{20,16},{24,20},{28,24},{1,13},{... | collective-permute-start | bytes 1769480 | tf_op jit(solution)/shard_map/cond/branch_0_fun/ppermute | solution.py:462
  45.5 7.7 %collective-permute-start.3 = (f32[1,384]{1,0:T(1,128)S(1)}, f32[1,384]{1,0:T(1,128)S(1)}, u32[]{:S(2)}, u32[]{:S(2)}) collective-permute-start(f32[1,384]{1,0:T(1,128)S(1)} %get-tuple-element.174.refs_0_), channel_id=1, source_target_pairs={{0,1},{1,2},{2,3},{3,0},{4,5},{5,6},{6,7},{7,4},{8,9},{9,10},{10,1... | collective-permute-start | bytes 4616 | tf_op jit(solution)/shard_map/cond/branch_0_fun/ppermute | solution.py:27
  47.1 6.1 %collective-permute-start.2 = (f32[1,384]{1,0:T(1,128)S(1)}, f32[1,384]{1,0:T(1,128)S(1)}, u32[]{:S(2)}, u32[]{:S(2)}) collective-permute-start(f32[1,384]{1,0:T(1,128)S(1)} %get-tuple-element.174.refs_0_), channel_id=1, source_target_pairs={{0,2},{1,3},{2,0},{3,1},{4,6},{5,7},{6,4},{7,5},{8,10},{9,11},{10,... | collective-permute-start | bytes 4616 | tf_op jit(solution)/shard_map/cond/branch_0_fun/ppermute | solution.py:27
  49.7 3.6 %collective-permute-start.1 = (f32[1,384]{1,0:T(1,128)S(1)}, f32[1,384]{1,0:T(1,128)S(1)}, u32[]{:S(2)}, u32[]{:S(2)}) collective-permute-start(f32[1,384]{1,0:T(1,128)S(1)} %get-tuple-element.174.refs_0_), channel_id=1, source_target_pairs={{0,3},{1,0},{2,1},{3,2},{4,7},{5,4},{6,5},{7,6},{8,11},{9,8},{10,9... | collective-permute-start | bytes 4616 | tf_op jit(solution)/shard_map/cond/branch_0_fun/ppermute | solution.py:27
